TPU v7x, 128 devices: a whole 4x4x4 slice. The times are simulated.
128 devices in a mesh: row: 16 (over z, y), col: 8 (over x, core).
Axes of the slice: x: 4, y: 4, z: 4, core: 2. Of those that a mesh axis runs over, the one named last changes fastest.
Arguments:
- rhs: float32 [262144, 256], P(('row', 'col')), may hold values from -6 to 6
- block_target: int32 [2048], P(('row', 'col')), may hold values from 0 to 255, as said below
- pivot_inverse: float32 [131072, 1024], P(('row', 'col')), may hold values from -0.25 to 3, as said below
- update_factor: float32 [131072, 1024], P(('row', 'col')), may hold values from -0.1875 to 0.1875
- root_inverse: float32 [16384, 16384], P('row', 'col'), may hold values from -0.25 to 3, as said below
- update_map: int32 [1024], P(('row', 'col')), may hold values from 0 to 127
Outputs:
- front_solution: float32 [131072, 256], P(('row', 'col'))
- root_solution: float32 [16384, 256], P(('row', 'col'))
Inputs may be any that keep to these rules, and one draw needn't show every extreme that they name: block_target[g] is e * 16 + s: block g goes to the device of row index e in its own column, slot s there. Each device sends exactly 2 blocks to each of 8 devices of its column and none to the others; every slot of every device is filled exactly once. `pivot_inverse`: each device's block of 1024 rows is lower triangular with its diagonal positive. `root_inverse`: lower triangular with its diagonal positive.
All inputs are finite; a program needn't handle non-finite values.
Results may differ from a plain program's by a relative error of at most 0.000073.
Values sent between devices are 32-bit elements; how exact they have to be, the bound alone decides.
No kernel may reach another device: no remote copies, remote signals or barrier semaphores. Data moves between devices by JAX's collectives and lax.ppermute only.
A program may use at most 192 MiB of HBM per device.

v0:
```python
import jax
import jax.numpy as jnp
from jax import lax
from jax.sharding import PartitionSpec as P

BLK = 128
NRHS = 256
RB_DEV = 16
CAP = 2


def shards(rhs, block_target, pivot_inverse, update_factor, root_inverse, update_map):
    row_count = lax.axis_size("row")
    col_count = lax.axis_size("col")
    target_row = block_target // RB_DEV
    slot_index = block_target % RB_DEV
    same_peer = target_row[:, None] == target_row[None, :]
    earlier = lax.broadcasted_iota(jnp.int32, (RB_DEV, RB_DEV), 1) < lax.broadcasted_iota(
        jnp.int32, (RB_DEV, RB_DEV), 0
    )
    peer_rank = jnp.sum(jnp.logical_and(same_peer, earlier), axis=1)
    position = target_row * CAP + peer_rank
    flat_rhs = rhs.reshape(RB_DEV, BLK * NRHS)
    outgoing = jnp.zeros((row_count * CAP, BLK * NRHS), jnp.float32).at[position].set(flat_rhs)
    outgoing_slots = jnp.full((row_count * CAP,), -1, jnp.int32).at[position].set(slot_index)
    arrived, arrived_slots = (
        lax.all_to_all(
            outgoing.reshape(row_count, CAP, BLK * NRHS),
            "row",
            split_axis=0,
            concat_axis=0,
            tiled=True,
        ),
        lax.all_to_all(
            outgoing_slots.reshape(row_count, CAP), "row", split_axis=0, concat_axis=0, tiled=True
        ),
    )
    slot_list = arrived_slots.reshape(-1)
    placement_index = jnp.where(slot_list >= 0, slot_list, RB_DEV)
    front_blocks = (
        jnp.zeros((RB_DEV + 1, BLK * NRHS), jnp.float32)
        .at[placement_index]
        .set(arrived.reshape(row_count * CAP, BLK * NRHS))
    )
    front_rhs = front_blocks[:RB_DEV].reshape(RB_DEV * BLK, NRHS)
    pivot_rows = pivot_inverse.shape[0]
    solved = jnp.dot(
        pivot_inverse,
        front_rhs[:pivot_rows],
        precision=lax.Precision.HIGHEST,
        preferred_element_type=jnp.float32,
    )
    updated = front_rhs[pivot_rows:] - jnp.dot(
        update_factor, solved, precision=lax.Precision.HIGHEST, preferred_element_type=jnp.float32
    )
    root_rows = root_inverse.shape[1] * col_count
    root_blocks = root_rows // BLK
    update_blocks = updated.reshape(-1, BLK, NRHS)
    scattered = jnp.zeros((root_blocks, BLK, NRHS), jnp.float32).at[update_map].add(update_blocks)
    reordered = (
        scattered.reshape(col_count, row_count, BLK, NRHS)
        .transpose(1, 0, 2, 3)
        .reshape(root_rows, NRHS)
    )
    root_piece = lax.psum_scatter(reordered, ("row", "col"), scatter_dimension=0, tiled=True)
    partial_value = jnp.dot(
        root_inverse,
        lax.all_gather(root_piece, "row", axis=0, tiled=True),
        precision=lax.Precision.HIGHEST,
        preferred_element_type=jnp.float32,
    )
    root_solution = lax.psum_scatter(partial_value, "col", scatter_dimension=0, tiled=True)
    return (solved, root_solution)


def solution(mesh):
    return jax.shard_map(
        shards,
        mesh=mesh,
        in_specs=(
            P(("row", "col"), None),
            P(("row", "col")),
            P(("row", "col"), None),
            P(("row", "col"), None),
            P("row", "col"),
            P(("row", "col")),
        ),
        out_specs=(P(("row", "col"), None), P(("row", "col"), None)),
        check_vma=False,
    )
```

profile of v0, /device:TPU:0, one launch (start us, length us, event | category | flops | bytes accessed | tf_op | source)
XLA Modules:
  0.0 913.8 jit_solution(11325415591808088879)
XLA Ops:
  7.2 0.7 and_select_fusion
  7.8 0.2 convert_reduce_fusion
  8.0 0.6 scatter_custom_fusion
  8.7 0.7 all_to_all.9
  9.3 8.1 all-to-all-start
  17.5 1.8 reshape.82
  19.2 3.8 scatter_custom_fusion.1
  23.1 5.8 reshape.65
  28.9 0.0 copy-start.2
  28.9 0.0 all-to-all-done
  28.9 7.4 all-to-all-start.1
  36.3 0.0 reduce-scatter.3.cloned.1.call-start
  36.4 0.0 copy-done.2
  36.4 0.5 broadcast.88
  36.9 0.7 reduce.3
  37.6 0.1 reshape.63
  37.7 60.1 %all-to-all-done.1 = f32[16,2,32768]{2,1,0:T(2,128)} async-done(((f32[16,2,32768]{2,1,0:T(2,128)}), f32[16,2,32768]{2,1,0:T(2,128)}, u32[]{:S(2)}, u32[]{:S(2)}) %all-to-all-start.1) | async-done | bytes 4194336 | tf_op jit(solution)/shard_map/all_to_all | solution.py:27
  97.8 6.0 reshape.90
  103.8 5.4 scatter_custom_fusion.2
  109.2 1.5 fusion.9
  110.7 0.0 copy-start.1
  110.7 1.5 slice.18
  112.2 0.3 copy.22
  112.5 0.0 copy-done.1
  112.5 1.1 slice.16
  113.6 0.0 copy-start
  113.6 9.1 fusion.10
  122.8 0.0 copy-done
  122.8 3.7 fusion.4
  126.5 0.3 copy.27
  126.9 7.8 broadcast_in_dim.31
  134.7 3.3 scatter_fusion
  138.0 11.6 %copy.24 = f32[8,16,128,256]{3,2,0,1:T(8,128)} copy(f32[8,16,128,256]{3,2,1,0:T(8,128)} %bitcast.24) | data formatting | bytes 33554432 | tf_op jit(solution)/shard_map/reshape | solution.py:61
  149.5 0.0 reduce-scatter.3.cloned.1.call-update
  149.6 0.0 all-gather.2.cloned.1.call-start
  149.6 665.4 %reduce-scatter.3.cloned.1.call-done = f32[128,256]{1,0:T(8,128)} async-done(((f32[16384,256]{1,0:T(8,128)}), f32[128,256]{1,0:T(8,128)}) %reduce-scatter.3.cloned.1.call-update) | async-done | bytes 131088 | tf_op jit(solution)/shard_map/reduce_scatter | solution.py:65
  815.1 0.0 all-gather.2.cloned.1.call-update
  815.1 0.3 reduce-scatter.5.cloned.1.call-start
  815.3 41.7 %all-gather.2.cloned.1.call-done = f32[2048,256]{1,0:T(8,128)} async-done(((f32[128,256]{1,0:T(8,128)}), f32[2048,256]{1,0:T(8,128)}) %all-gather.2.cloned.1.call-update) | async-done | bytes 2097168 | tf_op jit(solution)/shard_map/all_gather | solution.py:68
  857.1 17.4 %convolution_bitcast_fusion = f32[1024,256]{0,1:T(8,128)} fusion(f32[2048,256]{1,0:T(8,128)} %all-gather.2.cloned.1.call-done, f32[1024,2048]{1,0:T(8,128)} %param.10), kind=kOutput, calls=%fused_computation.8 | convolution fusion | flops 6442450944 | bytes 11534336 | tf_op jit(solution)/shard_map/dot_general | solution.py:66
  874.4 0.0 reduce-scatter.5.cloned.1.call-update
  874.5 1.3 copy.25
  875.8 29.8 %reduce-scatter.5.cloned.1.call-done = f32[128,256]{0,1:T(8,128)} async-done(((f32[1024,256]{0,1:T(8,128)}), f32[128,256]{0,1:T(8,128)}) %reduce-scatter.5.cloned.1.call-update) | async-done | bytes 131088 | tf_op jit(solution)/shard_map/reduce_scatter | solution.py:72
  905.6 1.7 copy.26
  (3 shorter events, 0.0 us)
Async XLA Ops:
  9.3 19.6 %all-to-all-start = ((s32[16,1,2]{2,1,0:T(1,128)}), s32[16,1,2]{2,1,0:T(1,128)S(1)}, u32[]{:S(2)}, u32[]{:S(2)}) async-start(s32[16,1,2]{2,1,0:T(1,128)} %bitcast), calls=%async_computation | async-start | bytes 16384 | tf_op jit(solution)/shard_map/all_to_all | solution.py:34
  28.9 7.5 copy-start.2
  28.9 68.9 %all-to-all-start.1 = ((f32[16,2,32768]{2,1,0:T(2,128)}), f32[16,2,32768]{2,1,0:T(2,128)}, u32[]{:S(2)}, u32[]{:S(2)}) async-start(f32[16,2,32768]{2,1,0:T(2,128)} %reshape.65), calls=%async_computation.1 | async-start | bytes 8388608 | tf_op jit(solution)/shard_map/all_to_all | solution.py:27
  36.3 778.7 %reduce-scatter.3.cloned.1.call-start = ((), (), s32[]{:S(2)}) async-start(), calls=%async_computation.4 | async-start | bytes 16908288 | tf_op jit(solution)/shard_map/reduce_scatter | solution.py:65
  110.7 1.8 copy-start.1
  113.6 9.1 %copy-start = (f32[1024,1024]{1,0:T(8,128)S(1)}, f32[1024,1024]{1,0:T(8,128)}, u32[]{:S(2)}) copy-start(f32[1024,1024]{1,0:T(8,128)} %param.9) | copy-start | bytes 12582916
  149.6 707.5 %all-gather.2.cloned.1.call-start = ((), (), s32[]{:S(2)}) async-start(), calls=%async_computation.5 | async-start | bytes 2228224 | tf_op jit(solution)/shard_map/all_gather | solution.py:68
  815.1 90.5 %reduce-scatter.5.cloned.1.call-start = ((), (), s32[]{:S(2)}) async-start(), calls=%async_computation.6 | async-start | bytes 1179648 | tf_op jit(solution)/shard_map/reduce_scatter | solution.py:72
Sparse Core Ops, SparseCore 0:
  149.7 665.3 reduce-scatter.2
  817.2 39.8 all-gather.1
  874.6 30.9 reduce-scatter.4
where the time goes:
time: 914 us
  waiting for transfers between devices  797 us (87%)
  local copies, waits for them, and re-layouts  51.8 us (6%)
  matrix products  30.2 us (3%)
  starting transfers between devices  15.9 us (2%)
  between operations  13.9 us (2%)
    reduce_scatter x1, waiting for transfers between devices, shards(): lax.psum_scatter(reordered, ('row', 'col'), scatter_dimension=0, tiled=True)  665 us
    all_to_all x1, waiting for transfers between devices, shards(): lax.all_to_all(outgoing.reshape(row_count, CAP, BLK * NRHS), 'row', split...  60.1 us
    all_gather x1, waiting for transfers between devices, shards(): lax.all_gather(root_piece, 'row', axis=0, tiled=True)  41.7 us
    reduce_scatter x1, waiting for transfers between devices, shards(): lax.psum_scatter(partial_value, 'col', scatter_dimension=0, tiled=True)  29.8 us
  transfers between devices with their start and end apart: 5, of which 4 were waited for; matrix products, arithmetic and copies ran while one was open for 2% of the time, Pallas kernels for 0%

commit v1 on v0

v1 whole, which is shorter than its diff:
```python
import functools

import jax
import jax.numpy as jnp
from jax import lax
from jax.experimental import pallas as pl
from jax.experimental.pallas import tpu as pltpu
from jax.sharding import PartitionSpec as P

BLK = 128
NRHS = 256
RB_DEV = 16
SUB = 8
VMEM_LIMIT = 56 << 20


def split(x):
    high = x.astype(jnp.bfloat16)
    low = (x - high.astype(jnp.float32)).astype(jnp.bfloat16)
    return high, low


def product(a, b_high, b_low):
    a_high, a_low = split(a)
    out = jnp.dot(a_high, b_high, preferred_element_type=jnp.float32)
    out += jnp.dot(a_high, b_low, preferred_element_type=jnp.float32)
    out += jnp.dot(a_low, b_high, preferred_element_type=jnp.float32)
    return out


def exchange(x, axis):
    return lax.all_to_all(x, axis, split_axis=0, concat_axis=0, tiled=True)


def route_kernel(rows, half, index_ref, arrived_ref, send_ref, acc_ref, placed):
    stride = RB_DEV + half
    slots = rows * half

    def place(source, carry):
        for block in range(RB_DEV):
            target = index_ref[source * stride + block]
            owner = target // RB_DEV
            slot = target % RB_DEV
            position = jnp.where(slot < half, owner * half + slot, slots + owner * half + slot - half)
            placed[position] = arrived_ref[source * RB_DEV + block]
        return carry

    lax.fori_loop(0, rows, place, 0)
    acc_ref[...] = jnp.zeros_like(acc_ref)
    send_ref[...] = placed[pl.ds(0, slots)]

    def add(owner, carry):
        for block in range(half):
            root = index_ref[owner * stride + RB_DEV + block]
            acc_ref[root] += placed[slots + owner * half + block]
        return carry

    lax.fori_loop(0, rows, add, 0)


def route(index, arrived, rows, half):
    slots = rows * half
    shape = jax.ShapeDtypeStruct((slots, SUB, NRHS), jnp.float32)
    root_shape = jax.ShapeDtypeStruct((BLK, SUB, NRHS), jnp.float32)
    return pl.pallas_call(
        functools.partial(route_kernel, rows, half),
        out_shape=(shape, root_shape),
        in_specs=[
            pl.BlockSpec(memory_space=pltpu.SMEM),
            pl.BlockSpec(memory_space=pltpu.VMEM),
        ],
        out_specs=(pl.BlockSpec(memory_space=pltpu.VMEM), pl.BlockSpec(memory_space=pltpu.VMEM)),
        scratch_shapes=[pltpu.VMEM((2 * slots, SUB, NRHS), jnp.float32)],
        compiler_params=pltpu.CompilerParams(vmem_limit_bytes=VMEM_LIMIT),
        name="route",
    )(index, arrived)


def front_kernel(tiles, tile, pivot_ref, factor_ref, arrived_ref, solved_ref, update_ref, p_high, p_low, s_high, s_low):
    step = pl.program_id(0)
    blocks = arrived_ref.shape[1]
    per_tile = tile // BLK

    @pl.when(step == 0)
    def _():
        for block in range(blocks):
            high, low = split(arrived_ref[:, block].reshape(BLK, NRHS))
            p_high[pl.ds(block * BLK, BLK)] = high
            p_low[pl.ds(block * BLK, BLK)] = low

    @pl.when(step < tiles)
    def _():
        value = product(pivot_ref[...], p_high[...], p_low[...])
        solved_ref[...] = value
        high, low = split(value)
        start = pl.multiple_of(step * tile, tile)
        s_high[pl.ds(start, tile)] = high
        s_low[pl.ds(start, tile)] = low

    @pl.when(step >= tiles)
    def _():
        value = product(factor_ref[...], s_high[...], s_low[...])
        for block in range(per_tile):
            update_ref[:, (step - tiles) * per_tile + block] = value[block * BLK : (block + 1) * BLK].reshape(
                update_ref.shape[0], SUB, NRHS
            )


def front(arrived, pivot_inverse, update_factor):
    rows, half = arrived.shape[:2]
    order = half * BLK
    tile = 256
    tiles = order // tile
    return pl.pallas_call(
        functools.partial(front_kernel, tiles, tile),
        grid=(2 * tiles,),
        out_shape=(
            jax.ShapeDtypeStruct((order, NRHS), jnp.float32),
            jax.ShapeDtypeStruct((rows, half, SUB, NRHS), jnp.float32),
        ),
        in_specs=[
            pl.BlockSpec((tile, order), lambda i: (jnp.minimum(i, tiles - 1), 0)),
            pl.BlockSpec((tile, order), lambda i: (jnp.maximum(i - tiles, 0), 0)),
            pl.BlockSpec((rows, half, SUB, NRHS), lambda i: (0, 0, 0, 0)),
        ],
        out_specs=(
            pl.BlockSpec((tile, NRHS), lambda i: (jnp.minimum(i, tiles - 1), 0)),
            pl.BlockSpec((rows, half, SUB, NRHS), lambda i: (0, 0, 0, 0)),
        ),
        scratch_shapes=[pltpu.VMEM((order, NRHS), jnp.bfloat16)] * 4,
        compiler_params=pltpu.CompilerParams(vmem_limit_bytes=VMEM_LIMIT),
        name="front",
    )(pivot_inverse, update_factor, arrived)


def subtract_kernel(rows, half, index_ref, arrived_ref, start_ref, acc_ref):
    stride = RB_DEV + half
    acc_ref[...] = start_ref[...]

    def add(owner, carry):
        for block in range(half):
            root = index_ref[owner * stride + RB_DEV + block]
            acc_ref[root] -= arrived_ref[owner * half + block]
        return carry

    lax.fori_loop(0, rows, add, 0)


def subtract(index, arrived, start, rows, half):
    return pl.pallas_call(
        functools.partial(subtract_kernel, rows, half),
        out_shape=jax.ShapeDtypeStruct(start.shape, jnp.float32),
        in_specs=[
            pl.BlockSpec(memory_space=pltpu.SMEM),
            pl.BlockSpec(memory_space=pltpu.VMEM),
            pl.BlockSpec(memory_space=pltpu.VMEM),
        ],
        out_specs=pl.BlockSpec(memory_space=pltpu.VMEM),
        compiler_params=pltpu.CompilerParams(vmem_limit_bytes=VMEM_LIMIT),
        name="subtract",
    )(index, arrived, start)


def root_kernel(gathered_ref, inverse_ref, out_ref, r_high, r_low):
    @pl.when(pl.program_id(0) == 0)
    def _():
        for block in range(gathered_ref.shape[1]):
            high, low = split(gathered_ref[:, block].reshape(BLK, NRHS))
            r_high[pl.ds(block * BLK, BLK)] = high
            r_low[pl.ds(block * BLK, BLK)] = low

    out_ref[...] = product(inverse_ref[...], r_high[...], r_low[...])


def root(gathered, root_inverse):
    height, depth = root_inverse.shape
    tile = 256
    return pl.pallas_call(
        root_kernel,
        grid=(height // tile,),
        out_shape=jax.ShapeDtypeStruct((height, NRHS), jnp.float32),
        in_specs=[
            pl.BlockSpec(gathered.shape, lambda i: (0, 0, 0, 0)),
            pl.BlockSpec((tile, depth), lambda i: (i, 0)),
        ],
        out_specs=pl.BlockSpec((tile, NRHS), lambda i: (i, 0)),
        scratch_shapes=[pltpu.VMEM((depth, NRHS), jnp.bfloat16)] * 2,
        compiler_params=pltpu.CompilerParams(vmem_limit_bytes=VMEM_LIMIT),
        name="root",
    )(gathered, root_inverse)


def shards(rhs, block_target, pivot_inverse, update_factor, root_inverse, update_map):
    rows = lax.axis_size("row")
    cols = lax.axis_size("col")
    half = update_map.shape[0]
    index = lax.all_gather(jnp.concatenate([block_target, update_map]), "row", axis=0, tiled=True)
    sliced = rhs.reshape(RB_DEV, rows, SUB, NRHS).transpose(1, 0, 2, 3)
    arrived = exchange(sliced, "row").reshape(rows * RB_DEV, SUB, NRHS)
    send, direct = route(index, arrived, rows, half)
    pivot = exchange(send.reshape(rows, half, SUB, NRHS), "row")
    solved, update = front(pivot, pivot_inverse, update_factor)
    returned = exchange(update, "row").reshape(rows * half, SUB, NRHS)
    partial_root = subtract(index, returned, direct, rows, half)
    per_col = BLK // cols
    piece = jnp.sum(exchange(partial_root.reshape(cols, per_col, SUB, NRHS), "col"), axis=0)
    gathered = exchange(jnp.broadcast_to(piece[None], (rows,) + piece.shape), "row")
    partial_value = root(gathered, root_inverse)
    root_solution = jnp.sum(exchange(partial_value.reshape(cols, -1, NRHS), "col"), axis=0)
    return (solved, root_solution)


def solution(mesh):
    return jax.shard_map(
        shards,
        mesh=mesh,
        in_specs=(
            P(("row", "col"), None),
            P(("row", "col")),
            P(("row", "col"), None),
            P(("row", "col"), None),
            P("row", "col"),
            P(("row", "col")),
        ),
        out_specs=(P(("row", "col"), None), P(("row", "col"), None)),
        check_vma=False,
    )
```

time: 914 us -> 188 us (0.21)
  waiting for transfers between devices: 797 us -> 0.01 us
  blocking collectives: 0 us -> 144 us
  local copies, waits for them, and re-layouts: 51.8 us -> 5.32 us
  matrix products: 30.2 us -> 0 us
  Pallas kernels: 0 us -> 26.6 us
  between operations: 13.9 us -> 1.35 us
    reduce_scatter x2 -> x0, waiting for transfers between devices: 695 us -> none  [the longest x1 665 us: shards(): lax.psum_scatter(reordered, ('row', 'col'), scatter_dimension=0, tiled=True)]
    all_to_all x0 -> x5, blocking collectives: none -> 108 us  [exchange(): return lax.all_to_all(x, axis, split_axis=0, concat_axis=0, tiled=True)]
    all_to_all x2 -> x1, waiting for transfers between devices: 60.1 us -> 0.01 us  [exchange(): return lax.all_to_all(x, axis, split_axis=0, concat_axis=0, tiled=True)]
    all_gather x1 -> x0, waiting for transfers between devices: 41.7 us -> none  [shards(): lax.all_gather(root_piece, 'row', axis=0, tiled=True)]
    unnamed x0 -> x1, blocking collectives: none -> 36.2 us
    dot_general x3 -> x0, matrix products: 30.2 us -> none  [the longest x1 17.4 us: shards(): jnp.dot(root_inverse, lax.all_gather(root_piece, 'row', axis=0, tiled=Tru...]
    pallas_call x0 -> x4, Pallas kernels: none -> 26.6 us  [the longest x1 9.99 us: front(): pl.pallas_call(functools.partial(front_kernel, tiles, tile), grid=(2 * ti...]
    reshape x6 -> x1, local copies, waits for them, and re-layouts: 25.6 us -> 3.17 us  [shards(): sliced = rhs.reshape(RB_DEV, rows, SUB, NRHS).transpose(1, 0, 2, 3)]
  transfers between devices with their start and end apart: 5 -> 1, of which waited for: 4 -> 0; matrix products, arithmetic and copies ran while one was open for 2% -> 0% of each run, Pallas kernels for 0% -> 0%
where the time goes in v1:
time: 188 us; the launch traced here: 187 us
  blocking collectives  144 us (77%)
  Pallas kernels  26.6 us (14%)
  starting transfers between devices  8.26 us (4%)
  local copies, waits for them, and re-layouts  5.32 us (3%)
    all_to_all x5, blocking collectives, exchange(): return lax.all_to_all(x, axis, split_axis=0, concat_axis=0, tiled=True)  108 us
    unnamed x1, blocking collectives  36.2 us
    pallas_call x1, Pallas kernels, front(): pl.pallas_call(functools.partial(front_kernel, tiles, tile), grid=(2 * ti...  9.99 us
    all_to_all x1, starting transfers between devices, exchange(): return lax.all_to_all(x, axis, split_axis=0, concat_axis=0, tiled=True)  8.26 us
    pallas_call x1, Pallas kernels, root(): pl.pallas_call(root_kernel, grid=(height // tile,), out_shape=jax.ShapeDt...  8.01 us
    pallas_call x1, Pallas kernels, route(): pl.pallas_call(functools.partial(route_kernel, rows, half), out_shape=(sh...  5.56 us
  transfers between devices with their start and end apart: 1, of which 0 were waited for; matrix products, arithmetic and copies ran while one was open for 0% of the time, Pallas kernels for 0%

profile of v1, /device:TPU:0, one launch (start us, length us, event | category | flops | bytes accessed | tf_op | source)
XLA Modules:
  0.0 186.8 jit_solution(1431628007053135807)
XLA Ops:
  0.6 3.2 %copy.10 = f32[16,16,8,256]{3,2,0,1:T(8,128)} copy(f32[16,16,8,256]{3,2,1,0:T(8,128)} %bitcast.15) | data formatting | bytes 4194304 | tf_op jit(solution)/shard_map/reshape | solution.py:198
  3.8 0.0 copy-start.3
  3.8 0.0 copy-start.1
  3.8 0.0 copy-start.2
  3.8 8.3 %all-to-all-start = ((f32[16,16,8,256]{3,2,1,0:T(8,128)}), f32[16,16,8,256]{3,2,1,0:T(8,128)S(1)}, u32[]{:S(2)}, u32[]{:S(2)}) async-start(f32[16,16,8,256]{3,2,1,0:T(8,128)} %bitcast.11), calls=%async_computation | async-start | bytes 4194304 | tf_op jit(solution)/shard_map/all_to_all | solution.py:32
  12.1 0.0 copy-done.3
  12.1 0.6 dynamic-slice
  13.3 0.0 copy-done.1
  13.3 0.0 copy-done.2
  13.4 0.2 add_dynamic-update-slice_fusion
  13.5 36.2 %all-reduce.index_ref = s32[384]{0:T(512)} all-reduce(s32[384]{0:T(512)S(1)} %add_dynamic-update-slice_fusion), channel_id=1, replica_groups=mesh['row'=16,'col'=8] {'row'}, use_global_device_ids=true, to_apply=%add | all-reduce | flops 384 | bytes 3072
  49.7 0.0 all-to-all-done
  49.7 0.0 copy-start
  49.7 1.4 copy-done
  51.0 5.6 %route.1 = (f32[128,8,256]{2,1,0:T(8,128)}, f32[128,8,256]{2,1,0:T(8,128)}) custom-call(s32[384]{0:T(512)} %all-reduce.index_ref, f32[256,8,256]{2,1,0:T(8,128)} %bitcast.10), custom_call_target="tpu_custom_call" | custom-call | tf_op jit(solution)/shard_map/route/pallas_call | solution.py:65
  56.6 19.3 %all_to_all.30.arrived_ref = f32[16,8,8,256]{3,2,1,0:T(8,128)} all-to-all(f32[16,8,8,256]{3,2,1,0:T(8,128)} %bitcast.16), channel_id=1, replica_groups=mesh['row'=16,'col'=8] {'row'}, dimensions={0} | all-to-all | bytes 2097152 | tf_op jit(solution)/shard_map/all_to_all | solution.py:32
  75.9 10.0 %front.1 = (f32[1024,256]{1,0:T(8,128)}, f32[16,8,8,256]{3,2,1,0:T(8,128)}) custom-call(f32[1024,1024]{1,0:T(8,128)} %pivot_ref.1, f32[1024,1024]{1,0:T(8,128)} %factor_ref.1, f32[16,8,8,256]{3,2,1,0:T(8,128)} %all_to_all.30.arrived_ref), custom_call_target="tpu_custom_call" | custom-call | tf_op jit(solution)/shard_map/front/pallas_call | solution.py:114
  85.9 17.3 %all_to_all.31 = f32[16,8,8,256]{3,2,1,0:T(8,128)} all-to-all(f32[16,8,8,256]{3,2,1,0:T(8,128)} %get-tuple-element.8), channel_id=1, replica_groups=mesh['row'=16,'col'=8] {'row'}, dimensions={0} | all-to-all | bytes 2097152 | tf_op jit(solution)/shard_map/all_to_all | solution.py:32
  103.2 3.1 %subtract.1 = f32[128,8,256]{2,1,0:T(8,128)} custom-call(s32[384]{0:T(512)} %all-reduce.index_ref, f32[128,8,256]{2,1,0:T(8,128)} %bitcast.12, f32[128,8,256]{2,1,0:T(8,128)} %get-tuple-element.9.start_ref), custom_call_target="tpu_custom_call" | custom-call | tf_op jit(solution)/shard_map/subtract/pallas_call | solution.py:150
  106.2 20.4 %all_to_all.32 = f32[8,16,8,256]{3,2,1,0:T(8,128)S(1)} all-to-all(f32[8,16,8,256]{3,2,1,0:T(8,128)} %bitcast.13), channel_id=1, replica_groups=mesh['row'=16,'col'=8] {'col'}, dimensions={0} | all-to-all | bytes 2097152 | tf_op jit(solution)/shard_map/all_to_all | solution.py:32
  126.6 0.1 reduce_sum.18
  126.7 0.2 broadcast_in_dim.2
  126.9 31.6 %all_to_all.33.gathered_ref = f32[16,16,8,256]{3,2,1,0:T(8,128)} all-to-all(f32[16,16,8,256]{3,2,1,0:T(8,128)S(1)} %broadcast_in_dim.2), channel_id=1, replica_groups=mesh['row'=16,'col'=8] {'row'}, dimensions={0} | all-to-all | bytes 4194304 | tf_op jit(solution)/shard_map/all_to_all | solution.py:32
  158.5 8.0 %root.1 = f32[1024,256]{1,0:T(8,128)} custom-call(f32[16,16,8,256]{3,2,1,0:T(8,128)} %all_to_all.33.gathered_ref, f32[1024,2048]{1,0:T(8,128)} %inverse_ref.1), custom_call_target="tpu_custom_call" | custom-call | tf_op jit(solution)/shard_map/root/pallas_call | solution.py:178
  166.5 19.6 %all_to_all.34 = f32[8,128,256]{2,1,0:T(8,128)S(1)} all-to-all(f32[8,128,256]{2,1,0:T(8,128)} %bitcast.14), channel_id=1, replica_groups=mesh['row'=16,'col'=8] {'col'}, dimensions={0} | all-to-all | bytes 2097152 | tf_op jit(solution)/shard_map/all_to_all | solution.py:32
  186.1 0.7 reduce_sum.19
  (1 shorter events, 0.0 us)
Async XLA Ops:
  3.8 8.3 %copy-start.3 = (u32[128]{0:T(128)S(1)}, u32[128]{0:T(128)}, u32[]{:S(2)}) copy-start(u32[128]{0:T(128)} %constant.6) | copy-start | bytes 1540
  3.8 9.5 %copy-start.1 = (s32[8]{0:T(128)S(1)}, s32[8]{0:T(128)}, u32[]{:S(2)}) copy-start(s32[8]{0:T(128)} %param.11) | copy-start | bytes 100
  3.8 9.5 %copy-start.2 = (s32[16]{0:T(128)S(1)}, s32[16]{0:T(128)}, u32[]{:S(2)}) copy-start(s32[16]{0:T(128)} %param.7) | copy-start | bytes 196
  3.8 45.9 %all-to-all-start = ((f32[16,16,8,256]{3,2,1,0:T(8,128)}), f32[16,16,8,256]{3,2,1,0:T(8,128)S(1)}, u32[]{:S(2)}, u32[]{:S(2)}) async-start(f32[16,16,8,256]{3,2,1,0:T(8,128)} %bitcast.11), calls=%async_computation | async-start | bytes 4194304 | tf_op jit(solution)/shard_map/all_to_all | solution.py:32
  49.7 1.4 copy-start

commit v2 on v0

v2 whole, which is shorter than its diff:
```python
import functools

import jax
import jax.numpy as jnp
from jax import lax
from jax.experimental import pallas as pl
from jax.experimental.pallas import tpu as pltpu
from jax.sharding import PartitionSpec as P

BLK = 128
NRHS = 256
RB_DEV = 16
SUB = 8
LANES = 128
CORES = 2
VMEM_LIMIT = 8 << 20
TILE = 256
VMEM = pl.BlockSpec(memory_space=pltpu.VMEM)
SMEM = pl.BlockSpec(memory_space=pltpu.SMEM)
ANY = pl.BlockSpec(memory_space=pl.ANY)
PARAMS = pltpu.CompilerParams(vmem_limit_bytes=VMEM_LIMIT)


def f32(*shape):
    return jax.ShapeDtypeStruct(shape, jnp.float32)


def far(x):
    return pltpu.with_memory_space_constraint(x, pltpu.HBM)


def split(x):
    high = x.astype(jnp.bfloat16)
    low = (x - high.astype(jnp.float32)).astype(jnp.bfloat16)
    return high, low


def product(a_high, a_low, b_high, b_low):
    out = jnp.dot(a_high, b_high, preferred_element_type=jnp.float32)
    out += jnp.dot(a_high, b_low, preferred_element_type=jnp.float32)
    out += jnp.dot(a_low, b_high, preferred_element_type=jnp.float32)
    return out


def exchange(x, axis):
    return lax.all_to_all(x, axis, split_axis=0, concat_axis=0, tiled=True)


def pack_kernel(rows, half, target_ref, map_ref, rhs_ref, out_ref, targets, roots, sems, table_sems):
    tables = [
        pltpu.make_async_copy(target_ref, targets, table_sems.at[0]),
        pltpu.make_async_copy(map_ref, roots, table_sems.at[1]),
    ]
    copies = [
        pltpu.make_async_copy(rhs_ref.at[block], out_ref.at[:, block], sems.at[block]) for block in range(RB_DEV)
    ]
    for copy in tables + copies:
        copy.start()
    for copy in tables:
        copy.wait()
    lane = lax.broadcasted_iota(jnp.int32, (SUB, NRHS), 1)
    words = jnp.zeros((SUB, NRHS), jnp.int32)
    for i in range(RB_DEV):
        words = jnp.where(lane == i, targets[i], words)
    for i in range(half):
        words = jnp.where(lane == RB_DEV + i, roots[i], words)
    words = words.astype(jnp.float32)
    for peer in range(rows):
        out_ref[peer, RB_DEV] = words
    for copy in copies:
        copy.wait()


def pack(rhs, block_target, update_map, rows):
    half = update_map.shape[0]
    return pl.pallas_call(
        functools.partial(pack_kernel, rows, half),
        out_shape=f32(rows, RB_DEV + 1, SUB, NRHS),
        in_specs=[ANY] * 3,
        out_specs=VMEM,
        scratch_shapes=[
            pltpu.SMEM((RB_DEV,), jnp.int32),
            pltpu.SMEM((half,), jnp.int32),
            pltpu.SemaphoreType.DMA((RB_DEV,)),
            pltpu.SemaphoreType.DMA((2,)),
        ],
        compiler_params=PARAMS,
        name="pack",
    )(far(block_target), far(update_map), far(rhs.reshape(RB_DEV, rows, SUB, NRHS)))


def relative(root, per_col, chips):
    me = lax.axis_index("col")
    col = root // per_col
    distance = (col // CORES - me // CORES + chips) % chips
    other = (col + me) % CORES
    return (other * chips + distance) * per_col + root % per_col


def route_kernel(rows, half, chips, arrived_ref, send_ref, acc_ref, root_ref, words, table, sem):
    slots = rows * half
    received = arrived_ref[:, RB_DEV, 0, :LANES].astype(jnp.int32)
    lane = lax.broadcasted_iota(jnp.int32, received.shape, 1)
    owner = received // RB_DEV
    slot = received % RB_DEV
    entry = owner * half + slot + jnp.where(slot < half, 0, slots - half)
    words[...] = jnp.where(lane < RB_DEV, entry, slots + relative(received, BLK // (CORES * chips), chips))
    copy = pltpu.make_async_copy(words, table, sem)
    copy.start()
    acc_ref[...] = jnp.zeros_like(acc_ref)
    copy.wait()

    def place(source, carry):
        for block in range(RB_DEV):
            where = table[source, block]
            update = where >= slots
            index = lax.bitwise_and(where, slots - 1)
            root = table[lax.shift_right_logical(index, half.bit_length() - 1), RB_DEV + lax.bitwise_and(index, half - 1)]
            position = jnp.where(update, root, index)
            acc_ref[position] += arrived_ref[source, block]
        return carry

    lax.fori_loop(0, rows, place, 0)
    send_ref[...] = acc_ref[pl.ds(0, slots)]
    for row in range(rows):
        for block in range(half):
            root_ref[row * half + block] = table[row, RB_DEV + block]


def route(arrived, rows, half, chips):
    slots = rows * half
    return pl.pallas_call(
        functools.partial(route_kernel, rows, half, chips),
        out_shape=(
            f32(slots, SUB, NRHS),
            f32(slots + BLK, SUB, NRHS),
            jax.ShapeDtypeStruct((slots,), jnp.int32),
        ),
        in_specs=[VMEM],
        out_specs=(VMEM, VMEM, SMEM),
        scratch_shapes=[
            pltpu.VMEM((rows, LANES), jnp.int32),
            pltpu.SMEM((rows, LANES), jnp.int32),
            pltpu.SemaphoreType.DMA,
        ],
        compiler_params=PARAMS,
        name="route",
    )(arrived)


def split_into(value, high_ref, low_ref, start):
    high, low = split(value)
    high_ref[pl.ds(start, value.shape[0])] = high
    low_ref[pl.ds(start, value.shape[0])] = low


def front_kernel(arrived_ref, pivot_ref, factor_ref, solved_ref, update_ref, p_high, p_low, s_high, s_low):
    rows, blocks = arrived_ref.shape[:2]
    order = blocks * BLK
    for block in range(blocks):
        split_into(arrived_ref[:, block].reshape(BLK, NRHS), p_high, p_low, block * BLK)
    for start in range(0, order, TILE):
        here, depth = pl.ds(start, TILE), pl.ds(0, start + TILE)
        value = product(*split(pivot_ref[here, depth]), p_high[depth], p_low[depth])
        solved_ref[here] = value
        split_into(value, s_high, s_low, start)
    for start in range(0, order, TILE):
        value = product(*split(factor_ref[pl.ds(start, TILE)]), s_high[...], s_low[...])
        for block in range(TILE // BLK):
            part = value[block * BLK : (block + 1) * BLK]
            update_ref[:, start // BLK + block] = part.reshape(rows, SUB, NRHS)


def front(arrived, pivot_inverse, update_factor):
    rows, half = arrived.shape[:2]
    order = half * BLK
    return pl.pallas_call(
        front_kernel,
        out_shape=(f32(order, NRHS), f32(rows, half, SUB, NRHS)),
        in_specs=[VMEM] * 3,
        out_specs=(VMEM, VMEM),
        scratch_shapes=[pltpu.VMEM((order, NRHS), jnp.bfloat16)] * 4,
        compiler_params=PARAMS,
        name="front",
    )(arrived, pivot_inverse, update_factor)


def subtract_kernel(rows, half, root_ref, arrived_ref, start_ref, mine_ref, other_ref, acc):
    slots = rows * half
    acc[...] = start_ref[pl.ds(slots, BLK)]

    def add(owner, carry):
        for block in range(half):
            acc[root_ref[owner * half + block] - slots] -= arrived_ref[owner, block]
        return carry

    lax.fori_loop(0, rows, add, 0)
    mine_ref[...] = acc[pl.ds(0, BLK // CORES)].reshape(mine_ref.shape)
    other_ref[...] = acc[pl.ds(BLK // CORES, BLK // CORES)].reshape(mine_ref.shape)


def subtract(root, arrived, start, chips):
    rows, half = arrived.shape[:2]
    out = f32(chips, BLK // (CORES * chips), SUB, NRHS)
    return pl.pallas_call(
        functools.partial(subtract_kernel, rows, half),
        out_shape=(out, out),
        in_specs=[SMEM, VMEM, VMEM],
        out_specs=(VMEM, VMEM),
        scratch_shapes=[pltpu.VMEM((BLK, SUB, NRHS), jnp.float32)],
        compiler_params=PARAMS,
        name="subtract",
    )(root, arrived, start)


def root_kernel(chips, gathered_ref, inverse_ref, mine_ref, other_ref, r_high, r_low):
    for block in range(gathered_ref.shape[1]):
        split_into(gathered_ref[:, block].reshape(BLK, NRHS), r_high, r_low, block * BLK)
    me = lax.axis_index("col")
    height = mine_ref.shape[1]
    for distance in range(chips):
        chip = (me // CORES + distance) % chips
        strip = inverse_ref[pl.ds(pl.multiple_of(chip * CORES * height, CORES * height), CORES * height)]
        value = product(*split(strip), r_high[...], r_low[...])
        first, second = value[:height], value[height:]
        even = me % CORES == 0
        mine_ref[distance] = jnp.where(even, first, second)
        other_ref[distance] = jnp.where(even, second, first)


def root(gathered, root_inverse, chips):
    height, depth = root_inverse.shape
    out = f32(chips, height // (CORES * chips), NRHS)
    return pl.pallas_call(
        functools.partial(root_kernel, chips),
        out_shape=(out, out),
        in_specs=[VMEM] * 2,
        out_specs=(VMEM, VMEM),
        scratch_shapes=[pltpu.VMEM((depth, NRHS), jnp.bfloat16)] * 2,
        compiler_params=PARAMS,
        name="root",
    )(gathered, root_inverse)


def reduce_cols(mine, other, cols):
    chips = cols // CORES
    sibling = lax.ppermute(other, "col", [(c, c ^ 1) for c in range(cols)])
    total = mine[0] + sibling[0]
    parts = [
        lax.ppermute(
            mine[distance] + sibling[distance], "col", [(c, (c + CORES * distance) % cols) for c in range(cols)]
        )
        for distance in range(1, chips)
    ]
    for part in parts:
        total = total + part
    return total


def shards(rhs, block_target, pivot_inverse, update_factor, root_inverse, update_map):
    rows = lax.axis_size("row")
    cols = lax.axis_size("col")
    chips = cols // CORES
    half = update_map.shape[0]
    arrived = exchange(pack(rhs, block_target, update_map, rows), "row")
    send, direct, root_index = route(arrived, rows, half, chips)
    pivot = exchange(send.reshape(rows, half, SUB, NRHS), "row")
    solved, update = front(pivot, pivot_inverse, update_factor)
    returned = exchange(update, "row")
    piece = reduce_cols(*subtract(root_index, returned, direct, chips), cols)
    gathered = exchange(jnp.broadcast_to(piece[None], (rows,) + piece.shape), "row")
    root_solution = reduce_cols(*root(gathered, root_inverse, chips), cols)
    return (solved, root_solution)


def solution(mesh):
    return jax.shard_map(
        shards,
        mesh=mesh,
        in_specs=(
            P(("row", "col"), None),
            P(("row", "col")),
            P(("row", "col"), None),
            P(("row", "col"), None),
            P("row", "col"),
            P(("row", "col")),
        ),
        out_specs=(P(("row", "col"), None), P(("row", "col"), None)),
        check_vma=False,
    )
```

time: 914 us -> 145 us (0.16)
  waiting for transfers between devices: 797 us -> 15.8 us
  blocking collectives: 0 us -> 106 us
  local copies, waits for them, and re-layouts: 51.8 us -> 0.21 us
  matrix products: 30.2 us -> 0 us
  between operations: 13.9 us -> 0.72 us
  Pallas kernels: 0 us -> 13.1 us
    reduce_scatter x2 -> x0, waiting for transfers between devices: 695 us -> none  [the longest x1 665 us: shards(): lax.psum_scatter(reordered, ('row', 'col'), scatter_dimension=0, tiled=True)]
    all_to_all x0 -> x4, blocking collectives: none -> 106 us  [exchange(): return lax.all_to_all(x, axis, split_axis=0, concat_axis=0, tiled=True)]
    all_to_all x2 -> x0, waiting for transfers between devices: 60.1 us -> none  [the longest x1 60.1 us: shards(): lax.all_to_all(outgoing.reshape(row_count, CAP, BLK * NRHS), 'row', split...]
    all_gather x1 -> x0, waiting for transfers between devices: 41.7 us -> none  [shards(): lax.all_gather(root_piece, 'row', axis=0, tiled=True)]
    dot_general x3 -> x0, matrix products: 30.2 us -> none  [the longest x1 17.4 us: shards(): jnp.dot(root_inverse, lax.all_gather(root_piece, 'row', axis=0, tiled=Tru...]
    reshape x6 -> x0, local copies, waits for them, and re-layouts: 25.6 us -> none  [the longest x1 11.6 us: shards(): scattered.reshape(col_count, row_count, BLK, NRHS).transpose(1, 0, 2, 3)]
    ppermute x0 -> x8, waiting for transfers between devices: none -> 15.8 us  [the longest x6 12 us: reduce_cols(): lax.ppermute(mine[distance] + sibling[distance], 'col', [(c, (c + CORES *...]
    all_to_all x2 -> x0, starting transfers between devices: 15.5 us -> none  [the longest x1 8.13 us: shards(): lax.all_to_all(outgoing_slots.reshape(row_count, CAP), 'row', split_axis=...]
  transfers between devices with their start and end apart: 5 -> 8, of which waited for: 4 -> 8; matrix products, arithmetic and copies ran while one was open for 2% -> 0% of each run, Pallas kernels for 0% -> 0%
where the time goes in v2:
time: 145 us
  blocking collectives  106 us (73%)
  waiting for transfers between devices  15.8 us (11%)
  Pallas kernels  13.1 us (9%)
  starting transfers between devices  8.59 us (6%)
    all_to_all x4, blocking collectives, exchange(): return lax.all_to_all(x, axis, split_axis=0, concat_axis=0, tiled=True)  106 us
    ppermute x6, waiting for transfers between devices, reduce_cols(): lax.ppermute(mine[distance] + sibling[distance], 'col', [(c, (c + CORES *...  12 us
    ppermute x6, starting transfers between devices, reduce_cols(): lax.ppermute(mine[distance] + sibling[distance], 'col', [(c, (c + CORES *...  8.42 us
    ppermute x2, waiting for transfers between devices, reduce_cols(): sibling = lax.ppermute(other, 'col', [(c, c ^ 1) for c in range(cols)])  3.79 us
    pallas_call x1, Pallas kernels, front(): pl.pallas_call(front_kernel, out_shape=(f32(order, NRHS), f32(rows, half,...  3.68 us
    pallas_call x1, Pallas kernels, root(): pl.pallas_call(functools.partial(root_kernel, chips), out_shape=(out, out...  3.42 us
    pallas_call x1, Pallas kernels, route(): pl.pallas_call(functools.partial(route_kernel, rows, half, chips), out_sh...  3.14 us
  transfers between devices with their start and end apart: 8, of which 8 were waited for; matrix products, arithmetic and copies ran while one was open for 0% of the time, Pallas kernels for 0%

profile of v2, /device:TPU:0, one launch (start us, length us, event | category | flops | bytes accessed | tf_op | source)
XLA Modules:
  0.0 145.2 jit_solution(15332943729206741856)
XLA Ops:
  0.6 1.8 %pack.1 = f32[16,17,8,256]{3,2,1,0:T(8,128)S(1)} custom-call(s32[16]{0:T(128)} %target_ref.1, s32[8]{0:T(128)} %map_ref.1, f32[16,16,8,256]{3,2,1,0:T(8,128)} %bitcast.33), custom_call_target="tpu_custom_call" | custom-call | tf_op jit(solution)/shard_map/pack/pallas_call | solution.py:76
  2.4 0.0 copy-start.1
  2.4 38.0 %all_to_all.20.arrived_ref = f32[16,17,8,256]{3,2,1,0:T(8,128)S(1)} all-to-all(f32[16,17,8,256]{3,2,1,0:T(8,128)S(1)} %pack.1), channel_id=1, replica_groups=mesh['row'=16,'col'=8] {'row'}, dimensions={0} | all-to-all | bytes 4456448 | tf_op jit(solution)/shard_map/all_to_all | solution.py:46
  40.4 0.0 copy-start
  40.4 3.1 %route.1 = (f32[128,8,256]{2,1,0:T(8,128)S(1)}, f32[256,8,256]{2,1,0:T(8,128)S(1)}, s32[128]{0:T(128)S(1)}) custom-call(f32[16,17,8,256]{3,2,1,0:T(8,128)S(1)} %all_to_all.20.arrived_ref), custom_call_target="tpu_custom_call" | custom-call | tf_op jit(solution)/shard_map/route/pallas_call | solution.py:132
  43.5 19.3 %all_to_all.21.arrived_ref = f32[16,8,8,256]{3,2,1,0:T(8,128)S(1)} all-to-all(f32[16,8,8,256]{3,2,1,0:T(8,128)S(1)} %bitcast.32), channel_id=1, replica_groups=mesh['row'=16,'col'=8] {'row'}, dimensions={0} | all-to-all | bytes 2097152 | tf_op jit(solution)/shard_map/all_to_all | solution.py:46
  62.9 0.0 copy-done.1
  62.9 0.0 copy-done
  62.9 0.0 slice-start
  62.9 3.7 %front.1 = (f32[1024,256]{1,0:T(8,128)}, f32[16,8,8,256]{3,2,1,0:T(8,128)S(1)}) custom-call(f32[16,8,8,256]{3,2,1,0:T(8,128)S(1)} %all_to_all.21.arrived_ref, f32[1024,1024]{1,0:T(8,128)S(1)} %copy-done, f32[1024,1024]{1,0:T(8,128)S(1)} %copy-done.1), custom_call_target="tpu_custom_call" | custom-call | tf_op jit(solution)/shard_map/front/pallas_call | solution.py:177
  66.6 17.9 %all_to_all.22.arrived_ref = f32[16,8,8,256]{3,2,1,0:T(8,128)S(1)} all-to-all(f32[16,8,8,256]{3,2,1,0:T(8,128)S(1)} %get-tuple-element.14), channel_id=1, replica_groups=mesh['row'=16,'col'=8] {'row'}, dimensions={0} | all-to-all | bytes 2097152 | tf_op jit(solution)/shard_map/all_to_all | solution.py:46
  84.4 0.0 slice-start.1
  84.4 1.1 subtract.1
  85.5 0.1 collective-permute-start
  85.6 1.9 %collective-permute-done = f32[4,16,8,256]{3,2,1,0:T(8,128)S(1)} collective-permute-done((f32[4,16,8,256]{3,2,1,0:T(8,128)S(1)}, f32[4,16,8,256]{3,2,1,0:T(8,128)S(1)}, u32[]{:S(2)}, u32[]{:S(2)}) %collective-permute-start) | collective-permute-done | bytes 524320 | tf_op jit(solution)/shard_map/ppermute | solution.py:247
  87.5 0.1 fusion.9
  87.6 1.6 %collective-permute-start.1 = (f32[16,8,256]{2,1,0:T(8,128)S(1)}, f32[16,8,256]{2,1,0:T(8,128)S(1)}, u32[]{:S(2)}, u32[]{:S(2)}) collective-permute-start(f32[16,8,256]{2,1,0:T(8,128)S(1)} %get-tuple-element.23), channel_id=1, source_target_pairs={{0,2},{1,3},{2,4},{3,5},{4,6},{5,7},{6,0},{7,1},{8,10},{9,11},{10,... | collective-permute-start | bytes 393224 | tf_op jit(solution)/shard_map/ppermute | solution.py:250
  89.1 1.7 %collective-permute-start.3 = (f32[16,8,256]{2,1,0:T(8,128)S(1)}, f32[16,8,256]{2,1,0:T(8,128)S(1)}, u32[]{:S(2)}, u32[]{:S(2)}) collective-permute-start(f32[16,8,256]{2,1,0:T(8,128)S(1)} %get-tuple-element.24), channel_id=1, source_target_pairs={{0,6},{1,7},{2,0},{3,1},{4,2},{5,3},{6,4},{7,5},{8,14},{9,15},{10,... | collective-permute-start | bytes 393224 | tf_op jit(solution)/shard_map/ppermute | solution.py:250
  90.9 1.8 %collective-permute-start.2 = (f32[16,8,256]{2,1,0:T(8,128)S(1)}, f32[16,8,256]{2,1,0:T(8,128)S(1)}, u32[]{:S(2)}, u32[]{:S(2)}) collective-permute-start(f32[16,8,256]{2,1,0:T(8,128)S(1)} %get-tuple-element.25), channel_id=1, source_target_pairs={{0,4},{1,5},{2,6},{3,7},{4,0},{5,1},{6,2},{7,3},{8,12},{9,13},{10,... | collective-permute-start | bytes 393224 | tf_op jit(solution)/shard_map/ppermute | solution.py:250
  92.7 1.7 %collective-permute-done.1 = f32[16,8,256]{2,1,0:T(8,128)S(1)} collective-permute-done((f32[16,8,256]{2,1,0:T(8,128)S(1)}, f32[16,8,256]{2,1,0:T(8,128)S(1)}, u32[]{:S(2)}, u32[]{:S(2)}) %collective-permute-start.1) | collective-permute-done | bytes 131104 | tf_op jit(solution)/shard_map/ppermute | solution.py:250
  94.4 2.1 %collective-permute-done.3 = f32[16,8,256]{2,1,0:T(8,128)S(1)} collective-permute-done((f32[16,8,256]{2,1,0:T(8,128)S(1)}, f32[16,8,256]{2,1,0:T(8,128)S(1)}, u32[]{:S(2)}, u32[]{:S(2)}) %collective-permute-start.3) | collective-permute-done | bytes 131104 | tf_op jit(solution)/shard_map/ppermute | solution.py:250
  96.5 1.7 %collective-permute-done.2 = f32[16,8,256]{2,1,0:T(8,128)S(1)} collective-permute-done((f32[16,8,256]{2,1,0:T(8,128)S(1)}, f32[16,8,256]{2,1,0:T(8,128)S(1)}, u32[]{:S(2)}, u32[]{:S(2)}) %collective-permute-start.2) | collective-permute-done | bytes 131104 | tf_op jit(solution)/shard_map/ppermute | solution.py:250
  98.2 0.2 broadcast_in_dim.2
  98.4 30.8 %all_to_all.23.gathered_ref = f32[16,16,8,256]{3,2,1,0:T(8,128)S(1)} all-to-all(f32[16,16,8,256]{3,2,1,0:T(8,128)S(1)} %broadcast_in_dim.2), channel_id=1, replica_groups=mesh['row'=16,'col'=8] {'row'}, dimensions={0} | all-to-all | bytes 4194304 | tf_op jit(solution)/shard_map/all_to_all | solution.py:46
  129.2 0.0 slice-done
  129.2 0.0 slice-done.1
  129.2 3.4 %root.1 = (f32[4,128,256]{2,1,0:T(8,128)S(1)}, f32[4,128,256]{2,1,0:T(8,128)S(1)}) custom-call(f32[16,16,8,256]{3,2,1,0:T(8,128)S(1)} %all_to_all.23.gathered_ref, f32[1024,2048]{1,0:T(8,128)S(1)} %bitcast.31), custom_call_target="tpu_custom_call" | custom-call | tf_op jit(solution)/shard_map/root/pallas_call | solution.py:234
  132.6 0.1 collective-permute-start.4
  132.7 1.9 %collective-permute-done.4 = f32[4,128,256]{2,1,0:T(8,128)S(1)} collective-permute-done((f32[4,128,256]{2,1,0:T(8,128)S(1)}, f32[4,128,256]{2,1,0:T(8,128)S(1)}, u32[]{:S(2)}, u32[]{:S(2)}) %collective-permute-start.4) | collective-permute-done | bytes 524320 | tf_op jit(solution)/shard_map/ppermute | solution.py:247
  134.6 0.1 fusion.2
  134.7 1.1 collective-permute-start.5
  135.7 2.2 %collective-permute-start.7 = (f32[128,256]{1,0:T(8,128)S(1)}, f32[128,256]{1,0:T(8,128)S(1)}, u32[]{:S(2)}, u32[]{:S(2)}) collective-permute-start(f32[128,256]{1,0:T(8,128)S(1)} %get-tuple-element.21), channel_id=1, source_target_pairs={{0,6},{1,7},{2,0},{3,1},{4,2},{5,3},{6,4},{7,5},{8,14},{9,15},{10,... | collective-permute-start | bytes 393224 | tf_op jit(solution)/shard_map/ppermute | solution.py:250
  138.0 0.0 collective-permute-start.6
  138.0 3.5 %collective-permute-done.5 = f32[128,256]{1,0:T(8,128)S(1)} collective-permute-done((f32[128,256]{1,0:T(8,128)S(1)}, f32[128,256]{1,0:T(8,128)S(1)}, u32[]{:S(2)}, u32[]{:S(2)}) %collective-permute-start.5) | collective-permute-done | bytes 131104 | tf_op jit(solution)/shard_map/ppermute | solution.py:250
  141.5 2.1 %collective-permute-done.7 = f32[128,256]{1,0:T(8,128)S(1)} collective-permute-done((f32[128,256]{1,0:T(8,128)S(1)}, f32[128,256]{1,0:T(8,128)S(1)}, u32[]{:S(2)}, u32[]{:S(2)}) %collective-permute-start.7) | collective-permute-done | bytes 131104 | tf_op jit(solution)/shard_map/ppermute | solution.py:250
  143.6 0.9 collective-permute-done.6
  144.5 0.7 fusion.6
  (2 shorter events, 0.0 us)
Async XLA Ops:
  2.4 60.5 %copy-start.1 = (f32[1024,1024]{1,0:T(8,128)S(1)}, f32[1024,1024]{1,0:T(8,128)}, u32[]{:S(2)}) copy-start(f32[1024,1024]{1,0:T(8,128)} %factor_ref.1) | copy-start | bytes 12582916
  40.4 22.5 %copy-start = (f32[1024,1024]{1,0:T(8,128)S(1)}, f32[1024,1024]{1,0:T(8,128)}, u32[]{:S(2)}) copy-start(f32[1024,1024]{1,0:T(8,128)} %pivot_ref.1) | copy-start | bytes 12582916
  62.9 66.3 %slice-start = ((s8[8388608]{0:T(1024)(128)(4,1)}), s8[4194304]{0:T(1024)(128)(4,1)S(1)}, s32[]{:S(2)}) async-start(s8[8388608]{0:T(1024)(128)(4,1)} %bitcast.30), calls=%async_computation.4 | async-start | bytes 8388608
  84.4 44.8 %slice-start.1 = ((s8[8388608]{0:T(1024)(128)(4,1)}), s8[4194304]{0:T(1024)(128)(4,1)S(1)}, s32[]{:S(2)}) async-start(s8[8388608]{0:T(1024)(128)(4,1)} %bitcast.30), calls=%async_computation.5 | async-start | bytes 8388608
  85.5 2.0 %collective-permute-start = (f32[4,16,8,256]{3,2,1,0:T(8,128)S(1)}, f32[4,16,8,256]{3,2,1,0:T(8,128)S(1)}, u32[]{:S(2)}, u32[]{:S(2)}) collective-permute-start(f32[4,16,8,256]{3,2,1,0:T(8,128)S(1)} %get-tuple-element.17), channel_id=1, source_target_pairs={{0,1},{1,0},{2,3},{3,2},{4,5},{5,4},{6,7},{7,6},{8,9},{9,8},{10,11... | collective-permute-start | bytes 1572872 | tf_op jit(solution)/shard_map/ppermute | solution.py:247
  87.6 6.8 %collective-permute-start.1 = (f32[16,8,256]{2,1,0:T(8,128)S(1)}, f32[16,8,256]{2,1,0:T(8,128)S(1)}, u32[]{:S(2)}, u32[]{:S(2)}) collective-permute-start(f32[16,8,256]{2,1,0:T(8,128)S(1)} %get-tuple-element.23), channel_id=1, source_target_pairs={{0,2},{1,3},{2,4},{3,5},{4,6},{5,7},{6,0},{7,1},{8,10},{9,11},{10,... | collective-permute-start | bytes 393224 | tf_op jit(solution)/shard_map/ppermute | solution.py:250
  89.1 7.4 %collective-permute-start.3 = (f32[16,8,256]{2,1,0:T(8,128)S(1)}, f32[16,8,256]{2,1,0:T(8,128)S(1)}, u32[]{:S(2)}, u32[]{:S(2)}) collective-permute-start(f32[16,8,256]{2,1,0:T(8,128)S(1)} %get-tuple-element.24), channel_id=1, source_target_pairs={{0,6},{1,7},{2,0},{3,1},{4,2},{5,3},{6,4},{7,5},{8,14},{9,15},{10,... | collective-permute-start | bytes 393224 | tf_op jit(solution)/shard_map/ppermute | solution.py:250
  90.9 7.3 %collective-permute-start.2 = (f32[16,8,256]{2,1,0:T(8,128)S(1)}, f32[16,8,256]{2,1,0:T(8,128)S(1)}, u32[]{:S(2)}, u32[]{:S(2)}) collective-permute-start(f32[16,8,256]{2,1,0:T(8,128)S(1)} %get-tuple-element.25), channel_id=1, source_target_pairs={{0,4},{1,5},{2,6},{3,7},{4,0},{5,1},{6,2},{7,3},{8,12},{9,13},{10,... | collective-permute-start | bytes 393224 | tf_op jit(solution)/shard_map/ppermute | solution.py:250
  132.6 2.0 %collective-permute-start.4 = (f32[4,128,256]{2,1,0:T(8,128)S(1)}, f32[4,128,256]{2,1,0:T(8,128)S(1)}, u32[]{:S(2)}, u32[]{:S(2)}) collective-permute-start(f32[4,128,256]{2,1,0:T(8,128)S(1)} %get-tuple-element.19), channel_id=1, source_target_pairs={{0,1},{1,0},{2,3},{3,2},{4,5},{5,4},{6,7},{7,6},{8,9},{9,8},{10,11... | collective-permute-start | bytes 1572872 | tf_op jit(solution)/shard_map/ppermute | solution.py:247
  134.7 6.8 %collective-permute-start.5 = (f32[128,256]{1,0:T(8,128)S(1)}, f32[128,256]{1,0:T(8,128)S(1)}, u32[]{:S(2)}, u32[]{:S(2)}) collective-permute-start(f32[128,256]{1,0:T(8,128)S(1)} %get-tuple-element.20), channel_id=1, source_target_pairs={{0,2},{1,3},{2,4},{3,5},{4,6},{5,7},{6,0},{7,1},{8,10},{9,11},{10,... | collective-permute-start | bytes 393224 | tf_op jit(solution)/shard_map/ppermute | solution.py:250
  135.7 7.9 %collective-permute-start.7 = (f32[128,256]{1,0:T(8,128)S(1)}, f32[128,256]{1,0:T(8,128)S(1)}, u32[]{:S(2)}, u32[]{:S(2)}) collective-permute-start(f32[128,256]{1,0:T(8,128)S(1)} %get-tuple-element.21), channel_id=1, source_target_pairs={{0,6},{1,7},{2,0},{3,1},{4,2},{5,3},{6,4},{7,5},{8,14},{9,15},{10,... | collective-permute-start | bytes 393224 | tf_op jit(solution)/shard_map/ppermute | solution.py:250
  138.0 6.5 %collective-permute-start.6 = (f32[128,256]{1,0:T(8,128)S(1)}, f32[128,256]{1,0:T(8,128)S(1)}, u32[]{:S(2)}, u32[]{:S(2)}) collective-permute-start(f32[128,256]{1,0:T(8,128)S(1)} %get-tuple-element.22), channel_id=1, source_target_pairs={{0,4},{1,5},{2,6},{3,7},{4,0},{5,1},{6,2},{7,3},{8,12},{9,13},{10,... | collective-permute-start | bytes 393224 | tf_op jit(solution)/shard_map/ppermute | solution.py:250

commit v3 on v2

v3 whole, which is shorter than its diff:
```python
import functools

import jax
import jax.numpy as jnp
from jax import lax
from jax.experimental import pallas as pl
from jax.experimental.pallas import tpu as pltpu
from jax.sharding import PartitionSpec as P

BLK = 128
NRHS = 256
RB_DEV = 16
SUB = 8
LANES = 128
TILES = NRHS // LANES
CORES = 2
VMEM_LIMIT = 8 << 20
TILE = 256
VMEM = pl.BlockSpec(memory_space=pltpu.VMEM)
SMEM = pl.BlockSpec(memory_space=pltpu.SMEM)
ANY = pl.BlockSpec(memory_space=pl.ANY)
PARAMS = pltpu.CompilerParams(vmem_limit_bytes=VMEM_LIMIT)


def f32(*shape):
    return jax.ShapeDtypeStruct(shape, jnp.float32)


def far(x):
    return pltpu.with_memory_space_constraint(x, pltpu.HBM)


def split(x):
    high = x.astype(jnp.bfloat16)
    low = (x - high.astype(jnp.float32)).astype(jnp.bfloat16)
    return high, low


def product(a_high, a_low, b_high, b_low):
    out = jnp.dot(a_high, b_high, preferred_element_type=jnp.float32)
    out += jnp.dot(a_high, b_low, preferred_element_type=jnp.float32)
    out += jnp.dot(a_low, b_high, preferred_element_type=jnp.float32)
    return out


def exchange(x, axis):
    return lax.all_to_all(x, axis, split_axis=0, concat_axis=0, tiled=True)


def pack_kernel(rows, half, target_ref, map_ref, rhs_ref, out_ref, targets, roots, sems, table_sems):
    tables = [
        pltpu.make_async_copy(target_ref, targets, table_sems.at[0]),
        pltpu.make_async_copy(map_ref, roots, table_sems.at[1]),
    ]
    copies = [
        pltpu.make_async_copy(
            rhs_ref.at[block, :, :, pl.ds(lane * LANES, LANES)],
            out_ref.at[:, block * TILES + lane],
            sems.at[block * TILES + lane],
        )
        for block in range(RB_DEV)
        for lane in range(TILES)
    ]
    for copy in tables + copies:
        copy.start()
    for copy in tables:
        copy.wait()
    lane = lax.broadcasted_iota(jnp.int32, (SUB, LANES), 1)
    words = jnp.zeros((SUB, LANES), jnp.int32)
    for i in range(RB_DEV):
        words = jnp.where(lane == i, targets[i], words)
    for i in range(half):
        words = jnp.where(lane == RB_DEV + i, roots[i], words)
    words = words.astype(jnp.float32)
    for peer in range(rows):
        out_ref[peer, RB_DEV * TILES] = words
    for copy in copies:
        copy.wait()


def pack(rhs, block_target, update_map, rows):
    half = update_map.shape[0]
    return pl.pallas_call(
        functools.partial(pack_kernel, rows, half),
        out_shape=f32(rows, RB_DEV * TILES + 1, SUB, LANES),
        in_specs=[ANY] * 3,
        out_specs=VMEM,
        scratch_shapes=[
            pltpu.SMEM((RB_DEV,), jnp.int32),
            pltpu.SMEM((half,), jnp.int32),
            pltpu.SemaphoreType.DMA((RB_DEV * TILES,)),
            pltpu.SemaphoreType.DMA((2,)),
        ],
        compiler_params=PARAMS,
        name="pack",
    )(far(block_target), far(update_map), far(rhs.reshape(RB_DEV, rows, SUB, NRHS)))


def relative(root, per_col, chips):
    me = lax.axis_index("col")
    col = root // per_col
    distance = (col // CORES - me // CORES + chips) % chips
    other = (col + me) % CORES
    return (other * chips + distance) * per_col + root % per_col


def route_kernel(rows, half, chips, arrived_ref, send_ref, acc_ref, words, table, sem):
    slots = rows * half
    received = arrived_ref[:, RB_DEV * TILES, 0].astype(jnp.int32)
    lane = lax.broadcasted_iota(jnp.int32, received.shape, 1)
    owner = received // RB_DEV
    slot = received % RB_DEV
    entry = owner * half + slot + jnp.where(slot < half, 0, slots - half)
    words[...] = jnp.where(lane < RB_DEV, entry, slots + relative(received, BLK // (CORES * chips), chips))
    copy = pltpu.make_async_copy(words, table, sem)
    copy.start()
    acc_ref[...] = jnp.zeros_like(acc_ref)
    copy.wait()

    def place(source, carry):
        for block in range(RB_DEV):
            where = table[source, block]
            update = where >= slots
            index = lax.bitwise_and(where, slots - 1)
            root = table[lax.shift_right_logical(index, half.bit_length() - 1), RB_DEV + lax.bitwise_and(index, half - 1)]
            position = jnp.where(update, root, index)
            acc_ref[position] += arrived_ref[source, pl.ds(block * TILES, TILES)]
        return carry

    lax.fori_loop(0, rows, place, 0)
    send_ref[...] = acc_ref[pl.ds(0, slots)]


def route(arrived, rows, half, chips):
    slots = rows * half
    return pl.pallas_call(
        functools.partial(route_kernel, rows, half, chips),
        out_shape=(
            f32(slots, TILES, SUB, LANES),
            f32(slots + BLK, TILES, SUB, LANES),
            jax.ShapeDtypeStruct((rows, LANES), jnp.int32),
        ),
        in_specs=[VMEM],
        out_specs=(VMEM, VMEM, VMEM),
        scratch_shapes=[
            pltpu.SMEM((rows, LANES), jnp.int32),
            pltpu.SemaphoreType.DMA,
        ],
        compiler_params=PARAMS,
        name="route",
    )(arrived)


def split_into(value, high_ref, low_ref, start, lane=0):
    high, low = split(value)
    here = (pl.ds(start, value.shape[0]), pl.ds(lane * LANES, value.shape[1]))
    high_ref[here] = high
    low_ref[here] = low


def join_slices(slices_ref, high_ref, low_ref):
    for block in range(slices_ref.shape[1]):
        for lane in range(TILES):
            split_into(slices_ref[:, block, lane].reshape(BLK, LANES), high_ref, low_ref, block * BLK, lane)


def front_kernel(arrived_ref, pivot_ref, factor_ref, solved_ref, update_ref, p_high, p_low, s_high, s_low):
    rows, blocks = arrived_ref.shape[:2]
    order = blocks * BLK
    join_slices(arrived_ref, p_high, p_low)
    for start in range(0, order, TILE):
        here, depth = pl.ds(start, TILE), pl.ds(0, start + TILE)
        value = product(*split(pivot_ref[here, depth]), p_high[depth], p_low[depth])
        solved_ref[here] = value
        split_into(value, s_high, s_low, start)
    for start in range(0, order, TILE):
        value = product(*split(factor_ref[pl.ds(start, TILE)]), s_high[...], s_low[...])
        for block in range(TILE // BLK):
            for lane in range(TILES):
                part = value[block * BLK : (block + 1) * BLK, lane * LANES : (lane + 1) * LANES]
                update_ref[:, start // BLK + block, lane] = part.reshape(rows, SUB, LANES)


def front(arrived, pivot_inverse, update_factor):
    rows, half = arrived.shape[:2]
    order = half * BLK
    return pl.pallas_call(
        front_kernel,
        out_shape=(f32(order, NRHS), f32(rows, half, TILES, SUB, LANES)),
        in_specs=[VMEM] * 3,
        out_specs=(VMEM, VMEM),
        scratch_shapes=[pltpu.VMEM((order, NRHS), jnp.bfloat16)] * 4,
        compiler_params=PARAMS,
        name="front",
    )(arrived, pivot_inverse, update_factor)


def subtract_kernel(rows, half, words_ref, arrived_ref, start_ref, mine_ref, other_ref, acc):
    slots = rows * half
    acc[...] = start_ref[pl.ds(slots, BLK)]

    def add(owner, carry):
        for block in range(half):
            acc[words_ref[owner, RB_DEV + block] - slots] -= arrived_ref[owner, block]
        return carry

    lax.fori_loop(0, rows, add, 0)
    mine_ref[...] = acc[pl.ds(0, BLK // CORES)].reshape(mine_ref.shape)
    other_ref[...] = acc[pl.ds(BLK // CORES, BLK // CORES)].reshape(mine_ref.shape)


def subtract(words, arrived, start, chips):
    rows, half = arrived.shape[:2]
    out = f32(chips, BLK // (CORES * chips), TILES, SUB, LANES)
    return pl.pallas_call(
        functools.partial(subtract_kernel, rows, half),
        out_shape=(out, out),
        in_specs=[SMEM, VMEM, VMEM],
        out_specs=(VMEM, VMEM),
        scratch_shapes=[pltpu.VMEM((BLK, TILES, SUB, LANES), jnp.float32)],
        compiler_params=PARAMS,
        name="subtract",
    )(words, arrived, start)


def root_rows(swap, inverse_ref, r_high, r_low, out_ref):
    me = lax.axis_index("col")
    chips, height = out_ref.shape[:2]
    for distance in range(chips):
        base = ((me // CORES + distance) % chips * CORES + (me + swap) % CORES) * height
        strip = inverse_ref[pl.ds(pl.multiple_of(base, height), height)]
        out_ref[distance] = product(*split(strip), r_high[...], r_low[...])


def root_other_kernel(gathered_ref, inverse_ref, other_ref, high_ref, low_ref):
    join_slices(gathered_ref, high_ref, low_ref)
    root_rows(1, inverse_ref, high_ref, low_ref, other_ref)


def root_mine_kernel(high_ref, low_ref, inverse_ref, mine_ref):
    root_rows(0, inverse_ref, high_ref, low_ref, mine_ref)


def root(gathered, root_inverse, chips):
    height, depth = root_inverse.shape
    out = f32(chips, height // (CORES * chips), NRHS)
    half = jax.ShapeDtypeStruct((depth, NRHS), jnp.bfloat16)
    cost = pl.CostEstimate(flops=3 * height * depth * NRHS, transcendentals=0, bytes_accessed=2 * height * depth)
    other, high, low = pl.pallas_call(
        root_other_kernel,
        out_shape=(out, half, half),
        in_specs=[VMEM] * 2,
        out_specs=(VMEM,) * 3,
        compiler_params=PARAMS,
        cost_estimate=cost,
        name="root_other",
    )(gathered, root_inverse)
    mine = pl.pallas_call(
        root_mine_kernel,
        out_shape=out,
        in_specs=[VMEM] * 3,
        out_specs=VMEM,
        compiler_params=PARAMS,
        cost_estimate=cost,
        name="root_mine",
    )(high, low, root_inverse)
    return mine, other


def reduce_cols(mine, other, cols):
    chips = cols // CORES
    sibling = lax.ppermute(other, "col", [(c, c ^ 1) for c in range(cols)])
    total = mine[0] + sibling[0]
    parts = [
        lax.ppermute(
            mine[distance] + sibling[distance], "col", [(c, (c + CORES * distance) % cols) for c in range(cols)]
        )
        for distance in range(1, chips)
    ]
    for part in parts:
        total = total + part
    return total


def shards(rhs, block_target, pivot_inverse, update_factor, root_inverse, update_map):
    rows = lax.axis_size("row")
    cols = lax.axis_size("col")
    chips = cols // CORES
    half = update_map.shape[0]
    arrived = exchange(pack(rhs, block_target, update_map, rows), "row")
    send, direct, words = route(arrived, rows, half, chips)
    pivot = exchange(send.reshape(rows, half, TILES, SUB, LANES), "row")
    solved, update = front(pivot, pivot_inverse, update_factor)
    returned = exchange(update, "row")
    piece = reduce_cols(*subtract(words, returned, direct, chips), cols)
    gathered = exchange(jnp.broadcast_to(piece[None], (rows,) + piece.shape), "row")
    root_solution = reduce_cols(*root(gathered, root_inverse, chips), cols)
    return (solved, root_solution)


def solution(mesh):
    return jax.shard_map(
        shards,
        mesh=mesh,
        in_specs=(
            P(("row", "col"), None),
            P(("row", "col")),
            P(("row", "col"), None),
            P(("row", "col"), None),
            P("row", "col"),
            P(("row", "col")),
        ),
        out_specs=(P(("row", "col"), None), P(("row", "col"), None)),
        check_vma=False,
    )
```

time: 145 us -> 142 us (0.979)
  waiting for transfers between devices: 15.8 us -> 14.3 us
    ppermute x2, waiting for transfers between devices: 3.79 us -> 2 us  [reduce_cols(): sibling = lax.ppermute(other, 'col', [(c, c ^ 1) for c in range(cols)])]
    pallas_call x1 -> x2, Pallas kernels: 3.42 us -> 3.8 us  [the longest x1 2.02 us: root(): pl.pallas_call(root_other_kernel, out_shape=(out, half, half), in_specs=[...]
  transfers between devices with their start and end apart: 8 -> 8, of which waited for: 8 -> 8; matrix products, arithmetic and copies ran while one was open for 0% -> 0% of each run, Pallas kernels for 0% -> 1%
where the time goes in v3:
time: 142 us
  blocking collectives  105 us (74%)
  waiting for transfers between devices  14.3 us (10%)
  Pallas kernels  12.1 us (9%)
  starting transfers between devices  8.59 us (6%)
    all_to_all x4, blocking collectives, exchange(): return lax.all_to_all(x, axis, split_axis=0, concat_axis=0, tiled=True)  105 us
    ppermute x6, waiting for transfers between devices, reduce_cols(): lax.ppermute(mine[distance] + sibling[distance], 'col', [(c, (c + CORES *...  12.3 us
    ppermute x6, starting transfers between devices, reduce_cols(): lax.ppermute(mine[distance] + sibling[distance], 'col', [(c, (c + CORES *...  8.42 us
    pallas_call x1, Pallas kernels, front(): pl.pallas_call(front_kernel, out_shape=(f32(order, NRHS), f32(rows, half,...  2.89 us
  transfers between devices with their start and end apart: 8, of which 8 were waited for; matrix products, arithmetic and copies ran while one was open for 0% of the time, Pallas kernels for 1%

profile of v3, /device:TPU:0, one launch (start us, length us, event | category | flops | bytes accessed | tf_op | source)
XLA Modules:
  0.0 142.2 jit_solution(537952180238984754)
XLA Ops:
  0.6 1.9 %pack.1 = f32[16,33,8,128]{3,2,1,0:T(8,128)S(1)} custom-call(s32[16]{0:T(128)} %target_ref.1, s32[8]{0:T(128)} %map_ref.1, f32[16,16,8,256]{3,2,1,0:T(8,128)} %bitcast.33), custom_call_target="tpu_custom_call" | custom-call | tf_op jit(solution)/shard_map/pack/pallas_call | solution.py:83
  2.5 0.0 copy-start.1
  2.5 37.3 %all_to_all.20.arrived_ref = f32[16,33,8,128]{3,2,1,0:T(8,128)S(1)} all-to-all(f32[16,33,8,128]{3,2,1,0:T(8,128)S(1)} %pack.1), channel_id=1, replica_groups=mesh['row'=16,'col'=8] {'row'}, dimensions={0} | all-to-all | bytes 4325376 | tf_op jit(solution)/shard_map/all_to_all | solution.py:47
  39.8 0.0 copy-start
  39.8 2.4 %route.1 = (f32[128,2,8,128]{3,2,1,0:T(8,128)S(1)}, f32[256,2,8,128]{3,2,1,0:T(8,128)S(1)}, s32[16,128]{1,0:T(8,128)S(1)}) custom-call(f32[16,33,8,128]{3,2,1,0:T(8,128)S(1)} %all_to_all.20.arrived_ref), custom_call_target="tpu_custom_call" | custom-call | tf_op jit(solution)/shard_map/route/pallas_call | solution.py:136
  42.2 19.4 %all_to_all.21.arrived_ref = f32[16,8,2,8,128]{4,3,2,1,0:T(8,128)S(1)} all-to-all(f32[16,8,2,8,128]{4,3,2,1,0:T(8,128)S(1)} %bitcast.32), channel_id=1, replica_groups=mesh['row'=16,'col'=8] {'row'}, dimensions={0} | all-to-all | bytes 2097152 | tf_op jit(solution)/shard_map/all_to_all | solution.py:47
  61.6 0.0 copy-done.1
  61.6 0.0 copy-done
  61.6 0.0 slice-start
  61.6 2.9 %front.1 = (f32[1024,256]{1,0:T(8,128)}, f32[16,8,2,8,128]{4,3,2,1,0:T(8,128)S(1)}) custom-call(f32[16,8,2,8,128]{4,3,2,1,0:T(8,128)S(1)} %all_to_all.21.arrived_ref, f32[1024,1024]{1,0:T(8,128)S(1)} %copy-done, f32[1024,1024]{1,0:T(8,128)S(1)} %copy-done.1), custom_call_target="tpu_custom_call" | custom-call | tf_op jit(solution)/shard_map/front/pallas_call | solution.py:187
  64.5 17.9 %all_to_all.22.arrived_ref = f32[16,8,2,8,128]{4,3,2,1,0:T(8,128)S(1)} all-to-all(f32[16,8,2,8,128]{4,3,2,1,0:T(8,128)S(1)} %get-tuple-element.15), channel_id=1, replica_groups=mesh['row'=16,'col'=8] {'row'}, dimensions={0} | all-to-all | bytes 2097152 | tf_op jit(solution)/shard_map/all_to_all | solution.py:47
  82.4 0.0 slice-start.1
  82.4 1.2 subtract.1
  83.6 0.1 collective-permute-start
  83.7 1.9 %collective-permute-done = f32[4,16,2,8,128]{4,3,2,1,0:T(8,128)S(1)} collective-permute-done((f32[4,16,2,8,128]{4,3,2,1,0:T(8,128)S(1)}, f32[4,16,2,8,128]{4,3,2,1,0:T(8,128)S(1)}, u32[]{:S(2)}, u32[]{:S(2)}) %collective-permute-start) | collective-permute-done | bytes 524320 | tf_op jit(solution)/shard_map/ppermute | solution.py:272
  85.6 0.1 fusion.9
  85.7 1.5 %collective-permute-start.1 = (f32[16,2,8,128]{3,2,1,0:T(8,128)S(1)}, f32[16,2,8,128]{3,2,1,0:T(8,128)S(1)}, u32[]{:S(2)}, u32[]{:S(2)}) collective-permute-start(f32[16,2,8,128]{3,2,1,0:T(8,128)S(1)} %get-tuple-element.25), channel_id=1, source_target_pairs={{0,2},{1,3},{2,4},{3,5},{4,6},{5,7},{6,0},{7,1},{8,10},{9,11},{10,... | collective-permute-start | bytes 393224 | tf_op jit(solution)/shard_map/ppermute | solution.py:275
  87.2 1.8 %collective-permute-start.3 = (f32[16,2,8,128]{3,2,1,0:T(8,128)S(1)}, f32[16,2,8,128]{3,2,1,0:T(8,128)S(1)}, u32[]{:S(2)}, u32[]{:S(2)}) collective-permute-start(f32[16,2,8,128]{3,2,1,0:T(8,128)S(1)} %get-tuple-element.26), channel_id=1, source_target_pairs={{0,6},{1,7},{2,0},{3,1},{4,2},{5,3},{6,4},{7,5},{8,14},{9,15},{10,... | collective-permute-start | bytes 393224 | tf_op jit(solution)/shard_map/ppermute | solution.py:275
  89.0 1.8 %collective-permute-start.2 = (f32[16,2,8,128]{3,2,1,0:T(8,128)S(1)}, f32[16,2,8,128]{3,2,1,0:T(8,128)S(1)}, u32[]{:S(2)}, u32[]{:S(2)}) collective-permute-start(f32[16,2,8,128]{3,2,1,0:T(8,128)S(1)} %get-tuple-element.27), channel_id=1, source_target_pairs={{0,4},{1,5},{2,6},{3,7},{4,0},{5,1},{6,2},{7,3},{8,12},{9,13},{10,... | collective-permute-start | bytes 393224 | tf_op jit(solution)/shard_map/ppermute | solution.py:275
  90.8 1.7 %collective-permute-done.1 = f32[16,2,8,128]{3,2,1,0:T(8,128)S(1)} collective-permute-done((f32[16,2,8,128]{3,2,1,0:T(8,128)S(1)}, f32[16,2,8,128]{3,2,1,0:T(8,128)S(1)}, u32[]{:S(2)}, u32[]{:S(2)}) %collective-permute-start.1) | collective-permute-done | bytes 131104 | tf_op jit(solution)/shard_map/ppermute | solution.py:275
  92.5 2.1 %collective-permute-done.3 = f32[16,2,8,128]{3,2,1,0:T(8,128)S(1)} collective-permute-done((f32[16,2,8,128]{3,2,1,0:T(8,128)S(1)}, f32[16,2,8,128]{3,2,1,0:T(8,128)S(1)}, u32[]{:S(2)}, u32[]{:S(2)}) %collective-permute-start.3) | collective-permute-done | bytes 131104 | tf_op jit(solution)/shard_map/ppermute | solution.py:275
  94.6 1.7 %collective-permute-done.2 = f32[16,2,8,128]{3,2,1,0:T(8,128)S(1)} collective-permute-done((f32[16,2,8,128]{3,2,1,0:T(8,128)S(1)}, f32[16,2,8,128]{3,2,1,0:T(8,128)S(1)}, u32[]{:S(2)}, u32[]{:S(2)}) %collective-permute-start.2) | collective-permute-done | bytes 131104 | tf_op jit(solution)/shard_map/ppermute | solution.py:275
  96.3 0.2 broadcast_in_dim.2
  96.5 30.8 %all_to_all.23.gathered_ref = f32[16,16,2,8,128]{4,3,2,1,0:T(8,128)S(1)} all-to-all(f32[16,16,2,8,128]{4,3,2,1,0:T(8,128)S(1)} %broadcast_in_dim.2), channel_id=1, replica_groups=mesh['row'=16,'col'=8] {'row'}, dimensions={0} | all-to-all | bytes 4194304 | tf_op jit(solution)/shard_map/all_to_all | solution.py:47
  127.3 0.0 slice-done
  127.3 0.0 slice-done.1
  127.3 2.0 %root_other.1 = (f32[4,128,256]{2,1,0:T(8,128)S(1)}, bf16[2048,256]{1,0:T(8,128)(2,1)S(1)}, bf16[2048,256]{1,0:T(8,128)(2,1)S(1)}) custom-call(f32[16,16,2,8,128]{4,3,2,1,0:T(8,128)S(1)} %all_to_all.23.gathered_ref, f32[1024,2048]{1,0:T(8,128)S(1)} %bitcast.31), custom_call_target="tpu_custom_call" | custom-call | flops 1610612736 | bytes 4194304 | tf_op jit(solution)/shard_map/root_other/pallas_call | solution.py:249
  129.3 0.1 collective-permute-start.4
  129.4 1.8 %root_mine.1 = f32[4,128,256]{2,1,0:T(8,128)S(1)} custom-call(bf16[2048,256]{1,0:T(8,128)(2,1)S(1)} %get-tuple-element.19.high_ref, bf16[2048,256]{1,0:T(8,128)(2,1)S(1)} %get-tuple-element.20.low_ref, f32[1024,2048]{1,0:T(8,128)S(1)} %bitcast.31), custom_call_target="tpu_custom_call" | custom-call | flops 1610612736 | bytes 4194304 | tf_op jit(solution)/shard_map/root_mine/pallas_call | solution.py:258
  131.2 0.1 collective-permute-done.4
  131.3 0.1 fusion.2
  131.4 1.1 collective-permute-start.5
  132.4 2.2 %collective-permute-start.7 = (f32[128,256]{1,0:T(8,128)S(1)}, f32[128,256]{1,0:T(8,128)S(1)}, u32[]{:S(2)}, u32[]{:S(2)}) collective-permute-start(f32[128,256]{1,0:T(8,128)S(1)} %get-tuple-element.23), channel_id=1, source_target_pairs={{0,6},{1,7},{2,0},{3,1},{4,2},{5,3},{6,4},{7,5},{8,14},{9,15},{10,... | collective-permute-start | bytes 393224 | tf_op jit(solution)/shard_map/ppermute | solution.py:275
  134.7 0.0 collective-permute-start.6
  134.7 3.8 %collective-permute-done.5 = f32[128,256]{1,0:T(8,128)S(1)} collective-permute-done((f32[128,256]{1,0:T(8,128)S(1)}, f32[128,256]{1,0:T(8,128)S(1)}, u32[]{:S(2)}, u32[]{:S(2)}) %collective-permute-start.5) | collective-permute-done | bytes 131104 | tf_op jit(solution)/shard_map/ppermute | solution.py:275
  138.5 2.1 %collective-permute-done.7 = f32[128,256]{1,0:T(8,128)S(1)} collective-permute-done((f32[128,256]{1,0:T(8,128)S(1)}, f32[128,256]{1,0:T(8,128)S(1)}, u32[]{:S(2)}, u32[]{:S(2)}) %collective-permute-start.7) | collective-permute-done | bytes 131104 | tf_op jit(solution)/shard_map/ppermute | solution.py:275
  140.6 0.9 collective-permute-done.6
  141.5 0.7 fusion.6
  (2 shorter events, 0.0 us)
Async XLA Ops:
  2.5 59.1 %copy-start.1 = (f32[1024,1024]{1,0:T(8,128)S(1)}, f32[1024,1024]{1,0:T(8,128)}, u32[]{:S(2)}) copy-start(f32[1024,1024]{1,0:T(8,128)} %factor_ref.1) | copy-start | bytes 12582916
  39.8 21.8 %copy-start = (f32[1024,1024]{1,0:T(8,128)S(1)}, f32[1024,1024]{1,0:T(8,128)}, u32[]{:S(2)}) copy-start(f32[1024,1024]{1,0:T(8,128)} %pivot_ref.1) | copy-start | bytes 12582916
  61.6 65.7 %slice-start = ((s8[8388608]{0:T(1024)(128)(4,1)}), s8[4194304]{0:T(1024)(128)(4,1)S(1)}, s32[]{:S(2)}) async-start(s8[8388608]{0:T(1024)(128)(4,1)} %bitcast.30), calls=%async_computation.4 | async-start | bytes 8388608
  82.4 44.9 %slice-start.1 = ((s8[8388608]{0:T(1024)(128)(4,1)}), s8[4194304]{0:T(1024)(128)(4,1)S(1)}, s32[]{:S(2)}) async-start(s8[8388608]{0:T(1024)(128)(4,1)} %bitcast.30), calls=%async_computation.5 | async-start | bytes 8388608
  83.6 2.0 %collective-permute-start = (f32[4,16,2,8,128]{4,3,2,1,0:T(8,128)S(1)}, f32[4,16,2,8,128]{4,3,2,1,0:T(8,128)S(1)}, u32[]{:S(2)}, u32[]{:S(2)}) collective-permute-start(f32[4,16,2,8,128]{4,3,2,1,0:T(8,128)S(1)} %get-tuple-element.18), channel_id=1, source_target_pairs={{0,1},{1,0},{2,3},{3,2},{4,5},{5,4},{6,7},{7,6},{8,9},{9,8},{10,11... | collective-permute-start | bytes 1572872 | tf_op jit(solution)/shard_map/ppermute | solution.py:272
  85.7 6.8 %collective-permute-start.1 = (f32[16,2,8,128]{3,2,1,0:T(8,128)S(1)}, f32[16,2,8,128]{3,2,1,0:T(8,128)S(1)}, u32[]{:S(2)}, u32[]{:S(2)}) collective-permute-start(f32[16,2,8,128]{3,2,1,0:T(8,128)S(1)} %get-tuple-element.25), channel_id=1, source_target_pairs={{0,2},{1,3},{2,4},{3,5},{4,6},{5,7},{6,0},{7,1},{8,10},{9,11},{10,... | collective-permute-start | bytes 393224 | tf_op jit(solution)/shard_map/ppermute | solution.py:275
  87.2 7.4 %collective-permute-start.3 = (f32[16,2,8,128]{3,2,1,0:T(8,128)S(1)}, f32[16,2,8,128]{3,2,1,0:T(8,128)S(1)}, u32[]{:S(2)}, u32[]{:S(2)}) collective-permute-start(f32[16,2,8,128]{3,2,1,0:T(8,128)S(1)} %get-tuple-element.26), channel_id=1, source_target_pairs={{0,6},{1,7},{2,0},{3,1},{4,2},{5,3},{6,4},{7,5},{8,14},{9,15},{10,... | collective-permute-start | bytes 393224 | tf_op jit(solution)/shard_map/ppermute | solution.py:275
  89.0 7.3 %collective-permute-start.2 = (f32[16,2,8,128]{3,2,1,0:T(8,128)S(1)}, f32[16,2,8,128]{3,2,1,0:T(8,128)S(1)}, u32[]{:S(2)}, u32[]{:S(2)}) collective-permute-start(f32[16,2,8,128]{3,2,1,0:T(8,128)S(1)} %get-tuple-element.27), channel_id=1, source_target_pairs={{0,4},{1,5},{2,6},{3,7},{4,0},{5,1},{6,2},{7,3},{8,12},{9,13},{10,... | collective-permute-start | bytes 393224 | tf_op jit(solution)/shard_map/ppermute | solution.py:275
  129.3 2.0 %collective-permute-start.4 = (f32[4,128,256]{2,1,0:T(8,128)S(1)}, f32[4,128,256]{2,1,0:T(8,128)S(1)}, u32[]{:S(2)}, u32[]{:S(2)}) collective-permute-start(f32[4,128,256]{2,1,0:T(8,128)S(1)} %get-tuple-element.21), channel_id=1, source_target_pairs={{0,1},{1,0},{2,3},{3,2},{4,5},{5,4},{6,7},{7,6},{8,9},{9,8},{10,11... | collective-permute-start | bytes 1572872 | tf_op jit(solution)/shard_map/ppermute | solution.py:272
  131.4 7.1 %collective-permute-start.5 = (f32[128,256]{1,0:T(8,128)S(1)}, f32[128,256]{1,0:T(8,128)S(1)}, u32[]{:S(2)}, u32[]{:S(2)}) collective-permute-start(f32[128,256]{1,0:T(8,128)S(1)} %get-tuple-element.22), channel_id=1, source_target_pairs={{0,2},{1,3},{2,4},{3,5},{4,6},{5,7},{6,0},{7,1},{8,10},{9,11},{10,... | collective-permute-start | bytes 393224 | tf_op jit(solution)/shard_map/ppermute | solution.py:275
  132.4 8.2 %collective-permute-start.7 = (f32[128,256]{1,0:T(8,128)S(1)}, f32[128,256]{1,0:T(8,128)S(1)}, u32[]{:S(2)}, u32[]{:S(2)}) collective-permute-start(f32[128,256]{1,0:T(8,128)S(1)} %get-tuple-element.23), channel_id=1, source_target_pairs={{0,6},{1,7},{2,0},{3,1},{4,2},{5,3},{6,4},{7,5},{8,14},{9,15},{10,... | collective-permute-start | bytes 393224 | tf_op jit(solution)/shard_map/ppermute | solution.py:275
  134.7 6.8 %collective-permute-start.6 = (f32[128,256]{1,0:T(8,128)S(1)}, f32[128,256]{1,0:T(8,128)S(1)}, u32[]{:S(2)}, u32[]{:S(2)}) collective-permute-start(f32[128,256]{1,0:T(8,128)S(1)} %get-tuple-element.24), channel_id=1, source_target_pairs={{0,4},{1,5},{2,6},{3,7},{4,0},{5,1},{6,2},{7,3},{8,12},{9,13},{10,... | collective-permute-start | bytes 393224 | tf_op jit(solution)/shard_map/ppermute | solution.py:275

commit v4 on v3

--- a/solution.py
+++ b/solution.py
@@ -1,4 +1,5 @@
 import functools
+import math
 
 import jax
 import jax.numpy as jnp
@@ -232,7 +233,14 @@
         out_ref[distance] = product(*split(strip), r_high[...], r_low[...])
 
 
-def root_other_kernel(gathered_ref, inverse_ref, other_ref, high_ref, low_ref):
+def root_other_kernel(side, inverse_ref, *refs):
+    pieces, (other_ref, high_ref, low_ref, gathered_ref) = refs[: 2 * side], refs[2 * side :]
+    me = lax.axis_index("row")
+    for i in range(side):
+        for j in range(side):
+            source = (me // side - i + side) % side * side + (me % side - j + side) % side
+            gathered_ref[source, :, 0] = pieces[i][j]
+            gathered_ref[source, :, 1] = pieces[side + j][i]
     join_slices(gathered_ref, high_ref, low_ref)
     root_rows(1, inverse_ref, high_ref, low_ref, other_ref)
 
@@ -241,20 +249,21 @@
     root_rows(0, inverse_ref, high_ref, low_ref, mine_ref)
 
 
-def root(gathered, root_inverse, chips):
+def root(pieces, root_inverse, rows, chips):
     height, depth = root_inverse.shape
     out = f32(chips, height // (CORES * chips), NRHS)
     half = jax.ShapeDtypeStruct((depth, NRHS), jnp.bfloat16)
     cost = pl.CostEstimate(flops=3 * height * depth * NRHS, transcendentals=0, bytes_accessed=2 * height * depth)
     other, high, low = pl.pallas_call(
-        root_other_kernel,
+        functools.partial(root_other_kernel, len(pieces) // 2),
         out_shape=(out, half, half),
-        in_specs=[VMEM] * 2,
+        in_specs=[VMEM] * (1 + len(pieces)),
         out_specs=(VMEM,) * 3,
+        scratch_shapes=[pltpu.VMEM((rows, depth // BLK, TILES, SUB, LANES), jnp.float32)],
         compiler_params=PARAMS,
         cost_estimate=cost,
         name="root_other",
-    )(gathered, root_inverse)
+    )(root_inverse, *pieces)
     mine = pl.pallas_call(
         root_mine_kernel,
         out_shape=out,
@@ -282,6 +291,21 @@
     return total
 
 
+def gather_rows(piece, rows, side):
+    def along_y(x):
+        return [x] + [
+            lax.ppermute(x, "row", [(i, i // side * side + (i + k) % side) for i in range(rows)])
+            for k in range(1, side)
+        ]
+
+    def along_z(x):
+        return [x] + [lax.ppermute(x, "row", [(i, (i + side * k) % rows) for i in range(rows)]) for k in range(1, side)]
+
+    first, second = lax.optimization_barrier((along_y(piece[:, 0]), along_z(piece[:, 1])))
+    first, second = lax.optimization_barrier((jnp.stack(first), jnp.stack(second)))
+    return along_z(first) + along_y(second)
+
+
 def shards(rhs, block_target, pivot_inverse, update_factor, root_inverse, update_map):
     rows = lax.axis_size("row")
     cols = lax.axis_size("col")
@@ -293,8 +317,8 @@
     solved, update = front(pivot, pivot_inverse, update_factor)
     returned = exchange(update, "row")
     piece = reduce_cols(*subtract(words, returned, direct, chips), cols)
-    gathered = exchange(jnp.broadcast_to(piece[None], (rows,) + piece.shape), "row")
-    root_solution = reduce_cols(*root(gathered, root_inverse, chips), cols)
+    pieces = gather_rows(piece, rows, math.isqrt(rows))
+    root_solution = reduce_cols(*root(pieces, root_inverse, rows, chips), cols)
     return (solved, root_solution)
 
 

time: 142 us -> 141 us (level)
  blocking collectives: 105 us -> 74.9 us
  waiting for transfers between devices: 14.3 us -> 30.4 us
  starting transfers between devices: 8.59 us -> 21.6 us
    all_to_all x4 -> x3, blocking collectives: 105 us -> 74.9 us  [exchange(): return lax.all_to_all(x, axis, split_axis=0, concat_axis=0, tiled=True)]
    ppermute x0 -> x12, waiting for transfers between devices: none -> 16.2 us  [the longest x6 9.51 us: along_z(): lax.ppermute(x, 'row', [(i, (i + side * k) % rows) for i in range(rows)])]
    ppermute x0 -> x12, starting transfers between devices: none -> 12.8 us  [the longest x6 7.72 us: along_z(): lax.ppermute(x, 'row', [(i, (i + side * k) % rows) for i in range(rows)])]
  transfers between devices with their start and end apart: 8 -> 20, of which waited for: 8 -> 17; matrix products, arithmetic and copies ran while one was open for 0% -> 0% of each run, Pallas kernels for 1% -> 1%
where the time goes in v4:
time: 141 us
  blocking collectives  74.9 us (53%)
  waiting for transfers between devices  30.4 us (22%)
  starting transfers between devices  21.6 us (15%)
  Pallas kernels  12.3 us (9%)
    all_to_all x3, blocking collectives, exchange(): return lax.all_to_all(x, axis, split_axis=0, concat_axis=0, tiled=True)  74.9 us
    ppermute x6, waiting for transfers between devices, reduce_cols(): lax.ppermute(mine[distance] + sibling[distance], 'col', [(c, (c + CORES *...  12.3 us
    ppermute x6, waiting for transfers between devices, along_z(): lax.ppermute(x, 'row', [(i, (i + side * k) % rows) for i in range(rows)])  9.51 us
    ppermute x6, starting transfers between devices, reduce_cols(): lax.ppermute(mine[distance] + sibling[distance], 'col', [(c, (c + CORES *...  8.43 us
    ppermute x6, starting transfers between devices, along_z(): lax.ppermute(x, 'row', [(i, (i + side * k) % rows) for i in range(rows)])  7.72 us
    ppermute x6, waiting for transfers between devices, along_y(): lax.ppermute(x, 'row', [(i, i // side * side + (i + k) % side) for i in r...  6.66 us
    ppermute x6, starting transfers between devices, along_y(): lax.ppermute(x, 'row', [(i, i // side * side + (i + k) % side) for i in r...  5.06 us
    pallas_call x1, Pallas kernels, front(): pl.pallas_call(front_kernel, out_shape=(f32(order, NRHS), f32(rows, half,...  2.89 us
  transfers between devices with their start and end apart: 20, of which 17 were waited for; matrix products, arithmetic and copies ran while one was open for 0% of the time, Pallas kernels for 1%

profile of v4, /device:TPU:0, one launch (start us, length us, event | category | flops | bytes accessed | tf_op | source)
XLA Modules:
  0.0 140.9 jit_solution(2168480984799311373)
XLA Ops:
  0.6 1.9 %pack.1 = f32[16,33,8,128]{3,2,1,0:T(8,128)S(1)} custom-call(s32[16]{0:T(128)} %target_ref.1, s32[8]{0:T(128)} %map_ref.1, f32[16,16,8,256]{3,2,1,0:T(8,128)} %bitcast.45), custom_call_target="tpu_custom_call" | custom-call | tf_op jit(solution)/shard_map/pack/pallas_call | solution.py:84
  2.5 37.3 %all_to_all.15.arrived_ref = f32[16,33,8,128]{3,2,1,0:T(8,128)S(1)} all-to-all(f32[16,33,8,128]{3,2,1,0:T(8,128)S(1)} %pack.1), channel_id=1, replica_groups=mesh['row'=16,'col'=8] {'row'}, dimensions={0} | all-to-all | bytes 4325376 | tf_op jit(solution)/shard_map/all_to_all | solution.py:48
  39.8 2.4 %route.1 = (f32[128,2,8,128]{3,2,1,0:T(8,128)S(1)}, f32[256,2,8,128]{3,2,1,0:T(8,128)S(1)}, s32[16,128]{1,0:T(8,128)S(1)}) custom-call(f32[16,33,8,128]{3,2,1,0:T(8,128)S(1)} %all_to_all.15.arrived_ref), custom_call_target="tpu_custom_call" | custom-call | tf_op jit(solution)/shard_map/route/pallas_call | solution.py:137
  42.2 19.4 %all_to_all.16.arrived_ref = f32[16,8,2,8,128]{4,3,2,1,0:T(8,128)S(1)} all-to-all(f32[16,8,2,8,128]{4,3,2,1,0:T(8,128)S(1)} %bitcast.44), channel_id=1, replica_groups=mesh['row'=16,'col'=8] {'row'}, dimensions={0} | all-to-all | bytes 2097152 | tf_op jit(solution)/shard_map/all_to_all | solution.py:48
  61.6 2.9 %front.1 = (f32[1024,256]{1,0:T(8,128)}, f32[16,8,2,8,128]{4,3,2,1,0:T(8,128)S(1)}) custom-call(f32[16,8,2,8,128]{4,3,2,1,0:T(8,128)S(1)} %all_to_all.16.arrived_ref, f32[1024,1024]{1,0:T(8,128)S(1)} %copy-done, f32[1024,1024]{1,0:T(8,128)S(1)} %copy-done.1), custom_call_target="tpu_custom_call" | custom-call | tf_op jit(solution)/shard_map/front/pallas_call | solution.py:188
  64.5 0.0 slice-start.1
  64.5 18.2 %all_to_all.17.arrived_ref = f32[16,8,2,8,128]{4,3,2,1,0:T(8,128)S(1)} all-to-all(f32[16,8,2,8,128]{4,3,2,1,0:T(8,128)S(1)} %get-tuple-element.25), channel_id=1, replica_groups=mesh['row'=16,'col'=8] {'row'}, dimensions={0} | all-to-all | bytes 2097152 | tf_op jit(solution)/shard_map/all_to_all | solution.py:48
  82.7 1.2 subtract.1
  83.9 0.1 collective-permute-start
  84.0 1.9 %collective-permute-done = f32[4,16,2,8,128]{4,3,1,2,0:T(8,128)S(1)} collective-permute-done((f32[4,16,2,8,128]{4,3,1,2,0:T(8,128)S(1)}, f32[4,16,2,8,128]{4,3,1,2,0:T(8,128)S(1)}, u32[]{:S(2)}, u32[]{:S(2)}) %collective-permute-start) | collective-permute-done | bytes 524320 | tf_op jit(solution)/shard_map/ppermute | solution.py:281
  86.0 1.6 %collective-permute-start.1 = (f32[16,2,8,128]{3,2,0,1:T(8,128)S(1)}, f32[16,2,8,128]{3,2,0,1:T(8,128)S(1)}, u32[]{:S(2)}, u32[]{:S(2)}) collective-permute-start(f32[16,2,8,128]{3,2,0,1:T(8,128)S(1)} %get-tuple-element.45), channel_id=1, source_target_pairs={{0,2},{1,3},{2,4},{3,5},{4,6},{5,7},{6,0},{7,1},{8,10},{9,11},{10,... | collective-permute-start | bytes 393224 | tf_op jit(solution)/shard_map/ppermute | solution.py:284
  87.5 1.7 %collective-permute-start.3 = (f32[16,2,8,128]{3,2,0,1:T(8,128)S(1)}, f32[16,2,8,128]{3,2,0,1:T(8,128)S(1)}, u32[]{:S(2)}, u32[]{:S(2)}) collective-permute-start(f32[16,2,8,128]{3,2,0,1:T(8,128)S(1)} %get-tuple-element.46), channel_id=1, source_target_pairs={{0,6},{1,7},{2,0},{3,1},{4,2},{5,3},{6,4},{7,5},{8,14},{9,15},{10,... | collective-permute-start | bytes 393224 | tf_op jit(solution)/shard_map/ppermute | solution.py:284
  89.3 1.8 %collective-permute-start.2 = (f32[16,2,8,128]{3,2,0,1:T(8,128)S(1)}, f32[16,2,8,128]{3,2,0,1:T(8,128)S(1)}, u32[]{:S(2)}, u32[]{:S(2)}) collective-permute-start(f32[16,2,8,128]{3,2,0,1:T(8,128)S(1)} %get-tuple-element.47), channel_id=1, source_target_pairs={{0,4},{1,5},{2,6},{3,7},{4,0},{5,1},{6,2},{7,3},{8,12},{9,13},{10,... | collective-permute-start | bytes 393224 | tf_op jit(solution)/shard_map/ppermute | solution.py:284
  91.1 1.7 %collective-permute-done.1 = f32[16,2,8,128]{3,2,0,1:T(8,128)S(1)} collective-permute-done((f32[16,2,8,128]{3,2,0,1:T(8,128)S(1)}, f32[16,2,8,128]{3,2,0,1:T(8,128)S(1)}, u32[]{:S(2)}, u32[]{:S(2)}) %collective-permute-start.1) | collective-permute-done | bytes 131104 | tf_op jit(solution)/shard_map/ppermute | solution.py:284
  92.8 2.1 %collective-permute-done.3 = f32[16,2,8,128]{3,2,0,1:T(8,128)S(1)} collective-permute-done((f32[16,2,8,128]{3,2,0,1:T(8,128)S(1)}, f32[16,2,8,128]{3,2,0,1:T(8,128)S(1)}, u32[]{:S(2)}, u32[]{:S(2)}) %collective-permute-start.3) | collective-permute-done | bytes 131104 | tf_op jit(solution)/shard_map/ppermute | solution.py:284
  94.9 1.7 %collective-permute-done.2 = f32[16,2,8,128]{3,2,0,1:T(8,128)S(1)} collective-permute-done((f32[16,2,8,128]{3,2,0,1:T(8,128)S(1)}, f32[16,2,8,128]{3,2,0,1:T(8,128)S(1)}, u32[]{:S(2)}, u32[]{:S(2)}) %collective-permute-start.2) | collective-permute-done | bytes 131104 | tf_op jit(solution)/shard_map/ppermute | solution.py:284
  96.7 0.9 collective-permute-start.9
  97.6 1.0 collective-permute-start.8
  98.5 0.4 collective-permute-start.7
  98.9 1.2 collective-permute-start.6
  100.1 1.4 %collective-permute-start.5 = (f32[16,8,128]{2,1,0:T(8,128)S(1)}, f32[16,8,128]{2,1,0:T(8,128)S(1)}, u32[]{:S(2)}, u32[]{:S(2)}) collective-permute-start(f32[16,8,128]{2,1,0:T(8,128)S(1)} %get-tuple-element.29), channel_id=1, source_target_pairs={{0,16},{8,24},{16,0},{24,8},{32,48},{40,56},{48,32},{56,40},{64,80... | collective-permute-start | bytes 196616 | tf_op jit(solution)/shard_map/ppermute | solution.py:297
  101.6 0.2 collective-permute-start.4
  101.8 1.8 %collective-permute-done.8 = f32[16,8,128]{2,1,0:T(8,128)S(1)} collective-permute-done((f32[16,8,128]{2,1,0:T(8,128)S(1)}, f32[16,8,128]{2,1,0:T(8,128)S(1)}, u32[]{:S(2)}, u32[]{:S(2)}) %collective-permute-start.8) | collective-permute-done | bytes 65568 | tf_op jit(solution)/shard_map/ppermute | solution.py:302
  103.6 0.7 collective-permute-done.7
  104.3 1.6 %collective-permute-done.5 = f32[16,8,128]{2,1,0:T(8,128)S(1)} collective-permute-done((f32[16,8,128]{2,1,0:T(8,128)S(1)}, f32[16,8,128]{2,1,0:T(8,128)S(1)}, u32[]{:S(2)}, u32[]{:S(2)}) %collective-permute-start.5) | collective-permute-done | bytes 65568 | tf_op jit(solution)/shard_map/ppermute | solution.py:297
  105.9 1.2 collective-permute-done.4
  107.1 2.6 %collective-permute-start.12 = (f32[4,16,8,128]{3,2,1,0:T(8,128)S(1)}, f32[4,16,8,128]{3,2,1,0:T(8,128)S(1)}, u32[]{:S(2)}, u32[]{:S(2)}) collective-permute-start(f32[4,16,8,128]{3,2,1,0:T(8,128)S(1)} %get-tuple-element.37.refs_0_), channel_id=1, source_target_pairs={{0,96},{8,104},{16,112},{24,120},{32,0},{40,8},{48,16},{56,24},{64... | collective-permute-start | bytes 786440 | tf_op jit(solution)/shard_map/ppermute | solution.py:302
  109.7 1.6 %collective-permute-start.11 = (f32[4,16,8,128]{3,2,1,0:T(8,128)S(1)}, f32[4,16,8,128]{3,2,1,0:T(8,128)S(1)}, u32[]{:S(2)}, u32[]{:S(2)}) collective-permute-start(f32[4,16,8,128]{3,2,1,0:T(8,128)S(1)} %get-tuple-element.37.refs_0_), channel_id=1, source_target_pairs={{0,64},{8,72},{16,80},{24,88},{32,96},{40,104},{48,112},{56,120},{... | collective-permute-start | bytes 786440 | tf_op jit(solution)/shard_map/ppermute | solution.py:302
  111.3 1.2 collective-permute-start.10
  112.5 0.9 collective-permute-start.15
  113.4 0.9 collective-permute-start.14
  114.3 3.8 %collective-permute-done.12.refs_3_ = f32[4,16,8,128]{3,2,1,0:T(8,128)S(1)} collective-permute-done((f32[4,16,8,128]{3,2,1,0:T(8,128)S(1)}, f32[4,16,8,128]{3,2,1,0:T(8,128)S(1)}, u32[]{:S(2)}, u32[]{:S(2)}) %collective-permute-start.12) | collective-permute-done | bytes 262176 | tf_op jit(solution)/shard_map/ppermute | solution.py:302
  118.1 0.5 collective-permute-start.13
  118.5 0.5 collective-permute-done.11.refs_2_
  119.1 2.7 %collective-permute-done.10.refs_1_ = f32[4,16,8,128]{3,2,1,0:T(8,128)S(1)} collective-permute-done((f32[4,16,8,128]{3,2,1,0:T(8,128)S(1)}, f32[4,16,8,128]{3,2,1,0:T(8,128)S(1)}, u32[]{:S(2)}, u32[]{:S(2)}) %collective-permute-start.10) | collective-permute-done | bytes 262176 | tf_op jit(solution)/shard_map/ppermute | solution.py:302
  121.8 0.1 collective-permute-done.14.refs_6_
  121.8 3.8 %collective-permute-done.13.refs_5_ = f32[4,16,8,128]{3,2,1,0:T(8,128)S(1)} collective-permute-done((f32[4,16,8,128]{3,2,1,0:T(8,128)S(1)}, f32[4,16,8,128]{3,2,1,0:T(8,128)S(1)}, u32[]{:S(2)}, u32[]{:S(2)}) %collective-permute-start.13) | collective-permute-done | bytes 262176 | tf_op jit(solution)/shard_map/ppermute | solution.py:297
  125.7 2.2 %root_other.1 = (f32[4,128,256]{2,1,0:T(8,128)S(1)}, bf16[2048,256]{1,0:T(8,128)(2,1)S(1)}, bf16[2048,256]{1,0:T(8,128)(2,1)S(1)}) custom-call(f32[1024,2048]{1,0:T(8,128)S(1)} %bitcast.43, f32[4,16,8,128]{3,2,1,0:T(8,128)S(1)} %get-tuple-element.37.refs_0_, f32[4,16,8,128]{3,2,1,0:T(8,128)S(1)} %collective-permute-done.10.refs_1_, ...), custom_call_target="tpu_custom_call" | custom-call | flops 1610612736 | bytes 4194304 | tf_op jit(solution)/shard_map/root_other/pallas_call | solution.py:257
  127.9 0.3 collective-permute-start.16
  128.1 1.8 %root_mine.1 = f32[4,128,256]{2,1,0:T(8,128)S(1)} custom-call(bf16[2048,256]{1,0:T(8,128)(2,1)S(1)} %get-tuple-element.39.high_ref, bf16[2048,256]{1,0:T(8,128)(2,1)S(1)} %get-tuple-element.40.low_ref, f32[1024,2048]{1,0:T(8,128)S(1)} %bitcast.43), custom_call_target="tpu_custom_call" | custom-call | flops 1610612736 | bytes 4194304 | tf_op jit(solution)/shard_map/root_mine/pallas_call | solution.py:267
  129.9 0.1 collective-permute-done.16
  130.0 0.1 fusion.2
  130.1 0.9 collective-permute-start.17
  131.0 2.4 %collective-permute-start.19 = (f32[128,256]{1,0:T(8,128)S(1)}, f32[128,256]{1,0:T(8,128)S(1)}, u32[]{:S(2)}, u32[]{:S(2)}) collective-permute-start(f32[128,256]{1,0:T(8,128)S(1)} %get-tuple-element.43), channel_id=1, source_target_pairs={{0,6},{1,7},{2,0},{3,1},{4,2},{5,3},{6,4},{7,5},{8,14},{9,15},{10,... | collective-permute-start | bytes 393224 | tf_op jit(solution)/shard_map/ppermute | solution.py:284
  133.4 3.8 %collective-permute-done.17 = f32[128,256]{1,0:T(8,128)S(1)} collective-permute-done((f32[128,256]{1,0:T(8,128)S(1)}, f32[128,256]{1,0:T(8,128)S(1)}, u32[]{:S(2)}, u32[]{:S(2)}) %collective-permute-start.17) | collective-permute-done | bytes 131104 | tf_op jit(solution)/shard_map/ppermute | solution.py:284
  137.2 2.1 %collective-permute-done.19 = f32[128,256]{1,0:T(8,128)S(1)} collective-permute-done((f32[128,256]{1,0:T(8,128)S(1)}, f32[128,256]{1,0:T(8,128)S(1)}, u32[]{:S(2)}, u32[]{:S(2)}) %collective-permute-start.19) | collective-permute-done | bytes 131104 | tf_op jit(solution)/shard_map/ppermute | solution.py:284
  139.3 0.9 collective-permute-done.18
  140.2 0.7 fusion.6
  (17 shorter events, 0.2 us)
Async XLA Ops:
  2.5 59.1 %copy-start.1 = (f32[1024,1024]{1,0:T(8,128)S(1)}, f32[1024,1024]{1,0:T(8,128)}, u32[]{:S(2)}) copy-start(f32[1024,1024]{1,0:T(8,128)} %factor_ref.1) | copy-start | bytes 12582916
  39.8 21.8 %copy-start = (f32[1024,1024]{1,0:T(8,128)S(1)}, f32[1024,1024]{1,0:T(8,128)}, u32[]{:S(2)}) copy-start(f32[1024,1024]{1,0:T(8,128)} %pivot_ref.1) | copy-start | bytes 12582916
  61.6 64.1 %slice-start = ((s8[8388608]{0:T(1024)(128)(4,1)}), s8[4194304]{0:T(1024)(128)(4,1)S(1)}, s32[]{:S(2)}) async-start(s8[8388608]{0:T(1024)(128)(4,1)} %bitcast.42), calls=%async_computation.3 | async-start | bytes 8388608
  64.5 61.2 %slice-start.1 = ((s8[8388608]{0:T(1024)(128)(4,1)}), s8[4194304]{0:T(1024)(128)(4,1)S(1)}, s32[]{:S(2)}) async-start(s8[8388608]{0:T(1024)(128)(4,1)} %bitcast.42), calls=%async_computation.4 | async-start | bytes 8388608
  83.9 2.0 %collective-permute-start = (f32[4,16,2,8,128]{4,3,1,2,0:T(8,128)S(1)}, f32[4,16,2,8,128]{4,3,1,2,0:T(8,128)S(1)}, u32[]{:S(2)}, u32[]{:S(2)}) collective-permute-start(f32[4,16,2,8,128]{4,3,1,2,0:T(8,128)S(1)} %copy.9), channel_id=1, source_target_pairs={{0,1},{1,0},{2,3},{3,2},{4,5},{5,4},{6,7},{7,6},{8,9},{9,8},{10,11... | collective-permute-start | bytes 1572872 | tf_op jit(solution)/shard_map/ppermute | solution.py:281
  86.0 6.8 %collective-permute-start.1 = (f32[16,2,8,128]{3,2,0,1:T(8,128)S(1)}, f32[16,2,8,128]{3,2,0,1:T(8,128)S(1)}, u32[]{:S(2)}, u32[]{:S(2)}) collective-permute-start(f32[16,2,8,128]{3,2,0,1:T(8,128)S(1)} %get-tuple-element.45), channel_id=1, source_target_pairs={{0,2},{1,3},{2,4},{3,5},{4,6},{5,7},{6,0},{7,1},{8,10},{9,11},{10,... | collective-permute-start | bytes 393224 | tf_op jit(solution)/shard_map/ppermute | solution.py:284
  87.5 7.4 %collective-permute-start.3 = (f32[16,2,8,128]{3,2,0,1:T(8,128)S(1)}, f32[16,2,8,128]{3,2,0,1:T(8,128)S(1)}, u32[]{:S(2)}, u32[]{:S(2)}) collective-permute-start(f32[16,2,8,128]{3,2,0,1:T(8,128)S(1)} %get-tuple-element.46), channel_id=1, source_target_pairs={{0,6},{1,7},{2,0},{3,1},{4,2},{5,3},{6,4},{7,5},{8,14},{9,15},{10,... | collective-permute-start | bytes 393224 | tf_op jit(solution)/shard_map/ppermute | solution.py:284
  89.3 7.3 %collective-permute-start.2 = (f32[16,2,8,128]{3,2,0,1:T(8,128)S(1)}, f32[16,2,8,128]{3,2,0,1:T(8,128)S(1)}, u32[]{:S(2)}, u32[]{:S(2)}) collective-permute-start(f32[16,2,8,128]{3,2,0,1:T(8,128)S(1)} %get-tuple-element.47), channel_id=1, source_target_pairs={{0,4},{1,5},{2,6},{3,7},{4,0},{5,1},{6,2},{7,3},{8,12},{9,13},{10,... | collective-permute-start | bytes 393224 | tf_op jit(solution)/shard_map/ppermute | solution.py:284
  96.7 4.9 %collective-permute-start.9 = (f32[16,8,128]{2,1,0:T(8,128)S(1)}, f32[16,8,128]{2,1,0:T(8,128)S(1)}, u32[]{:S(2)}, u32[]{:S(2)}) collective-permute-start(f32[16,8,128]{2,1,0:T(8,128)S(1)} %get-tuple-element.33), channel_id=1, source_target_pairs={{0,96},{8,104},{16,112},{24,120},{32,0},{40,8},{48,16},{56,24},{64... | collective-permute-start | bytes 196616 | tf_op jit(solution)/shard_map/ppermute | solution.py:302
  97.6 6.1 %collective-permute-start.8 = (f32[16,8,128]{2,1,0:T(8,128)S(1)}, f32[16,8,128]{2,1,0:T(8,128)S(1)}, u32[]{:S(2)}, u32[]{:S(2)}) collective-permute-start(f32[16,8,128]{2,1,0:T(8,128)S(1)} %get-tuple-element.33), channel_id=1, source_target_pairs={{0,64},{8,72},{16,80},{24,88},{32,96},{40,104},{48,112},{56,120},{... | collective-permute-start | bytes 196616 | tf_op jit(solution)/shard_map/ppermute | solution.py:302
  98.5 5.8 %collective-permute-start.7 = (f32[16,8,128]{2,1,0:T(8,128)S(1)}, f32[16,8,128]{2,1,0:T(8,128)S(1)}, u32[]{:S(2)}, u32[]{:S(2)}) collective-permute-start(f32[16,8,128]{2,1,0:T(8,128)S(1)} %get-tuple-element.33), channel_id=1, source_target_pairs={{0,32},{8,40},{16,48},{24,56},{32,64},{40,72},{48,80},{56,88},{64,... | collective-permute-start | bytes 196616 | tf_op jit(solution)/shard_map/ppermute | solution.py:302
  98.9 5.4 %collective-permute-start.6 = (f32[16,8,128]{2,1,0:T(8,128)S(1)}, f32[16,8,128]{2,1,0:T(8,128)S(1)}, u32[]{:S(2)}, u32[]{:S(2)}) collective-permute-start(f32[16,8,128]{2,1,0:T(8,128)S(1)} %get-tuple-element.29), channel_id=1, source_target_pairs={{0,24},{8,0},{16,8},{24,16},{32,56},{40,32},{48,40},{56,48},{64,88... | collective-permute-start | bytes 196616 | tf_op jit(solution)/shard_map/ppermute | solution.py:297
  100.1 5.8 %collective-permute-start.5 = (f32[16,8,128]{2,1,0:T(8,128)S(1)}, f32[16,8,128]{2,1,0:T(8,128)S(1)}, u32[]{:S(2)}, u32[]{:S(2)}) collective-permute-start(f32[16,8,128]{2,1,0:T(8,128)S(1)} %get-tuple-element.29), channel_id=1, source_target_pairs={{0,16},{8,24},{16,0},{24,8},{32,48},{40,56},{48,32},{56,40},{64,80... | collective-permute-start | bytes 196616 | tf_op jit(solution)/shard_map/ppermute | solution.py:297
  101.6 5.5 %collective-permute-start.4 = (f32[16,8,128]{2,1,0:T(8,128)S(1)}, f32[16,8,128]{2,1,0:T(8,128)S(1)}, u32[]{:S(2)}, u32[]{:S(2)}) collective-permute-start(f32[16,8,128]{2,1,0:T(8,128)S(1)} %get-tuple-element.29), channel_id=1, source_target_pairs={{0,8},{8,16},{16,24},{24,0},{32,40},{40,48},{48,56},{56,32},{64,72... | collective-permute-start | bytes 196616 | tf_op jit(solution)/shard_map/ppermute | solution.py:297
  107.1 11.0 %collective-permute-start.12 = (f32[4,16,8,128]{3,2,1,0:T(8,128)S(1)}, f32[4,16,8,128]{3,2,1,0:T(8,128)S(1)}, u32[]{:S(2)}, u32[]{:S(2)}) collective-permute-start(f32[4,16,8,128]{3,2,1,0:T(8,128)S(1)} %get-tuple-element.37.refs_0_), channel_id=1, source_target_pairs={{0,96},{8,104},{16,112},{24,120},{32,0},{40,8},{48,16},{56,24},{64... | collective-permute-start | bytes 786440 | tf_op jit(solution)/shard_map/ppermute | solution.py:302
  109.7 9.3 %collective-permute-start.11 = (f32[4,16,8,128]{3,2,1,0:T(8,128)S(1)}, f32[4,16,8,128]{3,2,1,0:T(8,128)S(1)}, u32[]{:S(2)}, u32[]{:S(2)}) collective-permute-start(f32[4,16,8,128]{3,2,1,0:T(8,128)S(1)} %get-tuple-element.37.refs_0_), channel_id=1, source_target_pairs={{0,64},{8,72},{16,80},{24,88},{32,96},{40,104},{48,112},{56,120},{... | collective-permute-start | bytes 786440 | tf_op jit(solution)/shard_map/ppermute | solution.py:302
  111.3 10.4 %collective-permute-start.10 = (f32[4,16,8,128]{3,2,1,0:T(8,128)S(1)}, f32[4,16,8,128]{3,2,1,0:T(8,128)S(1)}, u32[]{:S(2)}, u32[]{:S(2)}) collective-permute-start(f32[4,16,8,128]{3,2,1,0:T(8,128)S(1)} %get-tuple-element.37.refs_0_), channel_id=1, source_target_pairs={{0,32},{8,40},{16,48},{24,56},{32,64},{40,72},{48,80},{56,88},{64,... | collective-permute-start | bytes 786440 | tf_op jit(solution)/shard_map/ppermute | solution.py:302
  112.5 9.2 %collective-permute-start.15 = (f32[4,16,8,128]{3,2,1,0:T(8,128)S(1)}, f32[4,16,8,128]{3,2,1,0:T(8,128)S(1)}, u32[]{:S(2)}, u32[]{:S(2)}) collective-permute-start(f32[4,16,8,128]{3,2,1,0:T(8,128)S(1)} %get-tuple-element.38.refs_4_), channel_id=1, source_target_pairs={{0,24},{8,0},{16,8},{24,16},{32,56},{40,32},{48,40},{56,48},{64,88... | collective-permute-start | bytes 786440 | tf_op jit(solution)/shard_map/ppermute | solution.py:297
  113.4 8.4 %collective-permute-start.14 = (f32[4,16,8,128]{3,2,1,0:T(8,128)S(1)}, f32[4,16,8,128]{3,2,1,0:T(8,128)S(1)}, u32[]{:S(2)}, u32[]{:S(2)}) collective-permute-start(f32[4,16,8,128]{3,2,1,0:T(8,128)S(1)} %get-tuple-element.38.refs_4_), channel_id=1, source_target_pairs={{0,16},{8,24},{16,0},{24,8},{32,48},{40,56},{48,32},{56,40},{64,80... | collective-permute-start | bytes 786440 | tf_op jit(solution)/shard_map/ppermute | solution.py:297
  118.1 7.6 %collective-permute-start.13 = (f32[4,16,8,128]{3,2,1,0:T(8,128)S(1)}, f32[4,16,8,128]{3,2,1,0:T(8,128)S(1)}, u32[]{:S(2)}, u32[]{:S(2)}) collective-permute-start(f32[4,16,8,128]{3,2,1,0:T(8,128)S(1)} %get-tuple-element.38.refs_4_), channel_id=1, source_target_pairs={{0,8},{8,16},{16,24},{24,0},{32,40},{40,48},{48,56},{56,32},{64,72... | collective-permute-start | bytes 786440 | tf_op jit(solution)/shard_map/ppermute | solution.py:297
  127.9 2.2 %collective-permute-start.16 = (f32[4,128,256]{2,1,0:T(8,128)S(1)}, f32[4,128,256]{2,1,0:T(8,128)S(1)}, u32[]{:S(2)}, u32[]{:S(2)}) collective-permute-start(f32[4,128,256]{2,1,0:T(8,128)S(1)} %get-tuple-element.41), channel_id=1, source_target_pairs={{0,1},{1,0},{2,3},{3,2},{4,5},{5,4},{6,7},{7,6},{8,9},{9,8},{10,11... | collective-permute-start | bytes 1572872 | tf_op jit(solution)/shard_map/ppermute | solution.py:281
  130.1 7.1 %collective-permute-start.17 = (f32[128,256]{1,0:T(8,128)S(1)}, f32[128,256]{1,0:T(8,128)S(1)}, u32[]{:S(2)}, u32[]{:S(2)}) collective-permute-start(f32[128,256]{1,0:T(8,128)S(1)} %get-tuple-element.42), channel_id=1, source_target_pairs={{0,2},{1,3},{2,4},{3,5},{4,6},{5,7},{6,0},{7,1},{8,10},{9,11},{10,... | collective-permute-start | bytes 393224 | tf_op jit(solution)/shard_map/ppermute | solution.py:284
  131.0 8.3 %collective-permute-start.19 = (f32[128,256]{1,0:T(8,128)S(1)}, f32[128,256]{1,0:T(8,128)S(1)}, u32[]{:S(2)}, u32[]{:S(2)}) collective-permute-start(f32[128,256]{1,0:T(8,128)S(1)} %get-tuple-element.43), channel_id=1, source_target_pairs={{0,6},{1,7},{2,0},{3,1},{4,2},{5,3},{6,4},{7,5},{8,14},{9,15},{10,... | collective-permute-start | bytes 393224 | tf_op jit(solution)/shard_map/ppermute | solution.py:284
  133.4 6.8 %collective-permute-start.18 = (f32[128,256]{1,0:T(8,128)S(1)}, f32[128,256]{1,0:T(8,128)S(1)}, u32[]{:S(2)}, u32[]{:S(2)}) collective-permute-start(f32[128,256]{1,0:T(8,128)S(1)} %get-tuple-element.44), channel_id=1, source_target_pairs={{0,4},{1,5},{2,6},{3,7},{4,0},{5,1},{6,2},{7,3},{8,12},{9,13},{10,... | collective-permute-start | bytes 393224 | tf_op jit(solution)/shard_map/ppermute | solution.py:284

commit v5 on v4

--- a/solution.py
+++ b/solution.py
@@ -206,13 +206,15 @@
         return carry
 
     lax.fori_loop(0, rows, add, 0)
-    mine_ref[...] = acc[pl.ds(0, BLK // CORES)].reshape(mine_ref.shape)
-    other_ref[...] = acc[pl.ds(BLK // CORES, BLK // CORES)].reshape(mine_ref.shape)
+    part = mine_ref.shape[:1] + mine_ref.shape[2:]
+    for lane in range(TILES):
+        mine_ref[:, lane] = acc[pl.ds(0, BLK // CORES), lane].reshape(part)
+        other_ref[:, lane] = acc[pl.ds(BLK // CORES, BLK // CORES), lane].reshape(part)
 
 
 def subtract(words, arrived, start, chips):
     rows, half = arrived.shape[:2]
-    out = f32(chips, BLK // (CORES * chips), TILES, SUB, LANES)
+    out = f32(chips, TILES, BLK // (CORES * chips), SUB, LANES)
     return pl.pallas_call(
         functools.partial(subtract_kernel, rows, half),
         out_shape=(out, out),
@@ -236,9 +238,9 @@
 def root_other_kernel(side, inverse_ref, *refs):
     pieces, (other_ref, high_ref, low_ref, gathered_ref) = refs[: 2 * side], refs[2 * side :]
     me = lax.axis_index("row")
-    for i in range(side):
-        for j in range(side):
-            source = (me // side - i + side) % side * side + (me % side - j + side) % side
+    for i, z in enumerate(shifts(side)):
+        for j, y in enumerate(shifts(side)):
+            source = (me // side - z + side) % side * side + (me % side - y + side) % side
             gathered_ref[source, :, 0] = pieces[i][j]
             gathered_ref[source, :, 1] = pieces[side + j][i]
     join_slices(gathered_ref, high_ref, low_ref)
@@ -291,17 +293,20 @@
     return total
 
 
+def shifts(side):
+    return sorted(range(side), key=lambda k: (k > 0, k != side // 2, k))
+
+
 def gather_rows(piece, rows, side):
     def along_y(x):
-        return [x] + [
-            lax.ppermute(x, "row", [(i, i // side * side + (i + k) % side) for i in range(rows)])
-            for k in range(1, side)
-        ]
+        pairs = lambda k: [(i, i // side * side + (i + k) % side) for i in range(rows)]
+        return [x] + [lax.ppermute(x, "row", pairs(k)) for k in shifts(side)[1:]]
 
     def along_z(x):
-        return [x] + [lax.ppermute(x, "row", [(i, (i + side * k) % rows) for i in range(rows)]) for k in range(1, side)]
-
-    first, second = lax.optimization_barrier((along_y(piece[:, 0]), along_z(piece[:, 1])))
+        pairs = lambda k: [(i, (i + side * k) % rows) for i in range(rows)]
+        return [x] + [lax.ppermute(x, "row", pairs(k)) for k in shifts(side)[1:]]
+
+    first, second = lax.optimization_barrier((along_y(piece[0]), along_z(piece[1])))
     first, second = lax.optimization_barrier((jnp.stack(first), jnp.stack(second)))
     return along_z(first) + along_y(second)
 

time: 141 us -> 142 us (level)
  waiting for transfers between devices: 30.4 us -> 28.7 us
    ppermute x12, waiting for transfers between devices: 16.2 us -> 14.4 us  [the longest x6 7.85 us: along_z(): return [x] + [lax.ppermute(x, 'row', pairs(k)) for k in shifts(side)[1:]]]
  transfers between devices with their start and end apart: 20 -> 20, of which waited for: 17 -> 15; matrix products, arithmetic and copies ran while one was open for 0% -> 0% of each run, Pallas kernels for 1% -> 1%
where the time goes in v5:
time: 142 us; the launch traced here: 140 us
  blocking collectives  74.9 us (53%)
  waiting for transfers between devices  28.7 us (20%)
  starting transfers between devices  22.9 us (16%)
  Pallas kernels  12.3 us (9%)
    all_to_all x3, blocking collectives, exchange(): return lax.all_to_all(x, axis, split_axis=0, concat_axis=0, tiled=True)  74.9 us
    ppermute x6, waiting for transfers between devices, reduce_cols(): lax.ppermute(mine[distance] + sibling[distance], 'col', [(c, (c + CORES *...  12.3 us
    ppermute x6, starting transfers between devices, reduce_cols(): lax.ppermute(mine[distance] + sibling[distance], 'col', [(c, (c + CORES *...  8.42 us
    ppermute x6, waiting for transfers between devices, along_z(): return [x] + [lax.ppermute(x, 'row', pairs(k)) for k in shifts(side)[1:]]  7.85 us
    ppermute x6, starting transfers between devices, along_z(): return [x] + [lax.ppermute(x, 'row', pairs(k)) for k in shifts(side)[1:]]  7.72 us
    ppermute x6, waiting for transfers between devices, along_y(): return [x] + [lax.ppermute(x, 'row', pairs(k)) for k in shifts(side)[1:]]  6.59 us
    ppermute x6, starting transfers between devices, along_y(): return [x] + [lax.ppermute(x, 'row', pairs(k)) for k in shifts(side)[1:]]  6.44 us
    pallas_call x1, Pallas kernels, front(): pl.pallas_call(front_kernel, out_shape=(f32(order, NRHS), f32(rows, half,...  2.89 us
  transfers between devices with their start and end apart: 20, of which 15 were waited for; matrix products, arithmetic and copies ran while one was open for 0% of the time, Pallas kernels for 1%

profile of v5, /device:TPU:0, one launch (start us, length us, event | category | flops | bytes accessed | tf_op | source)
XLA Modules:
  0.0 140.5 jit_solution(14851162410347465128)
XLA Ops:
  0.6 1.9 %pack.1 = f32[16,33,8,128]{3,2,1,0:T(8,128)S(1)} custom-call(s32[16]{0:T(128)} %target_ref.1, s32[8]{0:T(128)} %map_ref.1, f32[16,16,8,256]{3,2,1,0:T(8,128)} %bitcast.45), custom_call_target="tpu_custom_call" | custom-call | tf_op jit(solution)/shard_map/pack/pallas_call | solution.py:84
  2.5 0.0 copy-start.1
  2.5 37.3 %all_to_all.15.arrived_ref = f32[16,33,8,128]{3,2,1,0:T(8,128)S(1)} all-to-all(f32[16,33,8,128]{3,2,1,0:T(8,128)S(1)} %pack.1), channel_id=1, replica_groups=mesh['row'=16,'col'=8] {'row'}, dimensions={0} | all-to-all | bytes 4325376 | tf_op jit(solution)/shard_map/all_to_all | solution.py:48
  39.8 2.4 %route.1 = (f32[128,2,8,128]{3,2,1,0:T(8,128)S(1)}, f32[256,2,8,128]{3,2,1,0:T(8,128)S(1)}, s32[16,128]{1,0:T(8,128)S(1)}) custom-call(f32[16,33,8,128]{3,2,1,0:T(8,128)S(1)} %all_to_all.15.arrived_ref), custom_call_target="tpu_custom_call" | custom-call | tf_op jit(solution)/shard_map/route/pallas_call | solution.py:137
  42.2 0.0 slice-start
  42.2 19.7 %all_to_all.16.arrived_ref = f32[16,8,2,8,128]{4,3,2,1,0:T(8,128)S(1)} all-to-all(f32[16,8,2,8,128]{4,3,2,1,0:T(8,128)S(1)} %bitcast.44), channel_id=1, replica_groups=mesh['row'=16,'col'=8] {'row'}, dimensions={0} | all-to-all | bytes 2097152 | tf_op jit(solution)/shard_map/all_to_all | solution.py:48
  61.9 2.9 %front.1 = (f32[1024,256]{1,0:T(8,128)}, f32[16,8,2,8,128]{4,3,2,1,0:T(8,128)S(1)}) custom-call(f32[16,8,2,8,128]{4,3,2,1,0:T(8,128)S(1)} %all_to_all.16.arrived_ref, f32[1024,1024]{1,0:T(8,128)S(1)} %copy-done, f32[1024,1024]{1,0:T(8,128)S(1)} %copy-done.1), custom_call_target="tpu_custom_call" | custom-call | tf_op jit(solution)/shard_map/front/pallas_call | solution.py:188
  64.8 17.9 %all_to_all.17.arrived_ref = f32[16,8,2,8,128]{4,3,2,1,0:T(8,128)S(1)} all-to-all(f32[16,8,2,8,128]{4,3,2,1,0:T(8,128)S(1)} %get-tuple-element.25), channel_id=1, replica_groups=mesh['row'=16,'col'=8] {'row'}, dimensions={0} | all-to-all | bytes 2097152 | tf_op jit(solution)/shard_map/all_to_all | solution.py:48
  82.7 1.2 subtract.1
  83.9 0.1 collective-permute-start
  84.0 1.9 %collective-permute-done = f32[4,2,16,8,128]{4,3,2,1,0:T(8,128)S(1)} collective-permute-done((f32[4,2,16,8,128]{4,3,2,1,0:T(8,128)S(1)}, f32[4,2,16,8,128]{4,3,2,1,0:T(8,128)S(1)}, u32[]{:S(2)}, u32[]{:S(2)}) %collective-permute-start) | collective-permute-done | bytes 524320 | tf_op jit(solution)/shard_map/ppermute | solution.py:283
  85.9 0.1 fusion.9
  86.0 1.6 %collective-permute-start.1 = (f32[2,16,8,128]{3,2,1,0:T(8,128)S(1)}, f32[2,16,8,128]{3,2,1,0:T(8,128)S(1)}, u32[]{:S(2)}, u32[]{:S(2)}) collective-permute-start(f32[2,16,8,128]{3,2,1,0:T(8,128)S(1)} %get-tuple-element.45), channel_id=1, source_target_pairs={{0,2},{1,3},{2,4},{3,5},{4,6},{5,7},{6,0},{7,1},{8,10},{9,11},{10,... | collective-permute-start | bytes 393224 | tf_op jit(solution)/shard_map/ppermute | solution.py:286
  87.5 1.7 %collective-permute-start.3 = (f32[2,16,8,128]{3,2,1,0:T(8,128)S(1)}, f32[2,16,8,128]{3,2,1,0:T(8,128)S(1)}, u32[]{:S(2)}, u32[]{:S(2)}) collective-permute-start(f32[2,16,8,128]{3,2,1,0:T(8,128)S(1)} %get-tuple-element.46), channel_id=1, source_target_pairs={{0,6},{1,7},{2,0},{3,1},{4,2},{5,3},{6,4},{7,5},{8,14},{9,15},{10,... | collective-permute-start | bytes 393224 | tf_op jit(solution)/shard_map/ppermute | solution.py:286
  89.3 1.8 %collective-permute-start.2 = (f32[2,16,8,128]{3,2,1,0:T(8,128)S(1)}, f32[2,16,8,128]{3,2,1,0:T(8,128)S(1)}, u32[]{:S(2)}, u32[]{:S(2)}) collective-permute-start(f32[2,16,8,128]{3,2,1,0:T(8,128)S(1)} %get-tuple-element.47), channel_id=1, source_target_pairs={{0,4},{1,5},{2,6},{3,7},{4,0},{5,1},{6,2},{7,3},{8,12},{9,13},{10,... | collective-permute-start | bytes 393224 | tf_op jit(solution)/shard_map/ppermute | solution.py:286
  91.1 1.7 %collective-permute-done.1 = f32[2,16,8,128]{3,2,1,0:T(8,128)S(1)} collective-permute-done((f32[2,16,8,128]{3,2,1,0:T(8,128)S(1)}, f32[2,16,8,128]{3,2,1,0:T(8,128)S(1)}, u32[]{:S(2)}, u32[]{:S(2)}) %collective-permute-start.1) | collective-permute-done | bytes 131104 | tf_op jit(solution)/shard_map/ppermute | solution.py:286
  92.8 2.1 %collective-permute-done.3 = f32[2,16,8,128]{3,2,1,0:T(8,128)S(1)} collective-permute-done((f32[2,16,8,128]{3,2,1,0:T(8,128)S(1)}, f32[2,16,8,128]{3,2,1,0:T(8,128)S(1)}, u32[]{:S(2)}, u32[]{:S(2)}) %collective-permute-start.3) | collective-permute-done | bytes 131104 | tf_op jit(solution)/shard_map/ppermute | solution.py:286
  94.9 1.7 %collective-permute-done.2 = f32[2,16,8,128]{3,2,1,0:T(8,128)S(1)} collective-permute-done((f32[2,16,8,128]{3,2,1,0:T(8,128)S(1)}, f32[2,16,8,128]{3,2,1,0:T(8,128)S(1)}, u32[]{:S(2)}, u32[]{:S(2)}) %collective-permute-start.2) | collective-permute-done | bytes 131104 | tf_op jit(solution)/shard_map/ppermute | solution.py:286
  96.6 0.9 collective-permute-start.9
  97.5 1.2 collective-permute-start.8
  98.7 0.8 collective-permute-start.7
  99.5 1.2 collective-permute-start.6
  100.7 0.8 collective-permute-start.5
  101.6 1.4 %collective-permute-start.4 = (f32[16,8,128]{2,1,0:T(8,128)S(1)}, f32[16,8,128]{2,1,0:T(8,128)S(1)}, u32[]{:S(2)}, u32[]{:S(2)}) collective-permute-start(f32[16,8,128]{2,1,0:T(8,128)S(1)} %get-tuple-element.29), channel_id=1, source_target_pairs={{0,16},{8,24},{16,0},{24,8},{32,48},{40,56},{48,32},{56,40},{64,80... | collective-permute-start | bytes 196616 | tf_op jit(solution)/shard_map/ppermute | solution.py:303
  103.0 0.2 collective-permute-done.8
  103.2 1.3 collective-permute-done.7
  104.5 1.7 %collective-permute-done.5 = f32[16,8,128]{2,1,0:T(8,128)S(1)} collective-permute-done((f32[16,8,128]{2,1,0:T(8,128)S(1)}, f32[16,8,128]{2,1,0:T(8,128)S(1)}, u32[]{:S(2)}, u32[]{:S(2)}) %collective-permute-start.5) | collective-permute-done | bytes 65568 | tf_op jit(solution)/shard_map/ppermute | solution.py:303
  106.2 1.1 collective-permute-done.4
  107.4 1.9 %collective-permute-start.12 = (f32[4,16,8,128]{3,2,1,0:T(8,128)S(1)}, f32[4,16,8,128]{3,2,1,0:T(8,128)S(1)}, u32[]{:S(2)}, u32[]{:S(2)}) collective-permute-start(f32[4,16,8,128]{3,2,1,0:T(8,128)S(1)} %get-tuple-element.37.refs_0_), channel_id=1, source_target_pairs={{0,96},{8,104},{16,112},{24,120},{32,0},{40,8},{48,16},{56,24},{64... | collective-permute-start | bytes 786440 | tf_op jit(solution)/shard_map/ppermute | solution.py:307
  109.3 0.3 collective-permute-start.11
  109.6 2.6 %collective-permute-start.10 = (f32[4,16,8,128]{3,2,1,0:T(8,128)S(1)}, f32[4,16,8,128]{3,2,1,0:T(8,128)S(1)}, u32[]{:S(2)}, u32[]{:S(2)}) collective-permute-start(f32[4,16,8,128]{3,2,1,0:T(8,128)S(1)} %get-tuple-element.37.refs_0_), channel_id=1, source_target_pairs={{0,64},{8,72},{16,80},{24,88},{32,96},{40,104},{48,112},{56,120},{... | collective-permute-start | bytes 786440 | tf_op jit(solution)/shard_map/ppermute | solution.py:307
  112.2 1.6 %collective-permute-start.15 = (f32[4,16,8,128]{3,2,1,0:T(8,128)S(1)}, f32[4,16,8,128]{3,2,1,0:T(8,128)S(1)}, u32[]{:S(2)}, u32[]{:S(2)}) collective-permute-start(f32[4,16,8,128]{3,2,1,0:T(8,128)S(1)} %get-tuple-element.38.refs_4_), channel_id=1, source_target_pairs={{0,24},{8,0},{16,8},{24,16},{32,56},{40,32},{48,40},{56,48},{64,88... | collective-permute-start | bytes 786440 | tf_op jit(solution)/shard_map/ppermute | solution.py:303
  113.8 0.4 collective-permute-start.14
  114.2 2.3 %collective-permute-done.12.refs_3_ = f32[4,16,8,128]{3,2,1,0:T(8,128)S(1)} collective-permute-done((f32[4,16,8,128]{3,2,1,0:T(8,128)S(1)}, f32[4,16,8,128]{3,2,1,0:T(8,128)S(1)}, u32[]{:S(2)}, u32[]{:S(2)}) %collective-permute-start.12) | collective-permute-done | bytes 262176 | tf_op jit(solution)/shard_map/ppermute | solution.py:307
  116.5 1.0 collective-permute-start.13
  117.4 4.1 %collective-permute-done.11.refs_2_ = f32[4,16,8,128]{3,2,1,0:T(8,128)S(1)} collective-permute-done((f32[4,16,8,128]{3,2,1,0:T(8,128)S(1)}, f32[4,16,8,128]{3,2,1,0:T(8,128)S(1)}, u32[]{:S(2)}, u32[]{:S(2)}) %collective-permute-start.11) | collective-permute-done | bytes 262176 | tf_op jit(solution)/shard_map/ppermute | solution.py:307
  121.5 3.8 %collective-permute-done.14.refs_6_ = f32[4,16,8,128]{3,2,1,0:T(8,128)S(1)} collective-permute-done((f32[4,16,8,128]{3,2,1,0:T(8,128)S(1)}, f32[4,16,8,128]{3,2,1,0:T(8,128)S(1)}, u32[]{:S(2)}, u32[]{:S(2)}) %collective-permute-start.14) | collective-permute-done | bytes 262176 | tf_op jit(solution)/shard_map/ppermute | solution.py:303
  125.3 2.2 %root_other.1 = (f32[4,128,256]{2,1,0:T(8,128)S(1)}, bf16[2048,256]{1,0:T(8,128)(2,1)S(1)}, bf16[2048,256]{1,0:T(8,128)(2,1)S(1)}) custom-call(f32[1024,2048]{1,0:T(8,128)S(1)} %bitcast.43, f32[4,16,8,128]{3,2,1,0:T(8,128)S(1)} %get-tuple-element.37.refs_0_, f32[4,16,8,128]{3,2,1,0:T(8,128)S(1)} %collective-permute-done.10.refs_1_, ...), custom_call_target="tpu_custom_call" | custom-call | flops 1610612736 | bytes 4194304 | tf_op jit(solution)/shard_map/root_other/pallas_call | solution.py:259
  127.5 0.3 collective-permute-start.16
  127.8 1.8 %root_mine.1 = f32[4,128,256]{2,1,0:T(8,128)S(1)} custom-call(bf16[2048,256]{1,0:T(8,128)(2,1)S(1)} %get-tuple-element.39.high_ref, bf16[2048,256]{1,0:T(8,128)(2,1)S(1)} %get-tuple-element.40.low_ref, f32[1024,2048]{1,0:T(8,128)S(1)} %bitcast.43), custom_call_target="tpu_custom_call" | custom-call | flops 1610612736 | bytes 4194304 | tf_op jit(solution)/shard_map/root_mine/pallas_call | solution.py:269
  129.6 0.1 collective-permute-done.16
  129.7 0.1 fusion.2
  129.7 0.6 collective-permute-start.17
  130.4 2.7 %collective-permute-start.19 = (f32[128,256]{1,0:T(8,128)S(1)}, f32[128,256]{1,0:T(8,128)S(1)}, u32[]{:S(2)}, u32[]{:S(2)}) collective-permute-start(f32[128,256]{1,0:T(8,128)S(1)} %get-tuple-element.43), channel_id=1, source_target_pairs={{0,6},{1,7},{2,0},{3,1},{4,2},{5,3},{6,4},{7,5},{8,14},{9,15},{10,... | collective-permute-start | bytes 393224 | tf_op jit(solution)/shard_map/ppermute | solution.py:286
  133.0 3.8 %collective-permute-done.17 = f32[128,256]{1,0:T(8,128)S(1)} collective-permute-done((f32[128,256]{1,0:T(8,128)S(1)}, f32[128,256]{1,0:T(8,128)S(1)}, u32[]{:S(2)}, u32[]{:S(2)}) %collective-permute-start.17) | collective-permute-done | bytes 131104 | tf_op jit(solution)/shard_map/ppermute | solution.py:286
  136.8 2.1 %collective-permute-done.19 = f32[128,256]{1,0:T(8,128)S(1)} collective-permute-done((f32[128,256]{1,0:T(8,128)S(1)}, f32[128,256]{1,0:T(8,128)S(1)}, u32[]{:S(2)}, u32[]{:S(2)}) %collective-permute-start.19) | collective-permute-done | bytes 131104 | tf_op jit(solution)/shard_map/ppermute | solution.py:286
  138.9 0.9 collective-permute-done.18
  139.8 0.7 fusion.6
  (16 shorter events, 0.1 us)
Async XLA Ops:
  2.5 59.4 %copy-start.1 = (f32[1024,1024]{1,0:T(8,128)S(1)}, f32[1024,1024]{1,0:T(8,128)}, u32[]{:S(2)}) copy-start(f32[1024,1024]{1,0:T(8,128)} %factor_ref.1) | copy-start | bytes 12582916
  39.8 22.1 %copy-start = (f32[1024,1024]{1,0:T(8,128)S(1)}, f32[1024,1024]{1,0:T(8,128)}, u32[]{:S(2)}) copy-start(f32[1024,1024]{1,0:T(8,128)} %pivot_ref.1) | copy-start | bytes 12582916
  42.2 83.1 %slice-start = ((s8[8388608]{0:T(1024)(128)(4,1)}), s8[4194304]{0:T(1024)(128)(4,1)S(1)}, s32[]{:S(2)}) async-start(s8[8388608]{0:T(1024)(128)(4,1)} %bitcast.42), calls=%async_computation.3 | async-start | bytes 8388608
  61.9 63.4 %slice-start.1 = ((s8[8388608]{0:T(1024)(128)(4,1)}), s8[4194304]{0:T(1024)(128)(4,1)S(1)}, s32[]{:S(2)}) async-start(s8[8388608]{0:T(1024)(128)(4,1)} %bitcast.42), calls=%async_computation.4 | async-start | bytes 8388608
  83.9 2.0 %collective-permute-start = (f32[4,2,16,8,128]{4,3,2,1,0:T(8,128)S(1)}, f32[4,2,16,8,128]{4,3,2,1,0:T(8,128)S(1)}, u32[]{:S(2)}, u32[]{:S(2)}) collective-permute-start(f32[4,2,16,8,128]{4,3,2,1,0:T(8,128)S(1)} %get-tuple-element.28), channel_id=1, source_target_pairs={{0,1},{1,0},{2,3},{3,2},{4,5},{5,4},{6,7},{7,6},{8,9},{9,8},{10,11... | collective-permute-start | bytes 1572872 | tf_op jit(solution)/shard_map/ppermute | solution.py:283
  86.0 6.8 %collective-permute-start.1 = (f32[2,16,8,128]{3,2,1,0:T(8,128)S(1)}, f32[2,16,8,128]{3,2,1,0:T(8,128)S(1)}, u32[]{:S(2)}, u32[]{:S(2)}) collective-permute-start(f32[2,16,8,128]{3,2,1,0:T(8,128)S(1)} %get-tuple-element.45), channel_id=1, source_target_pairs={{0,2},{1,3},{2,4},{3,5},{4,6},{5,7},{6,0},{7,1},{8,10},{9,11},{10,... | collective-permute-start | bytes 393224 | tf_op jit(solution)/shard_map/ppermute | solution.py:286
  87.5 7.4 %collective-permute-start.3 = (f32[2,16,8,128]{3,2,1,0:T(8,128)S(1)}, f32[2,16,8,128]{3,2,1,0:T(8,128)S(1)}, u32[]{:S(2)}, u32[]{:S(2)}) collective-permute-start(f32[2,16,8,128]{3,2,1,0:T(8,128)S(1)} %get-tuple-element.46), channel_id=1, source_target_pairs={{0,6},{1,7},{2,0},{3,1},{4,2},{5,3},{6,4},{7,5},{8,14},{9,15},{10,... | collective-permute-start | bytes 393224 | tf_op jit(solution)/shard_map/ppermute | solution.py:286
  89.3 7.3 %collective-permute-start.2 = (f32[2,16,8,128]{3,2,1,0:T(8,128)S(1)}, f32[2,16,8,128]{3,2,1,0:T(8,128)S(1)}, u32[]{:S(2)}, u32[]{:S(2)}) collective-permute-start(f32[2,16,8,128]{3,2,1,0:T(8,128)S(1)} %get-tuple-element.47), channel_id=1, source_target_pairs={{0,4},{1,5},{2,6},{3,7},{4,0},{5,1},{6,2},{7,3},{8,12},{9,13},{10,... | collective-permute-start | bytes 393224 | tf_op jit(solution)/shard_map/ppermute | solution.py:286
  96.6 4.9 %collective-permute-start.9 = (f32[16,8,128]{2,1,0:T(8,128)S(1)}, f32[16,8,128]{2,1,0:T(8,128)S(1)}, u32[]{:S(2)}, u32[]{:S(2)}) collective-permute-start(f32[16,8,128]{2,1,0:T(8,128)S(1)} %get-tuple-element.33), channel_id=1, source_target_pairs={{0,96},{8,104},{16,112},{24,120},{32,0},{40,8},{48,16},{56,24},{64... | collective-permute-start | bytes 196616 | tf_op jit(solution)/shard_map/ppermute | solution.py:307
  97.5 5.6 %collective-permute-start.8 = (f32[16,8,128]{2,1,0:T(8,128)S(1)}, f32[16,8,128]{2,1,0:T(8,128)S(1)}, u32[]{:S(2)}, u32[]{:S(2)}) collective-permute-start(f32[16,8,128]{2,1,0:T(8,128)S(1)} %get-tuple-element.33), channel_id=1, source_target_pairs={{0,32},{8,40},{16,48},{24,56},{32,64},{40,72},{48,80},{56,88},{64,... | collective-permute-start | bytes 196616 | tf_op jit(solution)/shard_map/ppermute | solution.py:307
  98.7 5.8 %collective-permute-start.7 = (f32[16,8,128]{2,1,0:T(8,128)S(1)}, f32[16,8,128]{2,1,0:T(8,128)S(1)}, u32[]{:S(2)}, u32[]{:S(2)}) collective-permute-start(f32[16,8,128]{2,1,0:T(8,128)S(1)} %get-tuple-element.33), channel_id=1, source_target_pairs={{0,64},{8,72},{16,80},{24,88},{32,96},{40,104},{48,112},{56,120},{... | collective-permute-start | bytes 196616 | tf_op jit(solution)/shard_map/ppermute | solution.py:307
  99.5 5.0 %collective-permute-start.6 = (f32[16,8,128]{2,1,0:T(8,128)S(1)}, f32[16,8,128]{2,1,0:T(8,128)S(1)}, u32[]{:S(2)}, u32[]{:S(2)}) collective-permute-start(f32[16,8,128]{2,1,0:T(8,128)S(1)} %get-tuple-element.29), channel_id=1, source_target_pairs={{0,24},{8,0},{16,8},{24,16},{32,56},{40,32},{48,40},{56,48},{64,88... | collective-permute-start | bytes 196616 | tf_op jit(solution)/shard_map/ppermute | solution.py:303
  100.7 5.5 %collective-permute-start.5 = (f32[16,8,128]{2,1,0:T(8,128)S(1)}, f32[16,8,128]{2,1,0:T(8,128)S(1)}, u32[]{:S(2)}, u32[]{:S(2)}) collective-permute-start(f32[16,8,128]{2,1,0:T(8,128)S(1)} %get-tuple-element.29), channel_id=1, source_target_pairs={{0,8},{8,16},{16,24},{24,0},{32,40},{40,48},{48,56},{56,32},{64,72... | collective-permute-start | bytes 196616 | tf_op jit(solution)/shard_map/ppermute | solution.py:303
  101.6 5.8 %collective-permute-start.4 = (f32[16,8,128]{2,1,0:T(8,128)S(1)}, f32[16,8,128]{2,1,0:T(8,128)S(1)}, u32[]{:S(2)}, u32[]{:S(2)}) collective-permute-start(f32[16,8,128]{2,1,0:T(8,128)S(1)} %get-tuple-element.29), channel_id=1, source_target_pairs={{0,16},{8,24},{16,0},{24,8},{32,48},{40,56},{48,32},{56,40},{64,80... | collective-permute-start | bytes 196616 | tf_op jit(solution)/shard_map/ppermute | solution.py:303
  107.4 9.1 %collective-permute-start.12 = (f32[4,16,8,128]{3,2,1,0:T(8,128)S(1)}, f32[4,16,8,128]{3,2,1,0:T(8,128)S(1)}, u32[]{:S(2)}, u32[]{:S(2)}) collective-permute-start(f32[4,16,8,128]{3,2,1,0:T(8,128)S(1)} %get-tuple-element.37.refs_0_), channel_id=1, source_target_pairs={{0,96},{8,104},{16,112},{24,120},{32,0},{40,8},{48,16},{56,24},{64... | collective-permute-start | bytes 786440 | tf_op jit(solution)/shard_map/ppermute | solution.py:307
  109.3 12.2 %collective-permute-start.11 = (f32[4,16,8,128]{3,2,1,0:T(8,128)S(1)}, f32[4,16,8,128]{3,2,1,0:T(8,128)S(1)}, u32[]{:S(2)}, u32[]{:S(2)}) collective-permute-start(f32[4,16,8,128]{3,2,1,0:T(8,128)S(1)} %get-tuple-element.37.refs_0_), channel_id=1, source_target_pairs={{0,32},{8,40},{16,48},{24,56},{32,64},{40,72},{48,80},{56,88},{64,... | collective-permute-start | bytes 786440 | tf_op jit(solution)/shard_map/ppermute | solution.py:307
  109.6 11.9 %collective-permute-start.10 = (f32[4,16,8,128]{3,2,1,0:T(8,128)S(1)}, f32[4,16,8,128]{3,2,1,0:T(8,128)S(1)}, u32[]{:S(2)}, u32[]{:S(2)}) collective-permute-start(f32[4,16,8,128]{3,2,1,0:T(8,128)S(1)} %get-tuple-element.37.refs_0_), channel_id=1, source_target_pairs={{0,64},{8,72},{16,80},{24,88},{32,96},{40,104},{48,112},{56,120},{... | collective-permute-start | bytes 786440 | tf_op jit(solution)/shard_map/ppermute | solution.py:307
  112.2 9.3 %collective-permute-start.15 = (f32[4,16,8,128]{3,2,1,0:T(8,128)S(1)}, f32[4,16,8,128]{3,2,1,0:T(8,128)S(1)}, u32[]{:S(2)}, u32[]{:S(2)}) collective-permute-start(f32[4,16,8,128]{3,2,1,0:T(8,128)S(1)} %get-tuple-element.38.refs_4_), channel_id=1, source_target_pairs={{0,24},{8,0},{16,8},{24,16},{32,56},{40,32},{48,40},{56,48},{64,88... | collective-permute-start | bytes 786440 | tf_op jit(solution)/shard_map/ppermute | solution.py:303
  113.8 11.5 %collective-permute-start.14 = (f32[4,16,8,128]{3,2,1,0:T(8,128)S(1)}, f32[4,16,8,128]{3,2,1,0:T(8,128)S(1)}, u32[]{:S(2)}, u32[]{:S(2)}) collective-permute-start(f32[4,16,8,128]{3,2,1,0:T(8,128)S(1)} %get-tuple-element.38.refs_4_), channel_id=1, source_target_pairs={{0,8},{8,16},{16,24},{24,0},{32,40},{40,48},{48,56},{56,32},{64,72... | collective-permute-start | bytes 786440 | tf_op jit(solution)/shard_map/ppermute | solution.py:303
  116.5 8.8 %collective-permute-start.13 = (f32[4,16,8,128]{3,2,1,0:T(8,128)S(1)}, f32[4,16,8,128]{3,2,1,0:T(8,128)S(1)}, u32[]{:S(2)}, u32[]{:S(2)}) collective-permute-start(f32[4,16,8,128]{3,2,1,0:T(8,128)S(1)} %get-tuple-element.38.refs_4_), channel_id=1, source_target_pairs={{0,16},{8,24},{16,0},{24,8},{32,48},{40,56},{48,32},{56,40},{64,80... | collective-permute-start | bytes 786440 | tf_op jit(solution)/shard_map/ppermute | solution.py:303
  127.5 2.2 %collective-permute-start.16 = (f32[4,128,256]{2,1,0:T(8,128)S(1)}, f32[4,128,256]{2,1,0:T(8,128)S(1)}, u32[]{:S(2)}, u32[]{:S(2)}) collective-permute-start(f32[4,128,256]{2,1,0:T(8,128)S(1)} %get-tuple-element.41), channel_id=1, source_target_pairs={{0,1},{1,0},{2,3},{3,2},{4,5},{5,4},{6,7},{7,6},{8,9},{9,8},{10,11... | collective-permute-start | bytes 1572872 | tf_op jit(solution)/shard_map/ppermute | solution.py:283
  129.7 7.1 %collective-permute-start.17 = (f32[128,256]{1,0:T(8,128)S(1)}, f32[128,256]{1,0:T(8,128)S(1)}, u32[]{:S(2)}, u32[]{:S(2)}) collective-permute-start(f32[128,256]{1,0:T(8,128)S(1)} %get-tuple-element.42), channel_id=1, source_target_pairs={{0,2},{1,3},{2,4},{3,5},{4,6},{5,7},{6,0},{7,1},{8,10},{9,11},{10,... | collective-permute-start | bytes 393224 | tf_op jit(solution)/shard_map/ppermute | solution.py:286
  130.4 8.6 %collective-permute-start.19 = (f32[128,256]{1,0:T(8,128)S(1)}, f32[128,256]{1,0:T(8,128)S(1)}, u32[]{:S(2)}, u32[]{:S(2)}) collective-permute-start(f32[128,256]{1,0:T(8,128)S(1)} %get-tuple-element.43), channel_id=1, source_target_pairs={{0,6},{1,7},{2,0},{3,1},{4,2},{5,3},{6,4},{7,5},{8,14},{9,15},{10,... | collective-permute-start | bytes 393224 | tf_op jit(solution)/shard_map/ppermute | solution.py:286
  133.0 6.8 %collective-permute-start.18 = (f32[128,256]{1,0:T(8,128)S(1)}, f32[128,256]{1,0:T(8,128)S(1)}, u32[]{:S(2)}, u32[]{:S(2)}) collective-permute-start(f32[128,256]{1,0:T(8,128)S(1)} %get-tuple-element.44), channel_id=1, source_target_pairs={{0,4},{1,5},{2,6},{3,7},{4,0},{5,1},{6,2},{7,3},{8,12},{9,13},{10,... | collective-permute-start | bytes 393224 | tf_op jit(solution)/shard_map/ppermute | solution.py:286

commit v6 on v4

--- a/solution.py
+++ b/solution.py
@@ -196,29 +196,38 @@
     )(arrived, pivot_inverse, update_factor)
 
 
-def subtract_kernel(rows, half, words_ref, arrived_ref, start_ref, mine_ref, other_ref, acc):
+def subtract_kernel(rows, half, words_ref, arrived_ref, start_ref, mine_ref, other_ref, acc, table, sem):
     slots = rows * half
+    copy = pltpu.make_async_copy(words_ref, table, sem)
+    copy.start()
     acc[...] = start_ref[pl.ds(slots, BLK)]
+    copy.wait()
 
     def add(owner, carry):
         for block in range(half):
-            acc[words_ref[owner, RB_DEV + block] - slots] -= arrived_ref[owner, block]
+            acc[table[owner, RB_DEV + block] - slots] -= arrived_ref[owner, block]
         return carry
 
     lax.fori_loop(0, rows, add, 0)
-    mine_ref[...] = acc[pl.ds(0, BLK // CORES)].reshape(mine_ref.shape)
-    other_ref[...] = acc[pl.ds(BLK // CORES, BLK // CORES)].reshape(mine_ref.shape)
+    part = mine_ref.shape[:1] + mine_ref.shape[2:]
+    for lane in range(TILES):
+        mine_ref[:, lane] = acc[pl.ds(0, BLK // CORES), lane].reshape(part)
+        other_ref[:, lane] = acc[pl.ds(BLK // CORES, BLK // CORES), lane].reshape(part)
 
 
 def subtract(words, arrived, start, chips):
     rows, half = arrived.shape[:2]
-    out = f32(chips, BLK // (CORES * chips), TILES, SUB, LANES)
+    out = f32(chips, TILES, BLK // (CORES * chips), SUB, LANES)
     return pl.pallas_call(
         functools.partial(subtract_kernel, rows, half),
         out_shape=(out, out),
-        in_specs=[SMEM, VMEM, VMEM],
+        in_specs=[VMEM] * 3,
         out_specs=(VMEM, VMEM),
-        scratch_shapes=[pltpu.VMEM((BLK, TILES, SUB, LANES), jnp.float32)],
+        scratch_shapes=[
+            pltpu.VMEM((BLK, TILES, SUB, LANES), jnp.float32),
+            pltpu.SMEM((rows, LANES), jnp.int32),
+            pltpu.SemaphoreType.DMA,
+        ],
         compiler_params=PARAMS,
         name="subtract",
     )(words, arrived, start)
@@ -301,7 +310,7 @@
     def along_z(x):
         return [x] + [lax.ppermute(x, "row", [(i, (i + side * k) % rows) for i in range(rows)]) for k in range(1, side)]
 
-    first, second = lax.optimization_barrier((along_y(piece[:, 0]), along_z(piece[:, 1])))
+    first, second = lax.optimization_barrier((along_y(piece[0]), along_z(piece[1])))
     first, second = lax.optimization_barrier((jnp.stack(first), jnp.stack(second)))
     return along_z(first) + along_y(second)
 

time: 141 us -> 141 us (level)
  no operation moved by 1% of the time
where the time goes in v6:
time: 141 us
  blocking collectives  74.9 us (53%)
  waiting for transfers between devices  30.4 us (22%)
  starting transfers between devices  21.6 us (15%)
  Pallas kernels  12.2 us (9%)
    all_to_all x3, blocking collectives, exchange(): return lax.all_to_all(x, axis, split_axis=0, concat_axis=0, tiled=True)  74.9 us
    ppermute x6, waiting for transfers between devices, reduce_cols(): lax.ppermute(mine[distance] + sibling[distance], 'col', [(c, (c + CORES *...  12.3 us
    ppermute x6, waiting for transfers between devices, along_z(): lax.ppermute(x, 'row', [(i, (i + side * k) % rows) for i in range(rows)])  9.51 us
    ppermute x6, starting transfers between devices, reduce_cols(): lax.ppermute(mine[distance] + sibling[distance], 'col', [(c, (c + CORES *...  8.43 us
    ppermute x6, starting transfers between devices, along_z(): lax.ppermute(x, 'row', [(i, (i + side * k) % rows) for i in range(rows)])  7.72 us
    ppermute x6, waiting for transfers between devices, along_y(): lax.ppermute(x, 'row', [(i, i // side * side + (i + k) % side) for i in r...  6.66 us
    ppermute x6, starting transfers between devices, along_y(): lax.ppermute(x, 'row', [(i, i // side * side + (i + k) % side) for i in r...  5.06 us
    pallas_call x1, Pallas kernels, front(): pl.pallas_call(front_kernel, out_shape=(f32(order, NRHS), f32(rows, half,...  2.89 us
  transfers between devices with their start and end apart: 20, of which 17 were waited for; matrix products, arithmetic and copies ran while one was open for 0% of the time, Pallas kernels for 1%

profile of v6, /device:TPU:0, one launch (start us, length us, event | category | flops | bytes accessed | tf_op | source)
XLA Modules:
  0.0 140.8 jit_solution(11600588379777877680)
XLA Ops:
  0.6 1.9 %pack.1 = f32[16,33,8,128]{3,2,1,0:T(8,128)S(1)} custom-call(s32[16]{0:T(128)} %target_ref.1, s32[8]{0:T(128)} %map_ref.1, f32[16,16,8,256]{3,2,1,0:T(8,128)} %bitcast.45), custom_call_target="tpu_custom_call" | custom-call | tf_op jit(solution)/shard_map/pack/pallas_call | solution.py:84
  2.5 37.3 %all_to_all.15.arrived_ref = f32[16,33,8,128]{3,2,1,0:T(8,128)S(1)} all-to-all(f32[16,33,8,128]{3,2,1,0:T(8,128)S(1)} %pack.1), channel_id=1, replica_groups=mesh['row'=16,'col'=8] {'row'}, dimensions={0} | all-to-all | bytes 4325376 | tf_op jit(solution)/shard_map/all_to_all | solution.py:48
  39.8 2.4 %route.1 = (f32[128,2,8,128]{3,2,1,0:T(8,128)S(1)}, f32[256,2,8,128]{3,2,1,0:T(8,128)S(1)}, s32[16,128]{1,0:T(8,128)S(1)}) custom-call(f32[16,33,8,128]{3,2,1,0:T(8,128)S(1)} %all_to_all.15.arrived_ref), custom_call_target="tpu_custom_call" | custom-call | tf_op jit(solution)/shard_map/route/pallas_call | solution.py:137
  42.2 19.7 %all_to_all.16.arrived_ref = f32[16,8,2,8,128]{4,3,2,1,0:T(8,128)S(1)} all-to-all(f32[16,8,2,8,128]{4,3,2,1,0:T(8,128)S(1)} %bitcast.44), channel_id=1, replica_groups=mesh['row'=16,'col'=8] {'row'}, dimensions={0} | all-to-all | bytes 2097152 | tf_op jit(solution)/shard_map/all_to_all | solution.py:48
  61.9 2.9 %front.1 = (f32[1024,256]{1,0:T(8,128)}, f32[16,8,2,8,128]{4,3,2,1,0:T(8,128)S(1)}) custom-call(f32[16,8,2,8,128]{4,3,2,1,0:T(8,128)S(1)} %all_to_all.16.arrived_ref, f32[1024,1024]{1,0:T(8,128)S(1)} %copy-done, f32[1024,1024]{1,0:T(8,128)S(1)} %copy-done.1), custom_call_target="tpu_custom_call" | custom-call | tf_op jit(solution)/shard_map/front/pallas_call | solution.py:188
  64.8 17.9 %all_to_all.17.arrived_ref = f32[16,8,2,8,128]{4,3,2,1,0:T(8,128)S(1)} all-to-all(f32[16,8,2,8,128]{4,3,2,1,0:T(8,128)S(1)} %get-tuple-element.25), channel_id=1, replica_groups=mesh['row'=16,'col'=8] {'row'}, dimensions={0} | all-to-all | bytes 2097152 | tf_op jit(solution)/shard_map/all_to_all | solution.py:48
  82.7 1.2 subtract.1
  83.8 0.1 collective-permute-start
  83.9 1.9 %collective-permute-done = f32[4,2,16,8,128]{4,3,2,1,0:T(8,128)S(1)} collective-permute-done((f32[4,2,16,8,128]{4,3,2,1,0:T(8,128)S(1)}, f32[4,2,16,8,128]{4,3,2,1,0:T(8,128)S(1)}, u32[]{:S(2)}, u32[]{:S(2)}) %collective-permute-start) | collective-permute-done | bytes 524320 | tf_op jit(solution)/shard_map/ppermute | solution.py:290
  85.8 0.1 fusion.9
  85.9 1.6 %collective-permute-start.1 = (f32[2,16,8,128]{3,2,1,0:T(8,128)S(1)}, f32[2,16,8,128]{3,2,1,0:T(8,128)S(1)}, u32[]{:S(2)}, u32[]{:S(2)}) collective-permute-start(f32[2,16,8,128]{3,2,1,0:T(8,128)S(1)} %get-tuple-element.45), channel_id=1, source_target_pairs={{0,2},{1,3},{2,4},{3,5},{4,6},{5,7},{6,0},{7,1},{8,10},{9,11},{10,... | collective-permute-start | bytes 393224 | tf_op jit(solution)/shard_map/ppermute | solution.py:293
  87.5 1.7 %collective-permute-start.3 = (f32[2,16,8,128]{3,2,1,0:T(8,128)S(1)}, f32[2,16,8,128]{3,2,1,0:T(8,128)S(1)}, u32[]{:S(2)}, u32[]{:S(2)}) collective-permute-start(f32[2,16,8,128]{3,2,1,0:T(8,128)S(1)} %get-tuple-element.46), channel_id=1, source_target_pairs={{0,6},{1,7},{2,0},{3,1},{4,2},{5,3},{6,4},{7,5},{8,14},{9,15},{10,... | collective-permute-start | bytes 393224 | tf_op jit(solution)/shard_map/ppermute | solution.py:293
  89.2 1.8 %collective-permute-start.2 = (f32[2,16,8,128]{3,2,1,0:T(8,128)S(1)}, f32[2,16,8,128]{3,2,1,0:T(8,128)S(1)}, u32[]{:S(2)}, u32[]{:S(2)}) collective-permute-start(f32[2,16,8,128]{3,2,1,0:T(8,128)S(1)} %get-tuple-element.47), channel_id=1, source_target_pairs={{0,4},{1,5},{2,6},{3,7},{4,0},{5,1},{6,2},{7,3},{8,12},{9,13},{10,... | collective-permute-start | bytes 393224 | tf_op jit(solution)/shard_map/ppermute | solution.py:293
  91.0 1.7 %collective-permute-done.1 = f32[2,16,8,128]{3,2,1,0:T(8,128)S(1)} collective-permute-done((f32[2,16,8,128]{3,2,1,0:T(8,128)S(1)}, f32[2,16,8,128]{3,2,1,0:T(8,128)S(1)}, u32[]{:S(2)}, u32[]{:S(2)}) %collective-permute-start.1) | collective-permute-done | bytes 131104 | tf_op jit(solution)/shard_map/ppermute | solution.py:293
  92.7 2.1 %collective-permute-done.3 = f32[2,16,8,128]{3,2,1,0:T(8,128)S(1)} collective-permute-done((f32[2,16,8,128]{3,2,1,0:T(8,128)S(1)}, f32[2,16,8,128]{3,2,1,0:T(8,128)S(1)}, u32[]{:S(2)}, u32[]{:S(2)}) %collective-permute-start.3) | collective-permute-done | bytes 131104 | tf_op jit(solution)/shard_map/ppermute | solution.py:293
  94.8 1.7 %collective-permute-done.2 = f32[2,16,8,128]{3,2,1,0:T(8,128)S(1)} collective-permute-done((f32[2,16,8,128]{3,2,1,0:T(8,128)S(1)}, f32[2,16,8,128]{3,2,1,0:T(8,128)S(1)}, u32[]{:S(2)}, u32[]{:S(2)}) %collective-permute-start.2) | collective-permute-done | bytes 131104 | tf_op jit(solution)/shard_map/ppermute | solution.py:293
  96.6 0.9 collective-permute-start.9
  97.5 1.0 collective-permute-start.8
  98.5 0.4 collective-permute-start.7
  98.9 1.2 collective-permute-start.6
  100.1 1.4 %collective-permute-start.5 = (f32[16,8,128]{2,1,0:T(8,128)S(1)}, f32[16,8,128]{2,1,0:T(8,128)S(1)}, u32[]{:S(2)}, u32[]{:S(2)}) collective-permute-start(f32[16,8,128]{2,1,0:T(8,128)S(1)} %get-tuple-element.29), channel_id=1, source_target_pairs={{0,16},{8,24},{16,0},{24,8},{32,48},{40,56},{48,32},{56,40},{64,80... | collective-permute-start | bytes 196616 | tf_op jit(solution)/shard_map/ppermute | solution.py:306
  101.5 0.2 collective-permute-start.4
  101.7 1.8 %collective-permute-done.8 = f32[16,8,128]{2,1,0:T(8,128)S(1)} collective-permute-done((f32[16,8,128]{2,1,0:T(8,128)S(1)}, f32[16,8,128]{2,1,0:T(8,128)S(1)}, u32[]{:S(2)}, u32[]{:S(2)}) %collective-permute-start.8) | collective-permute-done | bytes 65568 | tf_op jit(solution)/shard_map/ppermute | solution.py:311
  103.6 0.7 collective-permute-done.7
  104.2 1.6 %collective-permute-done.5 = f32[16,8,128]{2,1,0:T(8,128)S(1)} collective-permute-done((f32[16,8,128]{2,1,0:T(8,128)S(1)}, f32[16,8,128]{2,1,0:T(8,128)S(1)}, u32[]{:S(2)}, u32[]{:S(2)}) %collective-permute-start.5) | collective-permute-done | bytes 65568 | tf_op jit(solution)/shard_map/ppermute | solution.py:306
  105.8 1.2 collective-permute-done.4
  107.0 2.6 %collective-permute-start.12 = (f32[4,16,8,128]{3,2,1,0:T(8,128)S(1)}, f32[4,16,8,128]{3,2,1,0:T(8,128)S(1)}, u32[]{:S(2)}, u32[]{:S(2)}) collective-permute-start(f32[4,16,8,128]{3,2,1,0:T(8,128)S(1)} %get-tuple-element.37.refs_0_), channel_id=1, source_target_pairs={{0,96},{8,104},{16,112},{24,120},{32,0},{40,8},{48,16},{56,24},{64... | collective-permute-start | bytes 786440 | tf_op jit(solution)/shard_map/ppermute | solution.py:311
  109.7 1.6 %collective-permute-start.11 = (f32[4,16,8,128]{3,2,1,0:T(8,128)S(1)}, f32[4,16,8,128]{3,2,1,0:T(8,128)S(1)}, u32[]{:S(2)}, u32[]{:S(2)}) collective-permute-start(f32[4,16,8,128]{3,2,1,0:T(8,128)S(1)} %get-tuple-element.37.refs_0_), channel_id=1, source_target_pairs={{0,64},{8,72},{16,80},{24,88},{32,96},{40,104},{48,112},{56,120},{... | collective-permute-start | bytes 786440 | tf_op jit(solution)/shard_map/ppermute | solution.py:311
  111.3 1.2 collective-permute-start.10
  112.5 0.9 collective-permute-start.15
  113.3 0.9 collective-permute-start.14
  114.2 3.8 %collective-permute-done.12.refs_3_ = f32[4,16,8,128]{3,2,1,0:T(8,128)S(1)} collective-permute-done((f32[4,16,8,128]{3,2,1,0:T(8,128)S(1)}, f32[4,16,8,128]{3,2,1,0:T(8,128)S(1)}, u32[]{:S(2)}, u32[]{:S(2)}) %collective-permute-start.12) | collective-permute-done | bytes 262176 | tf_op jit(solution)/shard_map/ppermute | solution.py:311
  118.0 0.5 collective-permute-start.13
  118.5 0.5 collective-permute-done.11.refs_2_
  119.0 2.7 %collective-permute-done.10.refs_1_ = f32[4,16,8,128]{3,2,1,0:T(8,128)S(1)} collective-permute-done((f32[4,16,8,128]{3,2,1,0:T(8,128)S(1)}, f32[4,16,8,128]{3,2,1,0:T(8,128)S(1)}, u32[]{:S(2)}, u32[]{:S(2)}) %collective-permute-start.10) | collective-permute-done | bytes 262176 | tf_op jit(solution)/shard_map/ppermute | solution.py:311
  121.7 0.1 collective-permute-done.14.refs_6_
  121.8 3.8 %collective-permute-done.13.refs_5_ = f32[4,16,8,128]{3,2,1,0:T(8,128)S(1)} collective-permute-done((f32[4,16,8,128]{3,2,1,0:T(8,128)S(1)}, f32[4,16,8,128]{3,2,1,0:T(8,128)S(1)}, u32[]{:S(2)}, u32[]{:S(2)}) %collective-permute-start.13) | collective-permute-done | bytes 262176 | tf_op jit(solution)/shard_map/ppermute | solution.py:306
  125.6 2.2 %root_other.1 = (f32[4,128,256]{2,1,0:T(8,128)S(1)}, bf16[2048,256]{1,0:T(8,128)(2,1)S(1)}, bf16[2048,256]{1,0:T(8,128)(2,1)S(1)}) custom-call(f32[1024,2048]{1,0:T(8,128)S(1)} %bitcast.43, f32[4,16,8,128]{3,2,1,0:T(8,128)S(1)} %get-tuple-element.37.refs_0_, f32[4,16,8,128]{3,2,1,0:T(8,128)S(1)} %collective-permute-done.10.refs_1_, ...), custom_call_target="tpu_custom_call" | custom-call | flops 1610612736 | bytes 4194304 | tf_op jit(solution)/shard_map/root_other/pallas_call | solution.py:266
  127.8 0.3 collective-permute-start.16
  128.1 1.8 %root_mine.1 = f32[4,128,256]{2,1,0:T(8,128)S(1)} custom-call(bf16[2048,256]{1,0:T(8,128)(2,1)S(1)} %get-tuple-element.39.high_ref, bf16[2048,256]{1,0:T(8,128)(2,1)S(1)} %get-tuple-element.40.low_ref, f32[1024,2048]{1,0:T(8,128)S(1)} %bitcast.43), custom_call_target="tpu_custom_call" | custom-call | flops 1610612736 | bytes 4194304 | tf_op jit(solution)/shard_map/root_mine/pallas_call | solution.py:276
  129.8 0.1 collective-permute-done.16
  130.0 0.1 fusion.2
  130.0 0.9 collective-permute-start.17
  130.9 2.4 %collective-permute-start.19 = (f32[128,256]{1,0:T(8,128)S(1)}, f32[128,256]{1,0:T(8,128)S(1)}, u32[]{:S(2)}, u32[]{:S(2)}) collective-permute-start(f32[128,256]{1,0:T(8,128)S(1)} %get-tuple-element.43), channel_id=1, source_target_pairs={{0,6},{1,7},{2,0},{3,1},{4,2},{5,3},{6,4},{7,5},{8,14},{9,15},{10,... | collective-permute-start | bytes 393224 | tf_op jit(solution)/shard_map/ppermute | solution.py:293
  133.3 3.8 %collective-permute-done.17 = f32[128,256]{1,0:T(8,128)S(1)} collective-permute-done((f32[128,256]{1,0:T(8,128)S(1)}, f32[128,256]{1,0:T(8,128)S(1)}, u32[]{:S(2)}, u32[]{:S(2)}) %collective-permute-start.17) | collective-permute-done | bytes 131104 | tf_op jit(solution)/shard_map/ppermute | solution.py:293
  137.1 2.1 %collective-permute-done.19 = f32[128,256]{1,0:T(8,128)S(1)} collective-permute-done((f32[128,256]{1,0:T(8,128)S(1)}, f32[128,256]{1,0:T(8,128)S(1)}, u32[]{:S(2)}, u32[]{:S(2)}) %collective-permute-start.19) | collective-permute-done | bytes 131104 | tf_op jit(solution)/shard_map/ppermute | solution.py:293
  139.2 0.9 collective-permute-done.18
  140.1 0.7 fusion.6
  (16 shorter events, 0.1 us)
Async XLA Ops:
  2.5 59.4 %copy-start.1 = (f32[1024,1024]{1,0:T(8,128)S(1)}, f32[1024,1024]{1,0:T(8,128)}, u32[]{:S(2)}) copy-start(f32[1024,1024]{1,0:T(8,128)} %factor_ref.1) | copy-start | bytes 12582916
  39.8 22.1 %copy-start = (f32[1024,1024]{1,0:T(8,128)S(1)}, f32[1024,1024]{1,0:T(8,128)}, u32[]{:S(2)}) copy-start(f32[1024,1024]{1,0:T(8,128)} %pivot_ref.1) | copy-start | bytes 12582916
  42.2 83.4 %slice-start = ((s8[8388608]{0:T(1024)(128)(4,1)}), s8[4194304]{0:T(1024)(128)(4,1)S(1)}, s32[]{:S(2)}) async-start(s8[8388608]{0:T(1024)(128)(4,1)} %bitcast.42), calls=%async_computation.3 | async-start | bytes 8388608
  61.9 63.7 %slice-start.1 = ((s8[8388608]{0:T(1024)(128)(4,1)}), s8[4194304]{0:T(1024)(128)(4,1)S(1)}, s32[]{:S(2)}) async-start(s8[8388608]{0:T(1024)(128)(4,1)} %bitcast.42), calls=%async_computation.4 | async-start | bytes 8388608
  83.8 2.0 %collective-permute-start = (f32[4,2,16,8,128]{4,3,2,1,0:T(8,128)S(1)}, f32[4,2,16,8,128]{4,3,2,1,0:T(8,128)S(1)}, u32[]{:S(2)}, u32[]{:S(2)}) collective-permute-start(f32[4,2,16,8,128]{4,3,2,1,0:T(8,128)S(1)} %get-tuple-element.28), channel_id=1, source_target_pairs={{0,1},{1,0},{2,3},{3,2},{4,5},{5,4},{6,7},{7,6},{8,9},{9,8},{10,11... | collective-permute-start | bytes 1572872 | tf_op jit(solution)/shard_map/ppermute | solution.py:290
  85.9 6.8 %collective-permute-start.1 = (f32[2,16,8,128]{3,2,1,0:T(8,128)S(1)}, f32[2,16,8,128]{3,2,1,0:T(8,128)S(1)}, u32[]{:S(2)}, u32[]{:S(2)}) collective-permute-start(f32[2,16,8,128]{3,2,1,0:T(8,128)S(1)} %get-tuple-element.45), channel_id=1, source_target_pairs={{0,2},{1,3},{2,4},{3,5},{4,6},{5,7},{6,0},{7,1},{8,10},{9,11},{10,... | collective-permute-start | bytes 393224 | tf_op jit(solution)/shard_map/ppermute | solution.py:293
  87.5 7.4 %collective-permute-start.3 = (f32[2,16,8,128]{3,2,1,0:T(8,128)S(1)}, f32[2,16,8,128]{3,2,1,0:T(8,128)S(1)}, u32[]{:S(2)}, u32[]{:S(2)}) collective-permute-start(f32[2,16,8,128]{3,2,1,0:T(8,128)S(1)} %get-tuple-element.46), channel_id=1, source_target_pairs={{0,6},{1,7},{2,0},{3,1},{4,2},{5,3},{6,4},{7,5},{8,14},{9,15},{10,... | collective-permute-start | bytes 393224 | tf_op jit(solution)/shard_map/ppermute | solution.py:293
  89.2 7.3 %collective-permute-start.2 = (f32[2,16,8,128]{3,2,1,0:T(8,128)S(1)}, f32[2,16,8,128]{3,2,1,0:T(8,128)S(1)}, u32[]{:S(2)}, u32[]{:S(2)}) collective-permute-start(f32[2,16,8,128]{3,2,1,0:T(8,128)S(1)} %get-tuple-element.47), channel_id=1, source_target_pairs={{0,4},{1,5},{2,6},{3,7},{4,0},{5,1},{6,2},{7,3},{8,12},{9,13},{10,... | collective-permute-start | bytes 393224 | tf_op jit(solution)/shard_map/ppermute | solution.py:293
  96.6 4.9 %collective-permute-start.9 = (f32[16,8,128]{2,1,0:T(8,128)S(1)}, f32[16,8,128]{2,1,0:T(8,128)S(1)}, u32[]{:S(2)}, u32[]{:S(2)}) collective-permute-start(f32[16,8,128]{2,1,0:T(8,128)S(1)} %get-tuple-element.33), channel_id=1, source_target_pairs={{0,96},{8,104},{16,112},{24,120},{32,0},{40,8},{48,16},{56,24},{64... | collective-permute-start | bytes 196616 | tf_op jit(solution)/shard_map/ppermute | solution.py:311
  97.5 6.1 %collective-permute-start.8 = (f32[16,8,128]{2,1,0:T(8,128)S(1)}, f32[16,8,128]{2,1,0:T(8,128)S(1)}, u32[]{:S(2)}, u32[]{:S(2)}) collective-permute-start(f32[16,8,128]{2,1,0:T(8,128)S(1)} %get-tuple-element.33), channel_id=1, source_target_pairs={{0,64},{8,72},{16,80},{24,88},{32,96},{40,104},{48,112},{56,120},{... | collective-permute-start | bytes 196616 | tf_op jit(solution)/shard_map/ppermute | solution.py:311
  98.5 5.8 %collective-permute-start.7 = (f32[16,8,128]{2,1,0:T(8,128)S(1)}, f32[16,8,128]{2,1,0:T(8,128)S(1)}, u32[]{:S(2)}, u32[]{:S(2)}) collective-permute-start(f32[16,8,128]{2,1,0:T(8,128)S(1)} %get-tuple-element.33), channel_id=1, source_target_pairs={{0,32},{8,40},{16,48},{24,56},{32,64},{40,72},{48,80},{56,88},{64,... | collective-permute-start | bytes 196616 | tf_op jit(solution)/shard_map/ppermute | solution.py:311
  98.9 5.4 %collective-permute-start.6 = (f32[16,8,128]{2,1,0:T(8,128)S(1)}, f32[16,8,128]{2,1,0:T(8,128)S(1)}, u32[]{:S(2)}, u32[]{:S(2)}) collective-permute-start(f32[16,8,128]{2,1,0:T(8,128)S(1)} %get-tuple-element.29), channel_id=1, source_target_pairs={{0,24},{8,0},{16,8},{24,16},{32,56},{40,32},{48,40},{56,48},{64,88... | collective-permute-start | bytes 196616 | tf_op jit(solution)/shard_map/ppermute | solution.py:306
  100.1 5.8 %collective-permute-start.5 = (f32[16,8,128]{2,1,0:T(8,128)S(1)}, f32[16,8,128]{2,1,0:T(8,128)S(1)}, u32[]{:S(2)}, u32[]{:S(2)}) collective-permute-start(f32[16,8,128]{2,1,0:T(8,128)S(1)} %get-tuple-element.29), channel_id=1, source_target_pairs={{0,16},{8,24},{16,0},{24,8},{32,48},{40,56},{48,32},{56,40},{64,80... | collective-permute-start | bytes 196616 | tf_op jit(solution)/shard_map/ppermute | solution.py:306
  101.5 5.5 %collective-permute-start.4 = (f32[16,8,128]{2,1,0:T(8,128)S(1)}, f32[16,8,128]{2,1,0:T(8,128)S(1)}, u32[]{:S(2)}, u32[]{:S(2)}) collective-permute-start(f32[16,8,128]{2,1,0:T(8,128)S(1)} %get-tuple-element.29), channel_id=1, source_target_pairs={{0,8},{8,16},{16,24},{24,0},{32,40},{40,48},{48,56},{56,32},{64,72... | collective-permute-start | bytes 196616 | tf_op jit(solution)/shard_map/ppermute | solution.py:306
  107.0 11.0 %collective-permute-start.12 = (f32[4,16,8,128]{3,2,1,0:T(8,128)S(1)}, f32[4,16,8,128]{3,2,1,0:T(8,128)S(1)}, u32[]{:S(2)}, u32[]{:S(2)}) collective-permute-start(f32[4,16,8,128]{3,2,1,0:T(8,128)S(1)} %get-tuple-element.37.refs_0_), channel_id=1, source_target_pairs={{0,96},{8,104},{16,112},{24,120},{32,0},{40,8},{48,16},{56,24},{64... | collective-permute-start | bytes 786440 | tf_op jit(solution)/shard_map/ppermute | solution.py:311
  109.7 9.3 %collective-permute-start.11 = (f32[4,16,8,128]{3,2,1,0:T(8,128)S(1)}, f32[4,16,8,128]{3,2,1,0:T(8,128)S(1)}, u32[]{:S(2)}, u32[]{:S(2)}) collective-permute-start(f32[4,16,8,128]{3,2,1,0:T(8,128)S(1)} %get-tuple-element.37.refs_0_), channel_id=1, source_target_pairs={{0,64},{8,72},{16,80},{24,88},{32,96},{40,104},{48,112},{56,120},{... | collective-permute-start | bytes 786440 | tf_op jit(solution)/shard_map/ppermute | solution.py:311
  111.3 10.4 %collective-permute-start.10 = (f32[4,16,8,128]{3,2,1,0:T(8,128)S(1)}, f32[4,16,8,128]{3,2,1,0:T(8,128)S(1)}, u32[]{:S(2)}, u32[]{:S(2)}) collective-permute-start(f32[4,16,8,128]{3,2,1,0:T(8,128)S(1)} %get-tuple-element.37.refs_0_), channel_id=1, source_target_pairs={{0,32},{8,40},{16,48},{24,56},{32,64},{40,72},{48,80},{56,88},{64,... | collective-permute-start | bytes 786440 | tf_op jit(solution)/shard_map/ppermute | solution.py:311
  112.5 9.2 %collective-permute-start.15 = (f32[4,16,8,128]{3,2,1,0:T(8,128)S(1)}, f32[4,16,8,128]{3,2,1,0:T(8,128)S(1)}, u32[]{:S(2)}, u32[]{:S(2)}) collective-permute-start(f32[4,16,8,128]{3,2,1,0:T(8,128)S(1)} %get-tuple-element.38.refs_4_), channel_id=1, source_target_pairs={{0,24},{8,0},{16,8},{24,16},{32,56},{40,32},{48,40},{56,48},{64,88... | collective-permute-start | bytes 786440 | tf_op jit(solution)/shard_map/ppermute | solution.py:306
  113.3 8.4 %collective-permute-start.14 = (f32[4,16,8,128]{3,2,1,0:T(8,128)S(1)}, f32[4,16,8,128]{3,2,1,0:T(8,128)S(1)}, u32[]{:S(2)}, u32[]{:S(2)}) collective-permute-start(f32[4,16,8,128]{3,2,1,0:T(8,128)S(1)} %get-tuple-element.38.refs_4_), channel_id=1, source_target_pairs={{0,16},{8,24},{16,0},{24,8},{32,48},{40,56},{48,32},{56,40},{64,80... | collective-permute-start | bytes 786440 | tf_op jit(solution)/shard_map/ppermute | solution.py:306
  118.0 7.6 %collective-permute-start.13 = (f32[4,16,8,128]{3,2,1,0:T(8,128)S(1)}, f32[4,16,8,128]{3,2,1,0:T(8,128)S(1)}, u32[]{:S(2)}, u32[]{:S(2)}) collective-permute-start(f32[4,16,8,128]{3,2,1,0:T(8,128)S(1)} %get-tuple-element.38.refs_4_), channel_id=1, source_target_pairs={{0,8},{8,16},{16,24},{24,0},{32,40},{40,48},{48,56},{56,32},{64,72... | collective-permute-start | bytes 786440 | tf_op jit(solution)/shard_map/ppermute | solution.py:306
  127.8 2.2 %collective-permute-start.16 = (f32[4,128,256]{2,1,0:T(8,128)S(1)}, f32[4,128,256]{2,1,0:T(8,128)S(1)}, u32[]{:S(2)}, u32[]{:S(2)}) collective-permute-start(f32[4,128,256]{2,1,0:T(8,128)S(1)} %get-tuple-element.41), channel_id=1, source_target_pairs={{0,1},{1,0},{2,3},{3,2},{4,5},{5,4},{6,7},{7,6},{8,9},{9,8},{10,11... | collective-permute-start | bytes 1572872 | tf_op jit(solution)/shard_map/ppermute | solution.py:290
  130.0 7.1 %collective-permute-start.17 = (f32[128,256]{1,0:T(8,128)S(1)}, f32[128,256]{1,0:T(8,128)S(1)}, u32[]{:S(2)}, u32[]{:S(2)}) collective-permute-start(f32[128,256]{1,0:T(8,128)S(1)} %get-tuple-element.42), channel_id=1, source_target_pairs={{0,2},{1,3},{2,4},{3,5},{4,6},{5,7},{6,0},{7,1},{8,10},{9,11},{10,... | collective-permute-start | bytes 393224 | tf_op jit(solution)/shard_map/ppermute | solution.py:293
  130.9 8.3 %collective-permute-start.19 = (f32[128,256]{1,0:T(8,128)S(1)}, f32[128,256]{1,0:T(8,128)S(1)}, u32[]{:S(2)}, u32[]{:S(2)}) collective-permute-start(f32[128,256]{1,0:T(8,128)S(1)} %get-tuple-element.43), channel_id=1, source_target_pairs={{0,6},{1,7},{2,0},{3,1},{4,2},{5,3},{6,4},{7,5},{8,14},{9,15},{10,... | collective-permute-start | bytes 393224 | tf_op jit(solution)/shard_map/ppermute | solution.py:293
  133.3 6.8 %collective-permute-start.18 = (f32[128,256]{1,0:T(8,128)S(1)}, f32[128,256]{1,0:T(8,128)S(1)}, u32[]{:S(2)}, u32[]{:S(2)}) collective-permute-start(f32[128,256]{1,0:T(8,128)S(1)} %get-tuple-element.44), channel_id=1, source_target_pairs={{0,4},{1,5},{2,6},{3,7},{4,0},{5,1},{6,2},{7,3},{8,12},{9,13},{10,... | collective-permute-start | bytes 393224 | tf_op jit(solution)/shard_map/ppermute | solution.py:293

commit v7 on v6

--- a/solution.py
+++ b/solution.py
@@ -16,7 +16,7 @@
 TILES = NRHS // LANES
 CORES = 2
 VMEM_LIMIT = 8 << 20
-TILE = 256
+TILE = 128
 VMEM = pl.BlockSpec(memory_space=pltpu.VMEM)
 SMEM = pl.BlockSpec(memory_space=pltpu.SMEM)
 ANY = pl.BlockSpec(memory_space=pl.ANY)

time: 141 us -> 142 us (level)
  no operation moved by 1% of the time
where the time goes in v7:
time: 142 us
  blocking collectives  74.9 us (53%)
  waiting for transfers between devices  30.4 us (21%)
  starting transfers between devices  21.6 us (15%)
  Pallas kernels  13.1 us (9%)
    all_to_all x3, blocking collectives, exchange(): return lax.all_to_all(x, axis, split_axis=0, concat_axis=0, tiled=True)  74.9 us
    ppermute x6, waiting for transfers between devices, reduce_cols(): lax.ppermute(mine[distance] + sibling[distance], 'col', [(c, (c + CORES *...  12.3 us
    ppermute x6, waiting for transfers between devices, along_z(): lax.ppermute(x, 'row', [(i, (i + side * k) % rows) for i in range(rows)])  9.51 us
    ppermute x6, starting transfers between devices, reduce_cols(): lax.ppermute(mine[distance] + sibling[distance], 'col', [(c, (c + CORES *...  8.43 us
    ppermute x6, starting transfers between devices, along_z(): lax.ppermute(x, 'row', [(i, (i + side * k) % rows) for i in range(rows)])  7.72 us
    ppermute x6, waiting for transfers between devices, along_y(): lax.ppermute(x, 'row', [(i, i // side * side + (i + k) % side) for i in r...  6.66 us
    ppermute x6, starting transfers between devices, along_y(): lax.ppermute(x, 'row', [(i, i // side * side + (i + k) % side) for i in r...  5.06 us
    pallas_call x1, Pallas kernels, front(): pl.pallas_call(front_kernel, out_shape=(f32(order, NRHS), f32(rows, half,...  3.73 us
  transfers between devices with their start and end apart: 20, of which 17 were waited for; matrix products, arithmetic and copies ran while one was open for 0% of the time, Pallas kernels for 1%

profile of v7, /device:TPU:0, one launch (start us, length us, event | category | flops | bytes accessed | tf_op | source)
XLA Modules:
  0.0 141.6 jit_solution(17084369549780034698)
XLA Ops:
  0.6 1.9 %pack.1 = f32[16,33,8,128]{3,2,1,0:T(8,128)S(1)} custom-call(s32[16]{0:T(128)} %target_ref.1, s32[8]{0:T(128)} %map_ref.1, f32[16,16,8,256]{3,2,1,0:T(8,128)} %bitcast.45), custom_call_target="tpu_custom_call" | custom-call | tf_op jit(solution)/shard_map/pack/pallas_call | solution.py:84
  2.5 37.3 %all_to_all.15.arrived_ref = f32[16,33,8,128]{3,2,1,0:T(8,128)S(1)} all-to-all(f32[16,33,8,128]{3,2,1,0:T(8,128)S(1)} %pack.1), channel_id=1, replica_groups=mesh['row'=16,'col'=8] {'row'}, dimensions={0} | all-to-all | bytes 4325376 | tf_op jit(solution)/shard_map/all_to_all | solution.py:48
  39.8 2.4 %route.1 = (f32[128,2,8,128]{3,2,1,0:T(8,128)S(1)}, f32[256,2,8,128]{3,2,1,0:T(8,128)S(1)}, s32[16,128]{1,0:T(8,128)S(1)}) custom-call(f32[16,33,8,128]{3,2,1,0:T(8,128)S(1)} %all_to_all.15.arrived_ref), custom_call_target="tpu_custom_call" | custom-call | tf_op jit(solution)/shard_map/route/pallas_call | solution.py:137
  42.2 19.7 %all_to_all.16.arrived_ref = f32[16,8,2,8,128]{4,3,2,1,0:T(8,128)S(1)} all-to-all(f32[16,8,2,8,128]{4,3,2,1,0:T(8,128)S(1)} %bitcast.44), channel_id=1, replica_groups=mesh['row'=16,'col'=8] {'row'}, dimensions={0} | all-to-all | bytes 2097152 | tf_op jit(solution)/shard_map/all_to_all | solution.py:48
  61.9 3.7 %front.1 = (f32[1024,256]{1,0:T(8,128)}, f32[16,8,2,8,128]{4,3,2,1,0:T(8,128)S(1)}) custom-call(f32[16,8,2,8,128]{4,3,2,1,0:T(8,128)S(1)} %all_to_all.16.arrived_ref, f32[1024,1024]{1,0:T(8,128)S(1)} %copy-done, f32[1024,1024]{1,0:T(8,128)S(1)} %copy-done.1), custom_call_target="tpu_custom_call" | custom-call | tf_op jit(solution)/shard_map/front/pallas_call | solution.py:188
  65.6 17.9 %all_to_all.17.arrived_ref = f32[16,8,2,8,128]{4,3,2,1,0:T(8,128)S(1)} all-to-all(f32[16,8,2,8,128]{4,3,2,1,0:T(8,128)S(1)} %get-tuple-element.25), channel_id=1, replica_groups=mesh['row'=16,'col'=8] {'row'}, dimensions={0} | all-to-all | bytes 2097152 | tf_op jit(solution)/shard_map/all_to_all | solution.py:48
  83.5 1.2 subtract.1
  84.7 0.1 collective-permute-start
  84.8 1.9 %collective-permute-done = f32[4,2,16,8,128]{4,3,2,1,0:T(8,128)S(1)} collective-permute-done((f32[4,2,16,8,128]{4,3,2,1,0:T(8,128)S(1)}, f32[4,2,16,8,128]{4,3,2,1,0:T(8,128)S(1)}, u32[]{:S(2)}, u32[]{:S(2)}) %collective-permute-start) | collective-permute-done | bytes 524320 | tf_op jit(solution)/shard_map/ppermute | solution.py:290
  86.7 0.1 fusion.9
  86.7 1.6 %collective-permute-start.1 = (f32[2,16,8,128]{3,2,1,0:T(8,128)S(1)}, f32[2,16,8,128]{3,2,1,0:T(8,128)S(1)}, u32[]{:S(2)}, u32[]{:S(2)}) collective-permute-start(f32[2,16,8,128]{3,2,1,0:T(8,128)S(1)} %get-tuple-element.45), channel_id=1, source_target_pairs={{0,2},{1,3},{2,4},{3,5},{4,6},{5,7},{6,0},{7,1},{8,10},{9,11},{10,... | collective-permute-start | bytes 393224 | tf_op jit(solution)/shard_map/ppermute | solution.py:293
  88.3 1.7 %collective-permute-start.3 = (f32[2,16,8,128]{3,2,1,0:T(8,128)S(1)}, f32[2,16,8,128]{3,2,1,0:T(8,128)S(1)}, u32[]{:S(2)}, u32[]{:S(2)}) collective-permute-start(f32[2,16,8,128]{3,2,1,0:T(8,128)S(1)} %get-tuple-element.46), channel_id=1, source_target_pairs={{0,6},{1,7},{2,0},{3,1},{4,2},{5,3},{6,4},{7,5},{8,14},{9,15},{10,... | collective-permute-start | bytes 393224 | tf_op jit(solution)/shard_map/ppermute | solution.py:293
  90.0 1.8 %collective-permute-start.2 = (f32[2,16,8,128]{3,2,1,0:T(8,128)S(1)}, f32[2,16,8,128]{3,2,1,0:T(8,128)S(1)}, u32[]{:S(2)}, u32[]{:S(2)}) collective-permute-start(f32[2,16,8,128]{3,2,1,0:T(8,128)S(1)} %get-tuple-element.47), channel_id=1, source_target_pairs={{0,4},{1,5},{2,6},{3,7},{4,0},{5,1},{6,2},{7,3},{8,12},{9,13},{10,... | collective-permute-start | bytes 393224 | tf_op jit(solution)/shard_map/ppermute | solution.py:293
  91.8 1.7 %collective-permute-done.1 = f32[2,16,8,128]{3,2,1,0:T(8,128)S(1)} collective-permute-done((f32[2,16,8,128]{3,2,1,0:T(8,128)S(1)}, f32[2,16,8,128]{3,2,1,0:T(8,128)S(1)}, u32[]{:S(2)}, u32[]{:S(2)}) %collective-permute-start.1) | collective-permute-done | bytes 131104 | tf_op jit(solution)/shard_map/ppermute | solution.py:293
  93.5 2.1 %collective-permute-done.3 = f32[2,16,8,128]{3,2,1,0:T(8,128)S(1)} collective-permute-done((f32[2,16,8,128]{3,2,1,0:T(8,128)S(1)}, f32[2,16,8,128]{3,2,1,0:T(8,128)S(1)}, u32[]{:S(2)}, u32[]{:S(2)}) %collective-permute-start.3) | collective-permute-done | bytes 131104 | tf_op jit(solution)/shard_map/ppermute | solution.py:293
  95.6 1.7 %collective-permute-done.2 = f32[2,16,8,128]{3,2,1,0:T(8,128)S(1)} collective-permute-done((f32[2,16,8,128]{3,2,1,0:T(8,128)S(1)}, f32[2,16,8,128]{3,2,1,0:T(8,128)S(1)}, u32[]{:S(2)}, u32[]{:S(2)}) %collective-permute-start.2) | collective-permute-done | bytes 131104 | tf_op jit(solution)/shard_map/ppermute | solution.py:293
  97.4 0.9 collective-permute-start.9
  98.3 1.0 collective-permute-start.8
  99.3 0.4 collective-permute-start.7
  99.7 1.2 collective-permute-start.6
  100.9 1.4 %collective-permute-start.5 = (f32[16,8,128]{2,1,0:T(8,128)S(1)}, f32[16,8,128]{2,1,0:T(8,128)S(1)}, u32[]{:S(2)}, u32[]{:S(2)}) collective-permute-start(f32[16,8,128]{2,1,0:T(8,128)S(1)} %get-tuple-element.29), channel_id=1, source_target_pairs={{0,16},{8,24},{16,0},{24,8},{32,48},{40,56},{48,32},{56,40},{64,80... | collective-permute-start | bytes 196616 | tf_op jit(solution)/shard_map/ppermute | solution.py:306
  102.3 0.2 collective-permute-start.4
  102.6 1.8 %collective-permute-done.8 = f32[16,8,128]{2,1,0:T(8,128)S(1)} collective-permute-done((f32[16,8,128]{2,1,0:T(8,128)S(1)}, f32[16,8,128]{2,1,0:T(8,128)S(1)}, u32[]{:S(2)}, u32[]{:S(2)}) %collective-permute-start.8) | collective-permute-done | bytes 65568 | tf_op jit(solution)/shard_map/ppermute | solution.py:311
  104.4 0.7 collective-permute-done.7
  105.1 1.6 %collective-permute-done.5 = f32[16,8,128]{2,1,0:T(8,128)S(1)} collective-permute-done((f32[16,8,128]{2,1,0:T(8,128)S(1)}, f32[16,8,128]{2,1,0:T(8,128)S(1)}, u32[]{:S(2)}, u32[]{:S(2)}) %collective-permute-start.5) | collective-permute-done | bytes 65568 | tf_op jit(solution)/shard_map/ppermute | solution.py:306
  106.7 1.2 collective-permute-done.4
  107.9 2.6 %collective-permute-start.12 = (f32[4,16,8,128]{3,2,1,0:T(8,128)S(1)}, f32[4,16,8,128]{3,2,1,0:T(8,128)S(1)}, u32[]{:S(2)}, u32[]{:S(2)}) collective-permute-start(f32[4,16,8,128]{3,2,1,0:T(8,128)S(1)} %get-tuple-element.37.refs_0_), channel_id=1, source_target_pairs={{0,96},{8,104},{16,112},{24,120},{32,0},{40,8},{48,16},{56,24},{64... | collective-permute-start | bytes 786440 | tf_op jit(solution)/shard_map/ppermute | solution.py:311
  110.5 1.6 %collective-permute-start.11 = (f32[4,16,8,128]{3,2,1,0:T(8,128)S(1)}, f32[4,16,8,128]{3,2,1,0:T(8,128)S(1)}, u32[]{:S(2)}, u32[]{:S(2)}) collective-permute-start(f32[4,16,8,128]{3,2,1,0:T(8,128)S(1)} %get-tuple-element.37.refs_0_), channel_id=1, source_target_pairs={{0,64},{8,72},{16,80},{24,88},{32,96},{40,104},{48,112},{56,120},{... | collective-permute-start | bytes 786440 | tf_op jit(solution)/shard_map/ppermute | solution.py:311
  112.1 1.2 collective-permute-start.10
  113.3 0.9 collective-permute-start.15
  114.1 0.9 collective-permute-start.14
  115.0 3.8 %collective-permute-done.12.refs_3_ = f32[4,16,8,128]{3,2,1,0:T(8,128)S(1)} collective-permute-done((f32[4,16,8,128]{3,2,1,0:T(8,128)S(1)}, f32[4,16,8,128]{3,2,1,0:T(8,128)S(1)}, u32[]{:S(2)}, u32[]{:S(2)}) %collective-permute-start.12) | collective-permute-done | bytes 262176 | tf_op jit(solution)/shard_map/ppermute | solution.py:311
  118.8 0.5 collective-permute-start.13
  119.3 0.5 collective-permute-done.11.refs_2_
  119.8 2.7 %collective-permute-done.10.refs_1_ = f32[4,16,8,128]{3,2,1,0:T(8,128)S(1)} collective-permute-done((f32[4,16,8,128]{3,2,1,0:T(8,128)S(1)}, f32[4,16,8,128]{3,2,1,0:T(8,128)S(1)}, u32[]{:S(2)}, u32[]{:S(2)}) %collective-permute-start.10) | collective-permute-done | bytes 262176 | tf_op jit(solution)/shard_map/ppermute | solution.py:311
  122.5 0.1 collective-permute-done.14.refs_6_
  122.6 3.8 %collective-permute-done.13.refs_5_ = f32[4,16,8,128]{3,2,1,0:T(8,128)S(1)} collective-permute-done((f32[4,16,8,128]{3,2,1,0:T(8,128)S(1)}, f32[4,16,8,128]{3,2,1,0:T(8,128)S(1)}, u32[]{:S(2)}, u32[]{:S(2)}) %collective-permute-start.13) | collective-permute-done | bytes 262176 | tf_op jit(solution)/shard_map/ppermute | solution.py:306
  126.4 2.2 %root_other.1 = (f32[4,128,256]{2,1,0:T(8,128)S(1)}, bf16[2048,256]{1,0:T(8,128)(2,1)S(1)}, bf16[2048,256]{1,0:T(8,128)(2,1)S(1)}) custom-call(f32[1024,2048]{1,0:T(8,128)S(1)} %bitcast.43, f32[4,16,8,128]{3,2,1,0:T(8,128)S(1)} %get-tuple-element.37.refs_0_, f32[4,16,8,128]{3,2,1,0:T(8,128)S(1)} %collective-permute-done.10.refs_1_, ...), custom_call_target="tpu_custom_call" | custom-call | flops 1610612736 | bytes 4194304 | tf_op jit(solution)/shard_map/root_other/pallas_call | solution.py:266
  128.6 0.3 collective-permute-start.16
  128.9 1.8 %root_mine.1 = f32[4,128,256]{2,1,0:T(8,128)S(1)} custom-call(bf16[2048,256]{1,0:T(8,128)(2,1)S(1)} %get-tuple-element.39.high_ref, bf16[2048,256]{1,0:T(8,128)(2,1)S(1)} %get-tuple-element.40.low_ref, f32[1024,2048]{1,0:T(8,128)S(1)} %bitcast.43), custom_call_target="tpu_custom_call" | custom-call | flops 1610612736 | bytes 4194304 | tf_op jit(solution)/shard_map/root_mine/pallas_call | solution.py:276
  130.7 0.1 collective-permute-done.16
  130.8 0.1 fusion.2
  130.8 0.9 collective-permute-start.17
  131.7 2.4 %collective-permute-start.19 = (f32[128,256]{1,0:T(8,128)S(1)}, f32[128,256]{1,0:T(8,128)S(1)}, u32[]{:S(2)}, u32[]{:S(2)}) collective-permute-start(f32[128,256]{1,0:T(8,128)S(1)} %get-tuple-element.43), channel_id=1, source_target_pairs={{0,6},{1,7},{2,0},{3,1},{4,2},{5,3},{6,4},{7,5},{8,14},{9,15},{10,... | collective-permute-start | bytes 393224 | tf_op jit(solution)/shard_map/ppermute | solution.py:293
  134.1 3.8 %collective-permute-done.17 = f32[128,256]{1,0:T(8,128)S(1)} collective-permute-done((f32[128,256]{1,0:T(8,128)S(1)}, f32[128,256]{1,0:T(8,128)S(1)}, u32[]{:S(2)}, u32[]{:S(2)}) %collective-permute-start.17) | collective-permute-done | bytes 131104 | tf_op jit(solution)/shard_map/ppermute | solution.py:293
  137.9 2.1 %collective-permute-done.19 = f32[128,256]{1,0:T(8,128)S(1)} collective-permute-done((f32[128,256]{1,0:T(8,128)S(1)}, f32[128,256]{1,0:T(8,128)S(1)}, u32[]{:S(2)}, u32[]{:S(2)}) %collective-permute-start.19) | collective-permute-done | bytes 131104 | tf_op jit(solution)/shard_map/ppermute | solution.py:293
  140.0 0.9 collective-permute-done.18
  140.9 0.7 fusion.6
  (16 shorter events, 0.1 us)
Async XLA Ops:
  2.5 59.4 %copy-start.1 = (f32[1024,1024]{1,0:T(8,128)S(1)}, f32[1024,1024]{1,0:T(8,128)}, u32[]{:S(2)}) copy-start(f32[1024,1024]{1,0:T(8,128)} %factor_ref.1) | copy-start | bytes 12582916
  39.8 22.1 %copy-start = (f32[1024,1024]{1,0:T(8,128)S(1)}, f32[1024,1024]{1,0:T(8,128)}, u32[]{:S(2)}) copy-start(f32[1024,1024]{1,0:T(8,128)} %pivot_ref.1) | copy-start | bytes 12582916
  42.2 84.2 %slice-start = ((s8[8388608]{0:T(1024)(128)(4,1)}), s8[4194304]{0:T(1024)(128)(4,1)S(1)}, s32[]{:S(2)}) async-start(s8[8388608]{0:T(1024)(128)(4,1)} %bitcast.42), calls=%async_computation.3 | async-start | bytes 8388608
  61.9 64.5 %slice-start.1 = ((s8[8388608]{0:T(1024)(128)(4,1)}), s8[4194304]{0:T(1024)(128)(4,1)S(1)}, s32[]{:S(2)}) async-start(s8[8388608]{0:T(1024)(128)(4,1)} %bitcast.42), calls=%async_computation.4 | async-start | bytes 8388608
  84.7 2.0 %collective-permute-start = (f32[4,2,16,8,128]{4,3,2,1,0:T(8,128)S(1)}, f32[4,2,16,8,128]{4,3,2,1,0:T(8,128)S(1)}, u32[]{:S(2)}, u32[]{:S(2)}) collective-permute-start(f32[4,2,16,8,128]{4,3,2,1,0:T(8,128)S(1)} %get-tuple-element.28), channel_id=1, source_target_pairs={{0,1},{1,0},{2,3},{3,2},{4,5},{5,4},{6,7},{7,6},{8,9},{9,8},{10,11... | collective-permute-start | bytes 1572872 | tf_op jit(solution)/shard_map/ppermute | solution.py:290
  86.7 6.8 %collective-permute-start.1 = (f32[2,16,8,128]{3,2,1,0:T(8,128)S(1)}, f32[2,16,8,128]{3,2,1,0:T(8,128)S(1)}, u32[]{:S(2)}, u32[]{:S(2)}) collective-permute-start(f32[2,16,8,128]{3,2,1,0:T(8,128)S(1)} %get-tuple-element.45), channel_id=1, source_target_pairs={{0,2},{1,3},{2,4},{3,5},{4,6},{5,7},{6,0},{7,1},{8,10},{9,11},{10,... | collective-permute-start | bytes 393224 | tf_op jit(solution)/shard_map/ppermute | solution.py:293
  88.3 7.4 %collective-permute-start.3 = (f32[2,16,8,128]{3,2,1,0:T(8,128)S(1)}, f32[2,16,8,128]{3,2,1,0:T(8,128)S(1)}, u32[]{:S(2)}, u32[]{:S(2)}) collective-permute-start(f32[2,16,8,128]{3,2,1,0:T(8,128)S(1)} %get-tuple-element.46), channel_id=1, source_target_pairs={{0,6},{1,7},{2,0},{3,1},{4,2},{5,3},{6,4},{7,5},{8,14},{9,15},{10,... | collective-permute-start | bytes 393224 | tf_op jit(solution)/shard_map/ppermute | solution.py:293
  90.0 7.3 %collective-permute-start.2 = (f32[2,16,8,128]{3,2,1,0:T(8,128)S(1)}, f32[2,16,8,128]{3,2,1,0:T(8,128)S(1)}, u32[]{:S(2)}, u32[]{:S(2)}) collective-permute-start(f32[2,16,8,128]{3,2,1,0:T(8,128)S(1)} %get-tuple-element.47), channel_id=1, source_target_pairs={{0,4},{1,5},{2,6},{3,7},{4,0},{5,1},{6,2},{7,3},{8,12},{9,13},{10,... | collective-permute-start | bytes 393224 | tf_op jit(solution)/shard_map/ppermute | solution.py:293
  97.4 4.9 %collective-permute-start.9 = (f32[16,8,128]{2,1,0:T(8,128)S(1)}, f32[16,8,128]{2,1,0:T(8,128)S(1)}, u32[]{:S(2)}, u32[]{:S(2)}) collective-permute-start(f32[16,8,128]{2,1,0:T(8,128)S(1)} %get-tuple-element.33), channel_id=1, source_target_pairs={{0,96},{8,104},{16,112},{24,120},{32,0},{40,8},{48,16},{56,24},{64... | collective-permute-start | bytes 196616 | tf_op jit(solution)/shard_map/ppermute | solution.py:311
  98.3 6.1 %collective-permute-start.8 = (f32[16,8,128]{2,1,0:T(8,128)S(1)}, f32[16,8,128]{2,1,0:T(8,128)S(1)}, u32[]{:S(2)}, u32[]{:S(2)}) collective-permute-start(f32[16,8,128]{2,1,0:T(8,128)S(1)} %get-tuple-element.33), channel_id=1, source_target_pairs={{0,64},{8,72},{16,80},{24,88},{32,96},{40,104},{48,112},{56,120},{... | collective-permute-start | bytes 196616 | tf_op jit(solution)/shard_map/ppermute | solution.py:311
  99.3 5.8 %collective-permute-start.7 = (f32[16,8,128]{2,1,0:T(8,128)S(1)}, f32[16,8,128]{2,1,0:T(8,128)S(1)}, u32[]{:S(2)}, u32[]{:S(2)}) collective-permute-start(f32[16,8,128]{2,1,0:T(8,128)S(1)} %get-tuple-element.33), channel_id=1, source_target_pairs={{0,32},{8,40},{16,48},{24,56},{32,64},{40,72},{48,80},{56,88},{64,... | collective-permute-start | bytes 196616 | tf_op jit(solution)/shard_map/ppermute | solution.py:311
  99.7 5.4 %collective-permute-start.6 = (f32[16,8,128]{2,1,0:T(8,128)S(1)}, f32[16,8,128]{2,1,0:T(8,128)S(1)}, u32[]{:S(2)}, u32[]{:S(2)}) collective-permute-start(f32[16,8,128]{2,1,0:T(8,128)S(1)} %get-tuple-element.29), channel_id=1, source_target_pairs={{0,24},{8,0},{16,8},{24,16},{32,56},{40,32},{48,40},{56,48},{64,88... | collective-permute-start | bytes 196616 | tf_op jit(solution)/shard_map/ppermute | solution.py:306
  100.9 5.8 %collective-permute-start.5 = (f32[16,8,128]{2,1,0:T(8,128)S(1)}, f32[16,8,128]{2,1,0:T(8,128)S(1)}, u32[]{:S(2)}, u32[]{:S(2)}) collective-permute-start(f32[16,8,128]{2,1,0:T(8,128)S(1)} %get-tuple-element.29), channel_id=1, source_target_pairs={{0,16},{8,24},{16,0},{24,8},{32,48},{40,56},{48,32},{56,40},{64,80... | collective-permute-start | bytes 196616 | tf_op jit(solution)/shard_map/ppermute | solution.py:306
  102.3 5.5 %collective-permute-start.4 = (f32[16,8,128]{2,1,0:T(8,128)S(1)}, f32[16,8,128]{2,1,0:T(8,128)S(1)}, u32[]{:S(2)}, u32[]{:S(2)}) collective-permute-start(f32[16,8,128]{2,1,0:T(8,128)S(1)} %get-tuple-element.29), channel_id=1, source_target_pairs={{0,8},{8,16},{16,24},{24,0},{32,40},{40,48},{48,56},{56,32},{64,72... | collective-permute-start | bytes 196616 | tf_op jit(solution)/shard_map/ppermute | solution.py:306
  107.9 11.0 %collective-permute-start.12 = (f32[4,16,8,128]{3,2,1,0:T(8,128)S(1)}, f32[4,16,8,128]{3,2,1,0:T(8,128)S(1)}, u32[]{:S(2)}, u32[]{:S(2)}) collective-permute-start(f32[4,16,8,128]{3,2,1,0:T(8,128)S(1)} %get-tuple-element.37.refs_0_), channel_id=1, source_target_pairs={{0,96},{8,104},{16,112},{24,120},{32,0},{40,8},{48,16},{56,24},{64... | collective-permute-start | bytes 786440 | tf_op jit(solution)/shard_map/ppermute | solution.py:311
  110.5 9.3 %collective-permute-start.11 = (f32[4,16,8,128]{3,2,1,0:T(8,128)S(1)}, f32[4,16,8,128]{3,2,1,0:T(8,128)S(1)}, u32[]{:S(2)}, u32[]{:S(2)}) collective-permute-start(f32[4,16,8,128]{3,2,1,0:T(8,128)S(1)} %get-tuple-element.37.refs_0_), channel_id=1, source_target_pairs={{0,64},{8,72},{16,80},{24,88},{32,96},{40,104},{48,112},{56,120},{... | collective-permute-start | bytes 786440 | tf_op jit(solution)/shard_map/ppermute | solution.py:311
  112.1 10.4 %collective-permute-start.10 = (f32[4,16,8,128]{3,2,1,0:T(8,128)S(1)}, f32[4,16,8,128]{3,2,1,0:T(8,128)S(1)}, u32[]{:S(2)}, u32[]{:S(2)}) collective-permute-start(f32[4,16,8,128]{3,2,1,0:T(8,128)S(1)} %get-tuple-element.37.refs_0_), channel_id=1, source_target_pairs={{0,32},{8,40},{16,48},{24,56},{32,64},{40,72},{48,80},{56,88},{64,... | collective-permute-start | bytes 786440 | tf_op jit(solution)/shard_map/ppermute | solution.py:311
  113.3 9.2 %collective-permute-start.15 = (f32[4,16,8,128]{3,2,1,0:T(8,128)S(1)}, f32[4,16,8,128]{3,2,1,0:T(8,128)S(1)}, u32[]{:S(2)}, u32[]{:S(2)}) collective-permute-start(f32[4,16,8,128]{3,2,1,0:T(8,128)S(1)} %get-tuple-element.38.refs_4_), channel_id=1, source_target_pairs={{0,24},{8,0},{16,8},{24,16},{32,56},{40,32},{48,40},{56,48},{64,88... | collective-permute-start | bytes 786440 | tf_op jit(solution)/shard_map/ppermute | solution.py:306
  114.1 8.4 %collective-permute-start.14 = (f32[4,16,8,128]{3,2,1,0:T(8,128)S(1)}, f32[4,16,8,128]{3,2,1,0:T(8,128)S(1)}, u32[]{:S(2)}, u32[]{:S(2)}) collective-permute-start(f32[4,16,8,128]{3,2,1,0:T(8,128)S(1)} %get-tuple-element.38.refs_4_), channel_id=1, source_target_pairs={{0,16},{8,24},{16,0},{24,8},{32,48},{40,56},{48,32},{56,40},{64,80... | collective-permute-start | bytes 786440 | tf_op jit(solution)/shard_map/ppermute | solution.py:306
  118.8 7.6 %collective-permute-start.13 = (f32[4,16,8,128]{3,2,1,0:T(8,128)S(1)}, f32[4,16,8,128]{3,2,1,0:T(8,128)S(1)}, u32[]{:S(2)}, u32[]{:S(2)}) collective-permute-start(f32[4,16,8,128]{3,2,1,0:T(8,128)S(1)} %get-tuple-element.38.refs_4_), channel_id=1, source_target_pairs={{0,8},{8,16},{16,24},{24,0},{32,40},{40,48},{48,56},{56,32},{64,72... | collective-permute-start | bytes 786440 | tf_op jit(solution)/shard_map/ppermute | solution.py:306
  128.6 2.2 %collective-permute-start.16 = (f32[4,128,256]{2,1,0:T(8,128)S(1)}, f32[4,128,256]{2,1,0:T(8,128)S(1)}, u32[]{:S(2)}, u32[]{:S(2)}) collective-permute-start(f32[4,128,256]{2,1,0:T(8,128)S(1)} %get-tuple-element.41), channel_id=1, source_target_pairs={{0,1},{1,0},{2,3},{3,2},{4,5},{5,4},{6,7},{7,6},{8,9},{9,8},{10,11... | collective-permute-start | bytes 1572872 | tf_op jit(solution)/shard_map/ppermute | solution.py:290
  130.8 7.1 %collective-permute-start.17 = (f32[128,256]{1,0:T(8,128)S(1)}, f32[128,256]{1,0:T(8,128)S(1)}, u32[]{:S(2)}, u32[]{:S(2)}) collective-permute-start(f32[128,256]{1,0:T(8,128)S(1)} %get-tuple-element.42), channel_id=1, source_target_pairs={{0,2},{1,3},{2,4},{3,5},{4,6},{5,7},{6,0},{7,1},{8,10},{9,11},{10,... | collective-permute-start | bytes 393224 | tf_op jit(solution)/shard_map/ppermute | solution.py:293
  131.7 8.3 %collective-permute-start.19 = (f32[128,256]{1,0:T(8,128)S(1)}, f32[128,256]{1,0:T(8,128)S(1)}, u32[]{:S(2)}, u32[]{:S(2)}) collective-permute-start(f32[128,256]{1,0:T(8,128)S(1)} %get-tuple-element.43), channel_id=1, source_target_pairs={{0,6},{1,7},{2,0},{3,1},{4,2},{5,3},{6,4},{7,5},{8,14},{9,15},{10,... | collective-permute-start | bytes 393224 | tf_op jit(solution)/shard_map/ppermute | solution.py:293
  134.1 6.8 %collective-permute-start.18 = (f32[128,256]{1,0:T(8,128)S(1)}, f32[128,256]{1,0:T(8,128)S(1)}, u32[]{:S(2)}, u32[]{:S(2)}) collective-permute-start(f32[128,256]{1,0:T(8,128)S(1)} %get-tuple-element.44), channel_id=1, source_target_pairs={{0,4},{1,5},{2,6},{3,7},{4,0},{5,1},{6,2},{7,3},{8,12},{9,13},{10,... | collective-permute-start | bytes 393224 | tf_op jit(solution)/shard_map/ppermute | solution.py:293
